TPU v7x, 32 devices: a whole 2x2x4 slice. The times are simulated.
32 devices in a mesh: dp: 8 (over y, x, core), mp: 4 (over z).
Axes of the slice: x: 2, y: 2, z: 4, core: 2. Of those that a mesh axis runs over, the one named last changes fastest.
Arguments:
- layer_input: float32 [8192, 512], P('dp'), may hold values from -6 to 6
- encoder_memory: float32 [8192, 512], P('dp', 'mp'), may hold values from -6 to 6
- output_grad: float32 [8192, 512], P('dp'), may hold values from -6 to 6
- target_lengths: int32 [8, 32], P('dp'), may hold values from 1 to 64, 1024 in all within a row
- memory_lengths: int32 [8, 32], P('dp'), may hold values from 1 to 64, 1024 in all within a row
- source_slots: int32 [8192], P('dp'), may hold values from 0 to 1407, as said below
- pair_counts: int32 [8, 8], replicated, may hold values from 112 to 176, as said below
- attend_input: float32 [6, 512, 512], P(None, 'dp', 'mp'), may hold values from -0.25 to 0.25
- attend_output: float32 [2, 512, 512], P(None, 'mp', 'dp'), may hold values from -1.5 to 1.5
- expand_weight: float32 [512, 2048], P('dp', 'mp'), may hold values from -0.25 to 0.25
- reduce_weight: float32 [2048, 512], P('mp', 'dp'), may hold values from -0.125 to 0.125
- norm_vectors: float32 [7, 512], P(None, 'dp')
- expand_bias: float32 [2048], P(('mp', 'dp')), may hold values from -1.75 to 1.75
- attend_input_first: float32 [6, 512, 512], P(None, 'dp', 'mp'), may hold values from -0.0029296875 to 0.0029296875
- attend_input_second: float32 [6, 512, 512], P(None, 'dp', 'mp'), may hold values from 2.3809886e-07 to 9.5239545e-07
- attend_output_first: float32 [2, 512, 512], P(None, 'mp', 'dp'), may hold values from -0.0029296875 to 0.0029296875
- attend_output_second: float32 [2, 512, 512], P(None, 'mp', 'dp'), may hold values from 2.3809886e-07 to 9.5239545e-07
- expand_weight_first: float32 [512, 2048], P('dp', 'mp'), may hold values from -0.0029296875 to 0.0029296875
- expand_weight_second: float32 [512, 2048], P('dp', 'mp'), may hold values from 2.3809886e-07 to 9.5239545e-07
- reduce_weight_first: float32 [2048, 512], P('mp', 'dp'), may hold values from -0.0029296875 to 0.0029296875
- reduce_weight_second: float32 [2048, 512], P('mp', 'dp'), may hold values from 2.3809886e-07 to 9.5239545e-07
- norm_vectors_first: float32 [7, 512], P(None, 'dp'), may hold values from -0.0029296875 to 0.0029296875
- norm_vectors_second: float32 [7, 512], P(None, 'dp'), may hold values from 2.3809886e-07 to 9.5239545e-07
- expand_bias_first: float32 [2048], P(('mp', 'dp')), may hold values from -0.0029296875 to 0.0029296875
- expand_bias_second: float32 [2048], P(('mp', 'dp')), may hold values from 2.3809886e-07 to 9.5239545e-07
Outputs:
- layer_output: float32 [8192, 512], P('dp')
- input_grad: float32 [8192, 512], P('dp')
- memory_grad: float32 [8192, 512], P('dp', 'mp')
- grad_norm: float32 [1], replicated
- new_attend_input: float32 [6, 512, 512], P(None, 'dp', 'mp')
- new_attend_output: float32 [2, 512, 512], P(None, 'mp', 'dp')
- new_expand_weight: float32 [512, 2048], P('dp', 'mp')
- new_reduce_weight: float32 [2048, 512], P('mp', 'dp')
- new_norm_vectors: float32 [7, 512], P(None, 'dp')
- new_expand_bias: float32 [2048], P(('mp', 'dp'))
- attend_input_copy: bfloat16 [6, 512, 512], P(None, 'dp', 'mp')
- attend_output_copy: bfloat16 [2, 512, 512], P(None, 'mp', 'dp')
- expand_weight_copy: bfloat16 [512, 2048], P('dp', 'mp')
- reduce_weight_copy: bfloat16 [2048, 512], P('mp', 'dp')
- first_attend_input: float32 [6, 512, 512], P(None, 'dp', 'mp')
- second_attend_input: float32 [6, 512, 512], P(None, 'dp', 'mp')
- first_attend_output: float32 [2, 512, 512], P(None, 'mp', 'dp')
- second_attend_output: float32 [2, 512, 512], P(None, 'mp', 'dp')
- first_expand_weight: float32 [512, 2048], P('dp', 'mp')
- second_expand_weight: float32 [512, 2048], P('dp', 'mp')
- first_reduce_weight: float32 [2048, 512], P('mp', 'dp')
- second_reduce_weight: float32 [2048, 512], P('mp', 'dp')
- first_norm_vectors: float32 [7, 512], P(None, 'dp')
- second_norm_vectors: float32 [7, 512], P(None, 'dp')
- first_expand_bias: float32 [2048], P(('mp', 'dp'))
- second_expand_bias: float32 [2048], P(('mp', 'dp'))
- matrix_norms: float32 [2, 10], replicated
Inputs may be any that keep to these rules, and one draw needn't show every extreme that they name: `target_lengths`: each row's 32 lengths sum to 1024. `memory_lengths`: each row's 32 lengths sum to 1024. Every row and every column sums to 1024; device a's rows for device j are a run of its rows that starts at the sum of pair_counts[a, i] over i < j. `source_slots`: on device j each value a * 176 + s with s < pair_counts[a, j] appears exactly once.
All inputs are finite; a program needn't handle non-finite values.
Results may differ from a plain program's by a relative error of at most 0.001.
Values sent between devices are 32-bit elements; how exact they have to be, the bound alone decides.
No kernel may reach another device: no remote copies, remote signals or barrier semaphores. Data moves between devices by JAX's collectives and lax.ppermute only.
A program may use at most 192 MiB of HBM per device.

v0:
```python
import jax
import jax.numpy as jnp
from jax import lax
from jax.sharding import PartitionSpec as P

HD = 64
STEP_NUM = 6


highest = lax.Precision.HIGHEST
norm_eps = 1e-05
adam_eps = 1e-06
first_decay = 0.5
second_decay = 0.5
matrix_decay = 0.01
peak_rate = 0.6
warm_steps = 8.0
clip_norm = 1.0
neg_large = -1e30


def matmul(left_side, right_side):
    return jnp.dot(left_side, right_side, precision=highest, preferred_element_type=jnp.float32)


def segment_ids(lengths, length_total):
    segment_ends = jnp.cumsum(lengths)
    places = jnp.arange(length_total, dtype=jnp.int32)
    return jnp.sum((segment_ends[:, None] <= places[None, :]).astype(jnp.int32), axis=0)


def layer_norm(values, gain_row, shift_row):
    centre_mean = jnp.mean(values, axis=-1, keepdims=True)
    centred = values - centre_mean
    variance = jnp.mean(centred * centred, axis=-1, keepdims=True)
    return centred * lax.rsqrt(variance + norm_eps) * gain_row + shift_row


def apply_gelu(values):
    return (
        0.5
        * values
        * (1.0 + jnp.tanh(0.7978845608028654 * (values + 0.044715 * values * values * values)))
    )


def masked_scores(queries, keys_in, query_seg, key_seg):
    scores = jnp.einsum("qhe,khe->hqk", queries, keys_in, precision=highest) * queries.shape[2] ** (
        -0.5
    )
    allowed = query_seg[:, None] == key_seg[None, :]
    return jnp.where(allowed[None], scores, neg_large)


def attend(queries, keys_in, values_in, query_seg, key_seg):
    tok_rows = queries.shape[0]
    block_rows = min(512, tok_rows)
    outputs = []
    totals = []
    for block_start in range(0, tok_rows, block_rows):
        block_end = block_start + block_rows
        scores = masked_scores(
            queries[block_start:block_end], keys_in, query_seg[block_start:block_end], key_seg
        )
        row_top = jnp.max(scores, axis=-1, keepdims=True)
        weights = jnp.exp(scores - row_top)
        row_total = jnp.sum(weights, axis=-1, keepdims=True)
        outputs.append(
            jnp.einsum("hqk,khe->qhe", weights / row_total, values_in, precision=highest)
        )
        totals.append((row_top + jnp.log(row_total))[:, :, 0])
    return (jnp.concatenate(outputs, axis=0), jnp.concatenate(totals, axis=1))


def attend_back(queries, keys_in, values_in, outputs, totals, grad_out, query_seg, key_seg):
    tok_rows = queries.shape[0]
    block_rows = min(512, tok_rows)
    score_scale = queries.shape[2] ** (-0.5)
    row_dots = jnp.sum(grad_out * outputs, axis=2).T
    grad_keys = jnp.zeros_like(keys_in)
    grad_values = jnp.zeros_like(values_in)
    grad_queries = []
    for block_start in range(0, tok_rows, block_rows):
        block_end = block_start + block_rows
        query_block = queries[block_start:block_end]
        grad_block = grad_out[block_start:block_end]
        scores = masked_scores(query_block, keys_in, query_seg[block_start:block_end], key_seg)
        weights = jnp.exp(scores - totals[:, block_start:block_end, None])
        grad_values = grad_values + jnp.einsum(
            "hqk,qhe->khe", weights, grad_block, precision=highest
        )
        grad_weights = jnp.einsum("qhe,khe->hqk", grad_block, values_in, precision=highest)
        grad_scores = (
            weights * (grad_weights - row_dots[:, block_start:block_end, None]) * score_scale
        )
        grad_queries.append(jnp.einsum("hqk,khe->qhe", grad_scores, keys_in, precision=highest))
        grad_keys = grad_keys + jnp.einsum(
            "hqk,qhe->khe", grad_scores, query_block, precision=highest
        )
    return (jnp.concatenate(grad_queries, axis=0), grad_keys, grad_values)


def pack_rows(source, send_index, send_valid):
    row_width = source.shape[1]
    picked = jnp.take(source, send_index.reshape(-1), axis=0).reshape(
        send_index.shape[0], send_index.shape[1], row_width
    )
    return jnp.where(send_valid[:, :, None], picked, 0.0)


def unpack_rows(arrived, source_slots):
    return jnp.take(arrived.reshape(-1, arrived.shape[2]), source_slots, axis=0)


def place_back(grads_in, source_slots, sender_count, slot_cap):
    row_width = grads_in.shape[1]
    holder = (
        jnp.zeros((sender_count * slot_cap, row_width), jnp.float32).at[source_slots].set(grads_in)
    )
    return holder.reshape(sender_count, slot_cap, row_width)


def return_rows(returned, send_index, send_valid, tok_rows):
    row_width = returned.shape[2]
    masked = jnp.where(send_valid[:, :, None], returned, 0.0).reshape(-1, row_width)
    return jnp.zeros((tok_rows, row_width), jnp.float32).at[send_index.reshape(-1)].add(masked)


def branch_total(partial_sum):
    return lax.psum(partial_sum, "mp")


def input_total(partial_sum):
    return lax.psum(partial_sum, "mp")


def part_squares(arrays, divisor):
    return jnp.concatenate(
        [
            jnp.sum(arrays[0] * arrays[0], axis=(1, 2)),
            jnp.sum(arrays[1] * arrays[1], axis=(1, 2)),
            jnp.sum(arrays[2] * arrays[2])[None],
            jnp.sum(arrays[3] * arrays[3])[None],
            jnp.sum(arrays[4] * arrays[4], axis=1) / divisor,
            jnp.sum(arrays[5] * arrays[5])[None],
        ]
    )


def spread_parts(per_part):
    return (
        per_part[0:6][:, None, None],
        per_part[6:8][:, None, None],
        per_part[8],
        per_part[9],
        per_part[10:17][:, None],
        per_part[17],
    )


def shards(
    layer_input,
    encoder_memory,
    output_grad,
    target_lengths,
    memory_lengths,
    source_slots,
    pair_counts,
    attend_input,
    attend_output,
    expand_weight,
    reduce_weight,
    norm_vectors,
    expand_bias,
    attend_input_first,
    attend_input_second,
    attend_output_first,
    attend_output_second,
    expand_weight_first,
    expand_weight_second,
    reduce_weight_first,
    reduce_weight_second,
    norm_vectors_first,
    norm_vectors_second,
    expand_bias_first,
    expand_bias_second,
):
    data_count = lax.axis_size("dp")
    model_count = lax.axis_size("mp")
    my_index = lax.axis_index("dp")
    tok_rows = layer_input.shape[0]
    full_input, full_output, full_expand, full_reduce, full_vectors, full_bias = (
        lax.all_gather(attend_input, "dp", axis=1, tiled=True),
        lax.all_gather(attend_output, "dp", axis=2, tiled=True),
        lax.all_gather(expand_weight, "dp", axis=0, tiled=True),
        lax.all_gather(reduce_weight, "dp", axis=1, tiled=True),
        lax.all_gather(norm_vectors, "dp", axis=1, tiled=True),
        lax.all_gather(expand_bias, "dp", axis=0, tiled=True),
    )
    local_heads = full_input.shape[2] // HD
    tok_seg = segment_ids(target_lengths[0], tok_rows)
    mem_seg = segment_ids(memory_lengths[0], tok_rows)
    extra_slots = tok_rows // 16
    slot_cap = (tok_rows - data_count // 4 * extra_slots) // data_count + extra_slots
    my_counts = lax.dynamic_index_in_dim(pair_counts, my_index, 0, keepdims=False)
    my_starts = jnp.cumsum(my_counts) - my_counts
    slot_ids = jnp.arange(slot_cap, dtype=jnp.int32)
    send_valid = slot_ids[None, :] < my_counts[:, None]
    send_index = jnp.where(send_valid, my_starts[:, None] + slot_ids[None, :], 0)
    whole_memory = lax.all_gather(encoder_memory, "mp", axis=1, tiled=True)
    arrived = lax.all_to_all(
        pack_rows(whole_memory, send_index, send_valid),
        "dp",
        split_axis=0,
        concat_axis=0,
        tiled=True,
    )
    memory_target = unpack_rows(arrived, source_slots)

    def split_heads(values):
        return values.reshape(values.shape[0], local_heads, HD)

    def merge_heads(values):
        return values.reshape(values.shape[0], local_heads * HD)

    self_query = split_heads(matmul(layer_input, full_input[0]))
    self_key = split_heads(matmul(layer_input, full_input[1]))
    self_value = split_heads(matmul(layer_input, full_input[2]))
    self_heads, self_totals = attend(self_query, self_key, self_value, tok_seg, tok_seg)
    self_flat = merge_heads(self_heads)
    self_mix = branch_total(matmul(self_flat, full_output[0]))
    first_norm, first_back = jax.vjp(
        layer_norm, layer_input + self_mix, full_vectors[0], full_vectors[3]
    )
    cross_query = split_heads(matmul(first_norm, full_input[3]))
    cross_key = split_heads(matmul(memory_target, full_input[4]))
    cross_value = split_heads(matmul(memory_target, full_input[5]))
    cross_heads, cross_totals = attend(cross_query, cross_key, cross_value, tok_seg, mem_seg)
    cross_flat = merge_heads(cross_heads)
    cross_mix = branch_total(matmul(cross_flat, full_output[1]))
    second_norm, second_back = jax.vjp(
        layer_norm, first_norm + cross_mix, full_vectors[1], full_vectors[4]
    )
    expand_pre = matmul(second_norm, full_expand) + full_bias
    expanded, gelu_back = jax.vjp(apply_gelu, expand_pre)
    reduced = branch_total(matmul(expanded, full_reduce))
    layer_output, third_back = jax.vjp(
        layer_norm, second_norm + reduced + full_vectors[6], full_vectors[2], full_vectors[5]
    )
    resid_three_grad, gain_three, shift_three = third_back(output_grad)
    reduce_bias_grad = jnp.sum(resid_three_grad, axis=0)
    grad_reduce = matmul(expanded.T, resid_three_grad)
    (pre_grad,) = gelu_back(matmul(resid_three_grad, full_reduce.T))
    grad_expand = matmul(second_norm.T, pre_grad)
    grad_bias = jnp.sum(pre_grad, axis=0)
    second_grad = resid_three_grad + input_total(matmul(pre_grad, full_expand.T))
    resid_two_grad, gain_two, shift_two = second_back(second_grad)
    grad_cross_out = matmul(cross_flat.T, resid_two_grad)
    cross_out_grad = split_heads(matmul(resid_two_grad, full_output[1].T))
    cross_query_grad, cross_key_grad, cross_value_grad = attend_back(
        cross_query,
        cross_key,
        cross_value,
        cross_heads,
        cross_totals,
        cross_out_grad,
        tok_seg,
        mem_seg,
    )
    cross_query_flat = merge_heads(cross_query_grad)
    cross_key_flat = merge_heads(cross_key_grad)
    cross_value_flat = merge_heads(cross_value_grad)
    grad_cross_query = matmul(first_norm.T, cross_query_flat)
    grad_cross_key = matmul(memory_target.T, cross_key_flat)
    grad_cross_value = matmul(memory_target.T, cross_value_flat)
    first_grad = resid_two_grad + input_total(matmul(cross_query_flat, full_input[3].T))
    memory_partial = matmul(cross_key_flat, full_input[4].T) + matmul(
        cross_value_flat, full_input[5].T
    )
    resid_one_grad, gain_one, shift_one = first_back(first_grad)
    grad_self_out = matmul(self_flat.T, resid_one_grad)
    self_out_grad = split_heads(matmul(resid_one_grad, full_output[0].T))
    self_query_grad, self_key_grad, self_value_grad = attend_back(
        self_query, self_key, self_value, self_heads, self_totals, self_out_grad, tok_seg, tok_seg
    )
    self_query_flat = merge_heads(self_query_grad)
    self_key_flat = merge_heads(self_key_grad)
    self_value_flat = merge_heads(self_value_grad)
    grad_self_query = matmul(layer_input.T, self_query_flat)
    grad_self_key = matmul(layer_input.T, self_key_flat)
    grad_self_value = matmul(layer_input.T, self_value_flat)
    input_grad = resid_one_grad + input_total(
        matmul(self_query_flat, full_input[0].T)
        + matmul(self_key_flat, full_input[1].T)
        + matmul(self_value_flat, full_input[2].T)
    )
    returned = lax.all_to_all(
        place_back(memory_partial, source_slots, data_count, slot_cap),
        "dp",
        split_axis=0,
        concat_axis=0,
        tiled=True,
    )
    memory_grad = lax.psum_scatter(
        return_rows(returned, send_index, send_valid, tok_rows),
        "mp",
        scatter_dimension=1,
        tiled=True,
    )
    grad_input = jnp.stack(
        [
            grad_self_query,
            grad_self_key,
            grad_self_value,
            grad_cross_query,
            grad_cross_key,
            grad_cross_value,
        ]
    )
    grad_output = jnp.stack([grad_self_out, grad_cross_out])
    grad_vectors = jnp.stack(
        [gain_one, gain_two, gain_three, shift_one, shift_two, shift_three, reduce_bias_grad]
    )
    grad_shards = (
        lax.psum_scatter(grad_input, "dp", scatter_dimension=1, tiled=True),
        lax.psum_scatter(grad_output, "dp", scatter_dimension=2, tiled=True),
        lax.psum_scatter(grad_expand, "dp", scatter_dimension=0, tiled=True),
        lax.psum_scatter(grad_reduce, "dp", scatter_dimension=1, tiled=True),
        lax.psum_scatter(grad_vectors, "dp", scatter_dimension=1, tiled=True),
        lax.psum_scatter(grad_bias, "dp", scatter_dimension=0, tiled=True),
    )
    weights = (attend_input, attend_output, expand_weight, reduce_weight, norm_vectors, expand_bias)
    firsts = (
        attend_input_first,
        attend_output_first,
        expand_weight_first,
        reduce_weight_first,
        norm_vectors_first,
        expand_bias_first,
    )
    seconds = (
        attend_input_second,
        attend_output_second,
        expand_weight_second,
        reduce_weight_second,
        norm_vectors_second,
        expand_bias_second,
    )
    total_square, weight_square = lax.psum(
        (jnp.sum(part_squares(grad_shards, model_count)), part_squares(weights, model_count)),
        ("dp", "mp"),
    )
    grad_norm = jnp.sqrt(total_square)
    clip_factor = jnp.minimum(1.0, clip_norm / grad_norm)
    steps_done = jnp.float32(STEP_NUM)
    step_rate = peak_rate * jnp.minimum(steps_done / warm_steps, jnp.sqrt(warm_steps / steps_done))
    first_fix = 1.0 - first_decay**steps_done
    second_fix = 1.0 - second_decay**steps_done
    new_firsts = []
    new_seconds = []
    updates = []
    for number in range(6):
        clipped = grad_shards[number] * clip_factor
        moment_one = first_decay * firsts[number] + (1.0 - first_decay) * clipped
        moment_two = second_decay * seconds[number] + (1.0 - second_decay) * clipped * clipped
        decay_rate = matrix_decay if number < 4 else 0.0
        updates.append(
            moment_one / first_fix / (jnp.sqrt(moment_two / second_fix) + adam_eps)
            + decay_rate * weights[number]
        )
        new_firsts.append(moment_one)
        new_seconds.append(moment_two)
    update_square = lax.psum(part_squares(updates, model_count), ("dp", "mp"))
    ratios = spread_parts(jnp.sqrt(weight_square) / jnp.sqrt(update_square))
    new_weights = [
        weights[number] - step_rate * ratios[number] * updates[number] for number in range(6)
    ]
    matrix_norms = jnp.stack([jnp.sqrt(weight_square[:10]), jnp.sqrt(update_square[:10])])
    return (
        layer_output,
        input_grad,
        memory_grad,
        grad_norm[None],
        new_weights[0],
        new_weights[1],
        new_weights[2],
        new_weights[3],
        new_weights[4],
        new_weights[5],
        new_weights[0].astype(jnp.bfloat16),
        new_weights[1].astype(jnp.bfloat16),
        new_weights[2].astype(jnp.bfloat16),
        new_weights[3].astype(jnp.bfloat16),
        new_firsts[0],
        new_seconds[0],
        new_firsts[1],
        new_seconds[1],
        new_firsts[2],
        new_seconds[2],
        new_firsts[3],
        new_seconds[3],
        new_firsts[4],
        new_seconds[4],
        new_firsts[5],
        new_seconds[5],
        matrix_norms,
    )


def solution(mesh):
    in_specs = (
        P("dp", None),
        P("dp", "mp"),
        P("dp", None),
        P("dp", None),
        P("dp", None),
        P("dp"),
        P(),
        P(None, "dp", "mp"),
        P(None, "mp", "dp"),
        P("dp", "mp"),
        P("mp", "dp"),
        P(None, "dp"),
        P(("mp", "dp")),
        P(None, "dp", "mp"),
        P(None, "dp", "mp"),
        P(None, "mp", "dp"),
        P(None, "mp", "dp"),
        P("dp", "mp"),
        P("dp", "mp"),
        P("mp", "dp"),
        P("mp", "dp"),
        P(None, "dp"),
        P(None, "dp"),
        P(("mp", "dp")),
        P(("mp", "dp")),
    )
    out_specs = (
        P("dp", None),
        P("dp", None),
        P("dp", "mp"),
        P(),
        P(None, "dp", "mp"),
        P(None, "mp", "dp"),
        P("dp", "mp"),
        P("mp", "dp"),
        P(None, "dp"),
        P(("mp", "dp")),
        P(None, "dp", "mp"),
        P(None, "mp", "dp"),
        P("dp", "mp"),
        P("mp", "dp"),
        P(None, "dp", "mp"),
        P(None, "dp", "mp"),
        P(None, "mp", "dp"),
        P(None, "mp", "dp"),
        P("dp", "mp"),
        P("dp", "mp"),
        P("mp", "dp"),
        P("mp", "dp"),
        P(None, "dp"),
        P(None, "dp"),
        P(("mp", "dp")),
        P(("mp", "dp")),
        P(),
    )
    return jax.shard_map(shards, mesh=mesh, in_specs=in_specs, out_specs=out_specs, check_vma=False)
```

profile of v0, /device:TPU:0, one launch (start us, length us, event | category | flops | bytes accessed | tf_op | source)
XLA Modules:
  0.0 1049.5 jit_solution(8128215545025435978)
XLA Ops:
  11.7 14.6 %all_gather.22 = f32[2,128,512]{1,2,0:T(8,128)} all-gather(f32[2,128,64]{1,2,0:T(8,128)} %param.33), channel_id=1, replica_groups=mesh['dp'=8,'mp'=4] {'dp'}, dimensions={2}, use_global_device_ids=true | all-gather | bytes 589824 | tf_op jit(solution)/shard_map/all_gather | solution.py:194
  28.3 10.8 %all-gather.6.cloned.1.call-done = f32[6,512,128]{2,1,0:T(8,128)} async-done(((f32[6,64,128]{2,1,0:T(8,128)}), f32[6,512,128]{2,1,0:T(8,128)}) %all-gather.6.cloned.1.call-update) | async-done | bytes 1572880 | tf_op jit(solution)/shard_map/all_gather | solution.py:193
  39.1 3.4 fusion.175
  45.8 3.2 fusion.29
  49.0 5.2 fusion.16
  56.7 4.5 fusion.17
  63.6 5.2 fusion.115
  68.9 5.2 fusion.112
  79.9 7.0 all-gather.8.cloned.1.call-done
  86.9 6.6 gather_fusion
  95.5 3.8 all-to-all-start
  99.3 38.2 %all-gather = f32[8,64,7]{1,2,0:T(8,128)S(1)} all-gather(f32[1,64,7]{1,2,0:T(8,128)S(1)} %bitcast.311), channel_id=1, replica_groups=mesh['dp'=8,'mp'=4] {'dp'}, dimensions={0}, use_global_device_ids=true | all-gather | bytes 16128 | tf_op jit(solution)/shard_map/all_gather | solution.py:197
  141.3 33.3 %all-reduce.12.cloned.1.call-done = f32[1024,512]{1,0:T(8,128)} async-done(((f32[1024,512]{1,0:T(8,128)}), f32[1024,512]{1,0:T(8,128)}) %all-reduce.12.cloned.1.call-update) | async-done | bytes 2097168 | tf_op jit(solution)/shard_map/psum | solution.py:130
  177.5 3.9 fusion.129
  182.3 5.0 gather_fusion.1
  187.3 4.1 fusion.25
  194.0 4.1 fusion.19
  200.0 5.4 fusion.121
  205.4 4.1 fusion.18
  211.5 5.2 fusion.118
  224.1 14.8 %all-reduce = f32[512]{0:T(512)S(1)} all-reduce(f32[512]{0:T(512)S(1)} %dynamic-update-slice), channel_id=1, replica_groups=mesh['dp'=8,'mp'=4] {'dp'}, use_global_device_ids=true, to_apply=%add | all-reduce | flops 512 | bytes 4096
  238.9 68.1 %all-reduce.14.cloned.1.call-done = f32[1024,512]{1,0:T(8,128)} async-done(((f32[1024,512]{1,0:T(8,128)}), f32[1024,512]{1,0:T(8,128)}) %all-reduce.14.cloned.1.call-update) | async-done | bytes 2097168 | tf_op jit(solution)/shard_map/psum | solution.py:130
  307.0 3.4 fusion.237
  312.4 18.8 %all-gather.10.cloned.1.call-done = f32[512,512]{1,0:T(8,128)} async-done(((f32[64,512]{1,0:T(8,128)}), f32[512,512]{1,0:T(8,128)}) %all-gather.10.cloned.1.call-update) | async-done | bytes 1048592 | tf_op jit(solution)/shard_map/all_gather | solution.py:195
  331.2 6.9 fusion.131
  338.1 18.4 %all-gather.12.cloned.1.call-done = f32[512,512]{0,1:T(8,128)} async-done(((f32[512,64]{0,1:T(8,128)}), f32[512,512]{0,1:T(8,128)}) %all-gather.12.cloned.1.call-update) | async-done | bytes 1048592 | tf_op jit(solution)/shard_map/all_gather | solution.py:196
  356.5 7.2 fusion.164
  363.8 86.6 %all-reduce.16.cloned.1.call-done = f32[1024,512]{1,0:T(8,128)} async-done(((f32[1024,512]{1,0:T(8,128)}), f32[1024,512]{1,0:T(8,128)}) %all-reduce.16.cloned.1.call-update) | async-done | bytes 2097168 | tf_op jit(solution)/shard_map/psum | solution.py:130
  458.1 5.2 fusion.251
  464.7 4.8 fusion.252
  469.6 85.5 %all-reduce.18.cloned.1.call-done = f32[1024,512]{1,0:T(8,128)} async-done(((f32[1024,512]{1,0:T(8,128)}), f32[1024,512]{1,0:T(8,128)}) %all-reduce.18.cloned.1.call-update) | async-done | bytes 2097168 | tf_op jit(solution)/shard_map/psum | solution.py:134
  555.1 3.7 multiply_reduce_fusion.1
  564.4 4.8 multiply_multiply_fusion.2
  569.2 4.2 convolution_bitcast_fusion.6
  573.4 5.2 multiply_multiply_fusion.3
  578.7 4.2 convolution_bitcast_fusion.7
  582.9 4.3 fusion.177
  587.4 7.6 fusion.79
  595.2 7.1 fusion.130
  602.6 4.0 fusion.106
  606.5 6.0 fusion.12
  615.3 4.5 fusion.93
  619.7 3.9 convolution_add_fusion
  623.6 49.2 %all-reduce.20.cloned.1.call-done = f32[1024,512]{1,0:T(8,128)} async-done(((f32[1024,512]{1,0:T(8,128)}), f32[1024,512]{1,0:T(8,128)}) %all-reduce.20.cloned.1.call-update) | async-done | bytes 2097168 | tf_op jit(solution)/shard_map/psum | solution.py:134
  680.8 4.8 multiply_multiply_fusion.1
  685.7 4.9 convolution_bitcast_fusion.5
  690.6 3.6 fusion.253
  695.1 7.2 multiply_multiply_fusion
  702.3 4.2 convolution_bitcast_fusion.4
  714.3 3.6 fusion.14
  718.0 3.6 fusion.92
  740.6 4.1 fusion.167
  744.7 7.4 scatter_custom_fusion
  752.1 3.8 all-to-all-start.1
  762.0 4.3 add_add_fusion.3
  767.9 30.7 %all-reduce.2 = f32[512]{0:T(512)S(1)} all-reduce(f32[512]{0:T(512)S(1)} %get-tuple-element.278), channel_id=8, replica_groups=mesh['dp'=8,'mp'=4] {'dp'}, use_global_device_ids=true, to_apply=%region_55.56.clone | all-reduce | flops 512 | bytes 4096
  803.9 46.1 %all-reduce.24.cloned.1.call-done = f32[2,128,512]{1,0,2:T(2,128)} async-done(((f32[2,128,512]{1,0,2:T(2,128)}), f32[2,128,512]{1,0,2:T(2,128)}) %all-reduce.24.cloned.1.call-update) | async-done | bytes 524304
  853.5 12.1 %scatter_custom_fusion.1 = f32[1024,512]{1,0:T(8,128)} fusion(s32[1408]{0:T(1024)S(1)} %fusion.186, f32[1408,512]{1,0:T(8,128)} %bitcast.274, f32[]{:T(128)} %constant.55.clone.1), kind=kCustom, calls=%fused_computation.168 | custom fusion | flops 720896 | bytes 2097664 | tf_op jit(solution)/shard_map/scatter-add | solution.py:126
  865.6 28.5 %reduce-scatter.10.cloned.1.call-done = f32[6,64,128]{2,0,1:T(8,128)} async-done(((f32[6,512,128]{2,0,1:T(8,128)}), f32[6,64,128]{2,0,1:T(8,128)}) %reduce-scatter.10.cloned.1.call-update) | async-done | bytes 196624 | tf_op jit(solution)/shard_map/reduce_scatter | solution.py:325
  899.7 43.2 %psum.69 = f32[]{:T(128)} all-reduce(f32[]{:T(128)S(6)} %reduce_sum.525), channel_id=1, replica_groups=mesh['dp'=8,'mp'=4] {'dp','mp'}, use_global_device_ids=true, to_apply=%region_57.58 | all-reduce | flops 1 | bytes 8 | tf_op jit(solution)/shard_map/psum | solution.py:349
  951.5 3.2 concatenate.23
  961.3 23.1 %all-reduce.22.cloned.1.call-done = f32[1024,512]{1,0:T(8,128)} async-done(((f32[1024,512]{1,0:T(8,128)}), f32[1024,512]{1,0:T(8,128)}) %all-reduce.22.cloned.1.call-update) | async-done | bytes 2097168 | tf_op jit(solution)/shard_map/psum | solution.py:134
  984.4 3.2 add_add_fusion.5
  987.7 43.3 %all-reduce.3 = (f32[18]{0:T(128)S(1)}, f32[18]{0:T(128)S(1)}) all-reduce(f32[18]{0:T(128)S(1)} %concatenate.24, f32[18]{0:T(128)S(1)} %copy-done.114), channel_id=1, replica_groups=mesh['dp'=8,'mp'=4] {'dp','mp'}, use_global_device_ids=true, to_apply=%region_71.72 | all-reduce | flops 36 | bytes 288 | tf_op jit(solution)/shard_map/psum | solution.py:373
  (405 shorter events, 138.4 us)
Async XLA Ops:
  7.2 31.9 %copy-start = (f32[1024,512]{1,0:T(8,128)S(1)}, f32[1024,512]{1,0:T(8,128)}, u32[]{:S(2)}) copy-start(f32[1024,512]{1,0:T(8,128)} %param.25) | copy-start | bytes 6291460
  7.2 31.9 %all-gather.6.cloned.1.call-start = ((), (), s32[]{:S(2)}) async-start(), calls=%async_computation.7 | async-start | bytes 1769472 | tf_op jit(solution)/shard_map/all_gather | solution.py:193
  7.9 79.0 %all-gather.8.cloned.1.call-start = ((), (), s32[]{:S(2)}) async-start(), calls=%async_computation.9 | async-start | bytes 2621440 | tf_op jit(solution)/shard_map/all_gather | solution.py:210
  8.7 165.9 %all-reduce.12.cloned.1.call-start = ((), (), s32[]{:S(2)}) async-start(), calls=%async_computation.8 | async-start | bytes 4194304 | tf_op jit(solution)/shard_map/psum | solution.py:130
  28.3 35.3 %copy-start.24 = (pred[512,1024]{1,0:T(8,128)(4,1)}, pred[512,1024]{1,0:T(8,128)(4,1)S(1)}, u32[]{:S(2)}) copy-start(pred[512,1024]{1,0:T(8,128)(4,1)S(1)} %get-tuple-element.253) | copy-start | bytes 1572868
  43.2 5.8 copy-start.55
  54.3 14.6 %copy-start.6 = (f32[2,512,1024]{2,1,0:T(8,128)}, f32[2,512,1024]{2,1,0:T(8,128)S(1)}, u32[]{:S(2)}) copy-start(f32[2,512,1024]{2,1,0:T(8,128)S(1)} %get-tuple-element.269) | copy-start | bytes 12582916
  56.6 12.3 %copy-start.38 = (f32[1024,2,64]{0,2,1:T(8,128)}, f32[1024,2,64]{0,2,1:T(8,128)S(1)}, u32[]{:S(2)}) copy-start(f32[1024,2,64]{0,2,1:T(8,128)S(1)} %fusion.31) | copy-start | bytes 1572868
  68.9 5.3 copy-start.82
  68.9 6.8 copy-start.49
  95.5 42.2 %copy-start.104 = (s32[1024]{0:T(1024)S(1)}, s32[1024]{0:T(1024)}, u32[]{:S(2)}) copy-start(s32[1024]{0:T(1024)} %param.30) | copy-start | bytes 12292
  95.5 86.8 %all-to-all-start = ((f32[8,176,512]{2,1,0:T(8,128)}), f32[8,176,512]{2,1,0:T(8,128)S(1)}, u32[]{:S(2)}, u32[]{:S(2)}) async-start(f32[8,176,512]{2,1,0:T(8,128)} %select_select_fusion), calls=%async_computation | async-start | bytes 5767168 | tf_op jit(solution)/shard_map/all_to_all | solution.py:211
  99.3 207.7 %all-reduce.14.cloned.1.call-start = ((), (), s32[]{:S(2)}) async-start(), calls=%async_computation.10 | async-start | bytes 4194304 | tf_op jit(solution)/shard_map/psum | solution.py:130
  193.9 16.7 %copy-start.40 = (f32[1024,2,64]{0,2,1:T(8,128)}, f32[1024,2,64]{0,2,1:T(8,128)S(1)}, u32[]{:S(2)}) copy-start(f32[1024,2,64]{0,2,1:T(8,128)S(1)} %fusion.27) | copy-start | bytes 1572868
  200.0 5.4 copy-start.32
  200.0 5.4 copy-start.57
  205.4 11.2 %copy-start.86 = (f32[512,2,64]{0,2,1:T(8,128)}, f32[512,2,64]{0,2,1:T(8,128)S(1)}, u32[]{:S(2)}) copy-start(f32[512,2,64]{0,2,1:T(8,128)S(1)} %fusion.121) | copy-start | bytes 786436
  211.5 6.7 copy-start.50
  218.1 5.7 copy-start.110
  218.1 88.9 %copy-start.3 = (f32[1024,512]{1,0:T(8,128)S(1)}, f32[1024,512]{1,0:T(8,128)}, u32[]{:S(2)}) copy-start(f32[1024,512]{1,0:T(8,128)} %copy-done.2) | copy-start | bytes 6291460
  221.3 109.9 %all-gather.10.cloned.1.call-start = ((), (), s32[]{:S(2)}) async-start(), calls=%async_computation.11 | async-start | bytes 1179648 | tf_op jit(solution)/shard_map/all_gather | solution.py:195
  221.9 134.6 %all-gather.12.cloned.1.call-start = ((), (), s32[]{:S(2)}) async-start(), calls=%async_computation.12 | async-start | bytes 1179648 | tf_op jit(solution)/shard_map/all_gather | solution.py:196
  222.5 227.9 %all-reduce.16.cloned.1.call-start = ((), (), s32[]{:S(2)}) async-start(), calls=%async_computation.13 | async-start | bytes 4194304 | tf_op jit(solution)/shard_map/psum | solution.py:130
  363.7 191.4 %all-reduce.18.cloned.1.call-start = ((), (), s32[]{:S(2)}) async-start(), calls=%async_computation.14 | async-start | bytes 4194304 | tf_op jit(solution)/shard_map/psum | solution.py:134
  458.1 6.6 copy-start.53
  469.5 203.3 %all-reduce.20.cloned.1.call-start = ((), (), s32[]{:S(2)}) async-start(), calls=%async_computation.15 | async-start | bytes 4194304 | tf_op jit(solution)/shard_map/psum | solution.py:134
  558.8 5.3 copy-start.30
  558.8 5.3 copy-start.41
  564.1 9.3 copy-start.73
  587.2 212.0 %reduce-scatter.14.cloned.1.call-start = ((), (), s32[]{:S(2)}) async-start(), calls=%async_computation.20 | async-start | bytes 1179648 | tf_op jit(solution)/shard_map/reduce_scatter | solution.py:328
  595.1 205.7 %reduce-scatter.12.cloned.1.call-start = ((), (), s32[]{:S(2)}) async-start(), calls=%async_computation.19 | async-start | bytes 1179648 | tf_op jit(solution)/shard_map/reduce_scatter | solution.py:327
  602.3 200.0 %reduce-scatter.16.cloned.1.call-start = ((), (), s32[]{:S(2)}) async-start(), calls=%async_computation.21 | async-start | bytes 294912
  606.5 6.0 copy-start.19
  725.8 124.2 %all-reduce.24.cloned.1.call-start = ((), (), s32[]{:S(2)}) async-start(), calls=%async_computation.22 | async-start | bytes 1048576
  730.4 163.7 %reduce-scatter.10.cloned.1.call-start = ((), (), s32[]{:S(2)}) async-start(), calls=%async_computation.18 | async-start | bytes 2359296 | tf_op jit(solution)/shard_map/reduce_scatter | solution.py:325
  752.1 99.4 %all-to-all-start.1 = ((f32[8,176,512]{2,1,0:T(8,128)}), f32[8,176,512]{2,1,0:T(8,128)S(1)}, u32[]{:S(2)}, u32[]{:S(2)}) async-start(f32[8,176,512]{2,1,0:T(8,128)} %bitcast.68), calls=%async_computation.1 | async-start | bytes 5767168 | tf_op jit(solution)/shard_map/all_to_all | solution.py:297
  755.9 228.5 %all-reduce.22.cloned.1.call-start = ((), (), s32[]{:S(2)}) async-start(), calls=%async_computation.16 | async-start | bytes 4194304 | tf_op jit(solution)/shard_map/psum | solution.py:134
  766.3 275.3 %reduce-scatter.8.cloned.1.call-start = ((), (), s32[]{:S(2)}) async-start(), calls=%async_computation.17 | async-start | bytes 2621440 | tf_op jit(solution)/shard_map/reduce_scatter | solution.py:304
  853.4 90.2 %copy-start.111 = (f32[64]{0:T(128)S(1)}, f32[64]{0:T(128)}, u32[]{:S(2)}) copy-start(f32[64]{0:T(128)} %param.37) | copy-start | bytes 772
  853.4 90.2 %copy-start.115 = (f32[64]{0:T(128)S(1)}, f32[64]{0:T(128)}, u32[]{:S(2)}) copy-start(f32[64]{0:T(128)} %param.49) | copy-start | bytes 772
  853.4 90.2 %copy-start.116 = (f32[64]{0:T(128)S(1)}, f32[64]{0:T(128)}, u32[]{:S(2)}) copy-start(f32[64]{0:T(128)} %param.48) | copy-start | bytes 772
  853.4 91.4 %copy-start.107 = (f32[7,64]{1,0:T(8,128)S(1)}, f32[7,64]{1,0:T(8,128)}, u32[]{:S(2)}) copy-start(f32[7,64]{1,0:T(8,128)} %param.47) | copy-start | bytes 5380
  853.4 91.4 %copy-start.108 = (f32[7,64]{1,0:T(8,128)S(1)}, f32[7,64]{1,0:T(8,128)}, u32[]{:S(2)}) copy-start(f32[7,64]{1,0:T(8,128)} %param.46) | copy-start | bytes 5380
  853.4 92.1 %copy-start.91 = (f32[2,128,64]{1,2,0:T(8,128)S(1)}, f32[2,128,64]{1,2,0:T(8,128)}, u32[]{:S(2)}) copy-start(f32[2,128,64]{1,2,0:T(8,128)} %param.33) | copy-start | bytes 196612
  853.4 92.1 %copy-start.101 = (f32[2,128,64]{1,2,0:T(8,128)S(1)}, f32[2,128,64]{1,2,0:T(8,128)}, u32[]{:S(2)}) copy-start(f32[2,128,64]{1,2,0:T(8,128)} %param.41) | copy-start | bytes 196612
  853.5 92.1 %copy-start.102 = (f32[2,128,64]{1,2,0:T(8,128)S(1)}, f32[2,128,64]{1,2,0:T(8,128)}, u32[]{:S(2)}) copy-start(f32[2,128,64]{1,2,0:T(8,128)} %param.40) | copy-start | bytes 196612
  853.5 93.3 %copy-start.70 = (f32[64,512]{1,0:T(8,128)S(1)}, f32[64,512]{1,0:T(8,128)}, u32[]{:S(2)}) copy-start(f32[64,512]{1,0:T(8,128)} %param.34) | copy-start | bytes 393220
  853.5 93.3 %copy-start.93 = (f32[64,512]{1,0:T(8,128)S(1)}, f32[64,512]{1,0:T(8,128)}, u32[]{:S(2)}) copy-start(f32[64,512]{1,0:T(8,128)} %reduce-scatter.12.cloned.1.call-done) | copy-start | bytes 393220
  853.5 93.3 %copy-start.100 = (f32[64,512]{1,0:T(8,128)S(1)}, f32[64,512]{1,0:T(8,128)}, u32[]{:S(2)}) copy-start(f32[64,512]{1,0:T(8,128)} %param.43) | copy-start | bytes 393220
  865.6 83.5 %copy-start.69 = (f32[512,64]{0,1:T(8,128)S(1)}, f32[512,64]{0,1:T(8,128)}, u32[]{:S(2)}) copy-start(f32[512,64]{0,1:T(8,128)} %param.35) | copy-start | bytes 393220
  865.6 83.5 %copy-start.92 = (f32[512,64]{0,1:T(8,128)S(1)}, f32[512,64]{0,1:T(8,128)}, u32[]{:S(2)}) copy-start(f32[512,64]{0,1:T(8,128)} %reduce-scatter.14.cloned.1.call-done) | copy-start | bytes 393220
  895.7 60.1 %copy-start.79 = (f32[6,64,128]{2,0,1:T(8,128)S(1)}, f32[6,64,128]{2,0,1:T(8,128)}, u32[]{:S(2)}) copy-start(f32[6,64,128]{2,0,1:T(8,128)} %reduce-scatter.10.cloned.1.call-done) | copy-start | bytes 589828
  899.7 84.7 %copy-start.22 = (f32[1024,512]{1,0:T(8,128)S(1)}, f32[1024,512]{1,0:T(8,128)}, u32[]{:S(2)}) copy-start(f32[1024,512]{1,0:T(8,128)} %copy-done.20) | copy-start | bytes 6291460
  945.5 93.2 %copy-start.105 = (f32[7,64]{1,0:T(8,128)}, f32[7,64]{1,0:T(8,128)S(1)}, u32[]{:S(2)}) copy-start(f32[7,64]{1,0:T(8,128)S(1)} %get-tuple-element.193) | copy-start | bytes 5380
  945.5 93.2 %copy-start.106 = (f32[7,64]{1,0:T(8,128)}, f32[7,64]{1,0:T(8,128)S(1)}, u32[]{:S(2)}) copy-start(f32[7,64]{1,0:T(8,128)S(1)} %get-tuple-element.194) | copy-start | bytes 5380
  949.0 91.8 %copy-start.94 = (f32[64,512]{1,0:T(8,128)}, f32[64,512]{1,0:T(8,128)S(1)}, u32[]{:S(2)}) copy-start(f32[64,512]{1,0:T(8,128)S(1)} %get-tuple-element.197) | copy-start | bytes 393220
  961.3 26.3 %copy-start.114 = (f32[18]{0:T(128)S(1)}, f32[18]{0:T(128)}, u32[]{:S(2)}) copy-start(f32[18]{0:T(128)} %concatenate.23) | copy-start | bytes 220
  987.6 50.6 %copy-start.112 = (f32[64]{0:T(128)S(1)}, f32[64]{0:T(128)}, u32[]{:S(2)}) copy-start(f32[64]{0:T(128)} %param.37) | copy-start | bytes 772
  987.6 50.6 %copy-start.113 = (f32[64]{0:T(128)S(1)}, f32[64]{0:T(128)}, u32[]{:S(2)}) copy-start(f32[64]{0:T(128)} %get-tuple-element.190) | copy-start | bytes 772
  987.6 51.8 %copy-start.98 = (f32[2,128,64]{1,2,0:T(8,128)S(1)}, f32[2,128,64]{1,2,0:T(8,128)}, u32[]{:S(2)}) copy-start(f32[2,128,64]{1,2,0:T(8,128)} %get-tuple-element.199) | copy-start | bytes 196612
  987.6 51.7 %copy-start.99 = (f32[2,128,64]{1,2,0:T(8,128)S(1)}, f32[2,128,64]{1,2,0:T(8,128)}, u32[]{:S(2)}) copy-start(f32[2,128,64]{1,2,0:T(8,128)} %get-tuple-element.200) | copy-start | bytes 196612
  987.6 52.5 %copy-start.96 = (f32[512,64]{0,1:T(8,128)S(1)}, f32[512,64]{0,1:T(8,128)}, u32[]{:S(2)}) copy-start(f32[512,64]{0,1:T(8,128)} %get-tuple-element.195) | copy-start | bytes 393220
  987.6 52.4 %copy-start.97 = (f32[512,64]{0,1:T(8,128)S(1)}, f32[512,64]{0,1:T(8,128)}, u32[]{:S(2)}) copy-start(f32[512,64]{0,1:T(8,128)} %get-tuple-element.196) | copy-start | bytes 393220
  987.6 53.2 %copy-start.95 = (f32[64,512]{1,0:T(8,128)S(1)}, f32[64,512]{1,0:T(8,128)}, u32[]{:S(2)}) copy-start(f32[64,512]{1,0:T(8,128)} %get-tuple-element.198) | copy-start | bytes 393220
  (72 other events, 221.6 us)
Sparse Core Ops, SparseCore 0:
  10.0 29.0 all-gather.5
  40.6 46.2 all-gather.7
  89.9 84.6 all-reduce.11
  221.4 85.5 all-reduce.13
  308.7 22.4 all-gather.9
  332.9 23.4 all-gather.11
  363.8 86.4 all-reduce.15
  469.6 85.4 all-reduce.17
  587.3 85.4 all-reduce.19
  676.2 35.0 reduce-scatter.13
  714.7 35.9 reduce-scatter.11
  753.9 39.0 reduce-scatter.15
  796.1 53.8 all-reduce.23
  853.5 40.5 reduce-scatter.9
  896.9 87.4 all-reduce.21
  987.2 44.0 reduce-scatter.7
where the time goes:
time: 1060 us; the launch traced here: 1050 us
  waiting for transfers between devices  478 us (45%)
  matrix products  216 us (20%)
  blocking collectives  185 us (17%)
  other arithmetic  86.1 us (8%)
  local copies, waits for them, and re-layouts  50.1 us (5%)
  between operations  25 us (2%)
    psum x3, waiting for transfers between devices, branch_total(): return lax.psum(partial_sum, 'mp')  188 us
    psum x3, waiting for transfers between devices, input_total(): return lax.psum(partial_sum, 'mp')  158 us
    dot_general x30, matrix products, matmul(): jnp.dot(left_side, right_side, precision=highest, preferred_element_type=...  107 us
    unnamed x18, waiting for transfers between devices  48.8 us
    unnamed x2, blocking collectives  45.5 us
    psum x1, blocking collectives, shards(): update_square = lax.psum(part_squares(updates, model_count), ('dp', 'mp'))  43.3 us
    psum x1, blocking collectives, shards(): lax.psum((jnp.sum(part_squares(grad_shards, model_count)), part_squares(w...  43.2 us
    all_gather x1, blocking collectives, shards(): lax.all_gather(norm_vectors, 'dp', axis=1, tiled=True)  38.2 us
  transfers between devices with their start and end apart: 18, of which 12 were waited for; matrix products, arithmetic and copies ran while one was open for 24% of the time, Pallas kernels for 0%

commit v1 on v0

v1 whole, which is shorter than its diff:
```python
import functools

import jax
import jax.numpy as jnp
from jax import lax
from jax.experimental import pallas as pl
from jax.experimental.pallas import tpu as pltpu
from jax.sharding import PartitionSpec as P

HD = 64
STEP_NUM = 6

norm_eps = 1e-05
adam_eps = 1e-06
first_decay = 0.5
second_decay = 0.5
matrix_decay = 0.01
peak_rate = 0.6
warm_steps = 8.0
clip_norm = 1.0

bf16 = jnp.bfloat16
f32 = jnp.float32
neg_large = -1e30
q_rows = 128
key_rows = 256
pair_lanes = 128


def split_two(values):
    high = values.astype(bf16)
    return high, (values - high.astype(f32)).astype(bf16)


def dot_nn(left_side, right_side):
    return lax.dot_general(left_side, right_side, (((1,), (0,)), ((), ())), preferred_element_type=f32)


def dot_nt(left_side, right_side):
    return lax.dot_general(left_side, right_side, (((1,), (1,)), ((), ())), preferred_element_type=f32)


def dot_tn(left_side, right_side):
    return lax.dot_general(left_side, right_side, (((0,), (0,)), ((), ())), preferred_element_type=f32)


def three(dot, left_pair, right_pair):
    return (
        dot(left_pair[0], right_pair[0])
        + dot(left_pair[1], right_pair[0])
        + dot(left_pair[0], right_pair[1])
    )


def stack_heads(tile, low_half):
    return jnp.concatenate([jnp.where(low_half, tile, 0.0), jnp.where(low_half, 0.0, tile)], axis=0)


def merge_heads(stacked, low_half):
    return jnp.where(low_half, stacked[:q_rows], stacked[q_rows:])


def split_rows(source_ref, high_ref, low_ref):
    rows = source_ref.shape[0]

    def one(step, carry):
        at = pl.ds(pl.multiple_of(step * q_rows, q_rows), q_rows)
        high, low = split_two(source_ref[at, :])
        high_ref[at, :] = high
        low_ref[at, :] = low
        return carry

    lax.fori_loop(0, rows // q_rows, one, 0)
    if high_ref.shape[0] > rows:
        pad = jnp.zeros((high_ref.shape[0] - rows, high_ref.shape[1]), bf16)
        high_ref[rows:, :] = pad
        low_ref[rows:, :] = pad


def attend_kernel(
    unroll, scale, block_low, block_count,
    q_ref, k_ref, v_ref, low_ref, high_ref,
    o_ref, total_ref,
    kh_ref, kl_ref, vh_ref, vl_ref,
):
    rows, width = q_ref.shape
    split_rows(k_ref, kh_ref, kl_ref)
    split_rows(v_ref, vh_ref, vl_ref)
    groups = width // pair_lanes // unroll
    lanes = lax.broadcasted_iota(jnp.int32, (q_rows, pair_lanes), 1)
    low_half = lanes < pair_lanes // 2
    key_iota = lax.broadcasted_iota(jnp.int32, (2 * q_rows, key_rows), 1)

    def block(index, carry):
        at = pl.ds(pl.multiple_of(index * q_rows, q_rows), q_rows)
        first = low_ref[at, :]
        last = high_ref[at, :]
        first = jnp.concatenate([first, first], axis=0)
        last = jnp.concatenate([last, last], axis=0)
        total_tile = jnp.zeros((q_rows, pair_lanes), f32)
        for group in range(groups):
            columns = [
                pl.ds((group * unroll + u) * pair_lanes, pair_lanes) for u in range(unroll)
            ]
            queries = [
                split_two(stack_heads(q_ref[at, c] * scale, low_half)) for c in columns
            ]

            def chunk(step, state):
                start = pl.multiple_of(block_low[index] + step * key_rows, 16)
                here = pl.ds(start, key_rows)
                places = key_iota + start
                allowed = jnp.logical_and(places >= first, places < last)
                out = []
                for u in range(unroll):
                    top, total, held = state[u]
                    scores = three(
                        dot_nt, queries[u], (kh_ref[here, columns[u]], kl_ref[here, columns[u]])
                    )
                    scores = jnp.where(allowed, scores, neg_large)
                    new_top = jnp.maximum(top, jnp.max(scores, axis=1, keepdims=True))
                    weights = jnp.exp(scores - new_top)
                    shrink = jnp.exp(top - new_top)
                    total = total * shrink + jnp.sum(weights, axis=1, keepdims=True)
                    held = held * shrink + three(
                        dot_nn, split_two(weights), (vh_ref[here, columns[u]], vl_ref[here, columns[u]])
                    )
                    out.append((new_top, total, held))
                return tuple(out)

            start_state = tuple(
                (
                    jnp.full((2 * q_rows, 1), neg_large, f32),
                    jnp.zeros((2 * q_rows, 1), f32),
                    jnp.zeros((2 * q_rows, pair_lanes), f32),
                )
                for _ in range(unroll)
            )
            state = lax.fori_loop(0, block_count[index], chunk, start_state)
            for u in range(unroll):
                top, total, held = state[u]
                pair = group * unroll + u
                o_ref[at, columns[u]] = merge_heads(held / total, low_half)
                logs = top + jnp.log(total)
                total_tile = jnp.where(lanes == 2 * pair, logs[:q_rows], total_tile)
                total_tile = jnp.where(lanes == 2 * pair + 1, logs[q_rows:], total_tile)
        total_ref[at, :] = total_tile
        return carry

    lax.fori_loop(0, rows // q_rows, block, 0)


def attend_back_kernel(
    unroll, scale, block_low, block_count,
    q_ref, k_ref, v_ref, o_ref, g_ref, total_ref, low_ref, high_ref,
    dq_ref, dk_ref, dv_ref,
    kh_ref, kl_ref, vh_ref, vl_ref, dk_sum, dv_sum,
):
    rows, width = q_ref.shape
    split_rows(k_ref, kh_ref, kl_ref)
    split_rows(v_ref, vh_ref, vl_ref)
    dk_sum[...] = jnp.zeros_like(dk_sum)
    dv_sum[...] = jnp.zeros_like(dv_sum)
    groups = width // pair_lanes // unroll
    lanes = lax.broadcasted_iota(jnp.int32, (q_rows, pair_lanes), 1)
    low_half = lanes < pair_lanes // 2
    key_iota = lax.broadcasted_iota(jnp.int32, (2 * q_rows, key_rows), 1)

    def block(index, carry):
        at = pl.ds(pl.multiple_of(index * q_rows, q_rows), q_rows)
        first = low_ref[at, :]
        last = high_ref[at, :]
        first = jnp.concatenate([first, first], axis=0)
        last = jnp.concatenate([last, last], axis=0)
        total_tile = total_ref[at, :]
        for group in range(groups):
            columns = [
                pl.ds((group * unroll + u) * pair_lanes, pair_lanes) for u in range(unroll)
            ]
            queries, grads, logs, dots = [], [], [], []
            for u in range(unroll):
                pair = group * unroll + u
                queries.append(split_two(stack_heads(q_ref[at, columns[u]] * scale, low_half)))
                grad = stack_heads(g_ref[at, columns[u]], low_half)
                grads.append(split_two(grad))
                out = o_ref[at, columns[u]]
                dots.append(
                    jnp.sum(grad * jnp.concatenate([out, out], axis=0), axis=1, keepdims=True)
                )
                logs.append(
                    jnp.concatenate(
                        [
                            jnp.sum(jnp.where(lanes == 2 * pair, total_tile, 0.0), axis=1, keepdims=True),
                            jnp.sum(jnp.where(lanes == 2 * pair + 1, total_tile, 0.0), axis=1, keepdims=True),
                        ],
                        axis=0,
                    )
                )

            def chunk(step, state):
                start = pl.multiple_of(block_low[index] + step * key_rows, 16)
                here = pl.ds(start, key_rows)
                places = key_iota + start
                allowed = jnp.logical_and(places >= first, places < last)
                out = []
                for u in range(unroll):
                    keys = (kh_ref[here, columns[u]], kl_ref[here, columns[u]])
                    values = (vh_ref[here, columns[u]], vl_ref[here, columns[u]])
                    scores = three(dot_nt, queries[u], keys)
                    weights = jnp.where(allowed, jnp.exp(scores - logs[u]), 0.0)
                    grad_weights = three(dot_nt, grads[u], values)
                    grad_scores = split_two(weights * (grad_weights - dots[u]))
                    out.append(state[u] + three(dot_nn, grad_scores, keys))
                    dk_sum[here, columns[u]] += three(dot_tn, grad_scores, queries[u])
                    dv_sum[here, columns[u]] += three(dot_tn, split_two(weights), grads[u])
                return tuple(out)

            state = lax.fori_loop(
                0,
                block_count[index],
                chunk,
                tuple(jnp.zeros((2 * q_rows, pair_lanes), f32) for _ in range(unroll)),
            )
            for u in range(unroll):
                dq_ref[at, columns[u]] = merge_heads(state[u], low_half) * scale
        return carry

    lax.fori_loop(0, rows // q_rows, block, 0)
    dk_ref[...] = dk_sum[:rows, :]
    dv_ref[...] = dv_sum[:rows, :]


VM = functools.partial(pl.BlockSpec, memory_space=pltpu.VMEM)
SM = functools.partial(pl.BlockSpec, memory_space=pltpu.SMEM)


def attend(queries, keys_in, values_in, ranges, head_size, unroll=4):
    block_low, block_count, low, high = ranges
    rows, width = queries.shape
    pad_rows = keys_in.shape[0] + key_rows
    return pl.pallas_call(
        functools.partial(attend_kernel, unroll, head_size ** -0.5),
        out_shape=(
            jax.ShapeDtypeStruct((rows, width), f32),
            jax.ShapeDtypeStruct((rows, pair_lanes), f32),
        ),
        in_specs=[SM(), SM()] + [VM()] * 5,
        out_specs=(VM(), VM()),
        scratch_shapes=[pltpu.VMEM((pad_rows, width), bf16)] * 4,
        compiler_params=pltpu.CompilerParams(vmem_limit_bytes=48 << 20),
        cost_estimate=pl.CostEstimate(flops=12 * rows * key_rows * width, bytes_accessed=16 * rows * width, transcendentals=rows * key_rows * 8),
        name="attend",
    )(block_low, block_count, queries, keys_in, values_in, low, high)


def attend_back(queries, keys_in, values_in, outputs, totals, grad_out, ranges, head_size, unroll=4):
    block_low, block_count, low, high = ranges
    rows, width = queries.shape
    pad_rows = keys_in.shape[0] + key_rows
    return pl.pallas_call(
        functools.partial(attend_back_kernel, unroll, head_size ** -0.5),
        out_shape=tuple(jax.ShapeDtypeStruct((rows, width), f32) for _ in range(3)),
        in_specs=[SM(), SM()] + [VM()] * 8,
        out_specs=(VM(), VM(), VM()),
        scratch_shapes=[pltpu.VMEM((pad_rows, width), bf16)] * 4
        + [pltpu.VMEM((pad_rows, width), f32)] * 2,
        compiler_params=pltpu.CompilerParams(vmem_limit_bytes=56 << 20),
        cost_estimate=pl.CostEstimate(flops=30 * rows * key_rows * width, bytes_accessed=32 * rows * width, transcendentals=rows * key_rows * 8),
        name="attend_back",
    )(block_low, block_count, queries, keys_in, values_in, outputs, grad_out, totals, low, high)


def key_ranges(query_lengths, key_lengths, rows):
    query_ends = jnp.cumsum(query_lengths)
    query_starts = query_ends - query_lengths
    places = jnp.arange(rows, dtype=jnp.int32)
    low = jnp.sum(jnp.where(query_ends[None, :] <= places[:, None], key_lengths[None, :], 0), axis=1)
    high = jnp.sum(jnp.where(query_starts[None, :] <= places[:, None], key_lengths[None, :], 0), axis=1)
    block_low = low[::q_rows] // 16 * 16
    block_high = high[q_rows - 1 :: q_rows]
    block_count = (block_high - block_low + key_rows - 1) // key_rows
    return block_low, block_count, low[:, None], high[:, None]


def matmul(left_side, right_side):
    return jnp.dot(left_side, right_side, precision=lax.Precision.HIGH, preferred_element_type=f32)


def layer_norm(values, gain_row, shift_row):
    centre_mean = jnp.mean(values, axis=-1, keepdims=True)
    centred = values - centre_mean
    variance = jnp.mean(centred * centred, axis=-1, keepdims=True)
    return centred * lax.rsqrt(variance + norm_eps) * gain_row + shift_row


def apply_gelu(values):
    return (
        0.5
        * values
        * (1.0 + jnp.tanh(0.7978845608028654 * (values + 0.044715 * values * values * values)))
    )


def flip(value, axis, distance):
    pairs = [(i, i ^ distance) for i in range(lax.axis_size(axis))]
    return lax.ppermute(value, axis, pairs)


def tree_total(pieces):
    while len(pieces) > 1:
        pieces = [pieces[i] + pieces[i + 1] for i in range(0, len(pieces), 2)]
    return pieces[0]


def small_total(value):
    value = value + flip(value, "dp", 1)
    others = lax.axis_size("dp") // 2
    value = tree_total([value] + [flip(value, "dp", 2 * r) for r in range(1, others)])
    models = lax.axis_size("mp")
    return tree_total([value] + [flip(value, "mp", r) for r in range(1, models)])


def line_gather(own):
    count = lax.axis_size("mp")
    me = lax.axis_index("mp")
    left, right = [own], [own]
    for step in range(1, count):
        left.append(lax.ppermute(left[-1], "mp", [(i, i + 1) for i in range(step - 1, count - 1)]))
        right.append(lax.ppermute(right[-1], "mp", [(i, i - 1) for i in range(count - step, 0, -1)]))
    found = []
    for place in range(count):
        value = None
        for here in range(count):
            piece = left[here - place] if here >= place else right[place - here]
            value = piece if value is None else jnp.where(me == here, piece, value)
        found.append(value)
    return found


def cube_gather(own):
    count = lax.axis_size("dp")
    pieces = {0: own}
    step = 2
    while step < count:
        for at in list(pieces):
            pieces[at ^ step] = flip(pieces[at], "dp", step)
        step *= 2
    for at in list(pieces):
        pieces[at ^ 1] = flip(pieces[at], "dp", 1)
    return [pieces[r] for r in range(count)]


def place_kernel(parts, rows, columns, index_ref, *refs):
    pieces, (full_ref, rest_ref) = refs[:-2], refs[-2:]
    me = index_ref[0]
    for r, piece in enumerate(pieces):
        whose = me ^ r
        at = pl.ds(pl.multiple_of(whose * rows, rows), rows)
        for model in range(piece.shape[0]):
            for part in range(parts):
                full_ref[part, at, model * columns : (model + 1) * columns] = piece[
                    model, part * rows : (part + 1) * rows, :
                ]
            rest_ref[pl.ds(whose, 1), model] = piece[model, parts * rows :, :][None]


def place(pieces, me, parts, rows, columns):
    models, extra = pieces[0].shape[0], pieces[0].shape[1] - parts * rows
    count = len(pieces)
    return pl.pallas_call(
        functools.partial(place_kernel, parts, rows, columns),
        out_shape=(
            jax.ShapeDtypeStruct((parts, rows * count, columns * models), f32),
            jax.ShapeDtypeStruct((count, models, extra, columns), f32),
        ),
        in_specs=[SM()] + [VM()] * count,
        out_specs=(VM(), VM()),
        compiler_params=pltpu.CompilerParams(vmem_limit_bytes=40 << 20),
        name="place",
    )(me[None], *pieces)


def gather_matrices(own, me, parts, rows, columns):
    return place(cube_gather(jnp.stack(line_gather(own))), me, parts, rows, columns)


def pack_kernel(cap, starts_ref, source_ref, packed_ref, padded_ref):
    rows = source_ref.shape[0]
    padded_ref[:rows, :] = source_ref[...]
    padded_ref[rows:, :] = jnp.zeros((padded_ref.shape[0] - rows, source_ref.shape[1]), f32)

    def one(target, carry):
        packed_ref[pl.ds(target, 1)] = padded_ref[pl.ds(starts_ref[target], cap), :][None]
        return carry

    lax.fori_loop(0, packed_ref.shape[0], one, 0)


def pack_rows(source, starts, cap):
    rows, width = source.shape
    return pl.pallas_call(
        functools.partial(pack_kernel, cap),
        out_shape=jax.ShapeDtypeStruct((starts.shape[0], cap, width), f32),
        in_specs=[SM(), VM()],
        out_specs=VM(),
        scratch_shapes=[pltpu.VMEM((rows + cap, width), f32)],
        name="pack_rows",
    )(starts, source)


def unpack_kernel(slots_ref, arrived_ref, out_ref):
    def one(step, carry):
        for k in range(8):
            row = step * 8 + k
            out_ref[pl.ds(row, 1), :] = arrived_ref[pl.ds(slots_ref[row], 1), :]
        return carry

    lax.fori_loop(0, out_ref.shape[0] // 8, one, 0)


def unpack_rows(arrived, slots):
    return pl.pallas_call(
        unpack_kernel,
        out_shape=jax.ShapeDtypeStruct((slots.shape[0], arrived.shape[1]), f32),
        in_specs=[SM(), VM()],
        out_specs=VM(),
        name="unpack_rows",
    )(slots, arrived)


def place_back_kernel(slots_ref, grads_ref, out_ref):
    out_ref[...] = jnp.zeros_like(out_ref)

    def one(step, carry):
        for k in range(8):
            row = step * 8 + k
            out_ref[pl.ds(slots_ref[row], 1), :] = grads_ref[pl.ds(row, 1), :]
        return carry

    lax.fori_loop(0, grads_ref.shape[0] // 8, one, 0)


def place_back(grads_in, slots, total):
    return pl.pallas_call(
        place_back_kernel,
        out_shape=jax.ShapeDtypeStruct((total, grads_in.shape[1]), f32),
        in_specs=[SM(), VM()],
        out_specs=VM(),
        name="place_back",
    )(slots, grads_in)


def return_kernel(starts_ref, returned_ref, out_ref, padded_ref):
    cap = returned_ref.shape[1]

    def one(target, carry):
        padded_ref[pl.ds(starts_ref[target], cap), :] = returned_ref[pl.ds(target, 1)][0]
        return carry

    lax.fori_loop(0, returned_ref.shape[0], one, 0)
    out_ref[...] = padded_ref[: out_ref.shape[0], :]


def return_rows(returned, starts, rows):
    _, cap, width = returned.shape
    return pl.pallas_call(
        return_kernel,
        out_shape=jax.ShapeDtypeStruct((rows, width), f32),
        in_specs=[SM(), VM()],
        out_specs=VM(),
        scratch_shapes=[pltpu.VMEM((rows + cap, width), f32)],
        name="return_rows",
    )(starts, returned)


def cube_scatter(value):
    count = value.shape[0]
    others = count // 2
    me = lax.axis_index("dp")
    odd = me % 2 == 1
    view = value.reshape((others, 2) + value.shape[1:])
    send = jnp.where(odd, view[:, 0], view[:, 1])
    keep = jnp.where(odd, view[:, 1], view[:, 0])
    both = keep + flip(send, "dp", 1)
    block = lambda r: lax.dynamic_index_in_dim(both, (me // 2) ^ r, 0, keepdims=False)
    return tree_total([block(0)] + [flip(block(r), "dp", 2 * r) for r in range(1, others)])


def part_squares(arrays, divisor):
    return jnp.concatenate(
        [
            jnp.sum(arrays[0] * arrays[0], axis=(1, 2)),
            jnp.sum(arrays[1] * arrays[1], axis=(1, 2)),
            jnp.sum(arrays[2] * arrays[2])[None],
            jnp.sum(arrays[3] * arrays[3])[None],
            jnp.sum(arrays[4] * arrays[4], axis=1) / divisor,
            jnp.sum(arrays[5] * arrays[5])[None],
        ]
    )


def spread_parts(per_part):
    return (
        per_part[0:6][:, None, None],
        per_part[6:8][:, None, None],
        per_part[8],
        per_part[9],
        per_part[10:17][:, None],
        per_part[17],
    )


def shards(
    layer_input,
    encoder_memory,
    output_grad,
    target_lengths,
    memory_lengths,
    source_slots,
    pair_counts,
    attend_input,
    attend_output,
    expand_weight,
    reduce_weight,
    norm_vectors,
    expand_bias,
    attend_input_first,
    attend_input_second,
    attend_output_first,
    attend_output_second,
    expand_weight_first,
    expand_weight_second,
    reduce_weight_first,
    reduce_weight_second,
    norm_vectors_first,
    norm_vectors_second,
    expand_bias_first,
    expand_bias_second,
):
    data_count = lax.axis_size("dp")
    model_count = lax.axis_size("mp")
    me = lax.axis_index("dp")
    model = lax.axis_index("mp")
    tok_rows, width = layer_input.shape
    rows, columns = attend_input.shape[1:]
    units = expand_weight.shape[1]
    weights = (attend_input, attend_output, expand_weight, reduce_weight, norm_vectors, expand_bias)

    bias_rows = expand_bias.shape[0]
    vectors = jnp.concatenate(
        [
            jnp.pad(norm_vectors, ((0, 0), (0, columns - rows))),
            jnp.pad(expand_bias[None], ((0, 0), (0, columns - bias_rows))),
        ],
        axis=0,
    )
    own_self = jnp.concatenate(
        [attend_input[:3].reshape(3 * rows, columns), attend_output[0].T, vectors], axis=0
    )
    own_cross = jnp.concatenate(
        [attend_input[3:].reshape(3 * rows, columns), attend_output[1].T, vectors], axis=0
    )
    own_wide = jnp.concatenate([expand_weight, reduce_weight.T], axis=0)
    all_wide = lax.all_gather(own_wide, ("dp", "mp"))
    self_full, all_vectors = gather_matrices(own_self, me, 4, rows, columns)
    cross_full, _ = gather_matrices(own_cross, me, 4, rows, columns)
    all_wide = all_wide.reshape(data_count, model_count, 2, rows, units)
    all_wide = all_wide.transpose(2, 0, 3, 1, 4).reshape(2, rows * data_count, units * model_count)
    expand_full, reduce_turned = all_wide[0], all_wide[1]
    full_vectors = all_vectors[:, 0, :7, :rows].transpose(1, 0, 2).reshape(7, width)
    full_bias = all_vectors[:, :, 7, :bias_rows].transpose(1, 0, 2).reshape(units * model_count)

    extra_slots = tok_rows // 16
    slot_cap = (tok_rows - data_count // 4 * extra_slots) // data_count + extra_slots
    my_counts = lax.dynamic_index_in_dim(pair_counts, me, 0, keepdims=False)
    my_starts = jnp.cumsum(my_counts) - my_counts
    arrived = lax.all_to_all(
        pack_rows(encoder_memory, my_starts, slot_cap), "dp", split_axis=0, concat_axis=0, tiled=True
    )
    memory_own = unpack_rows(arrived.reshape(data_count * slot_cap, columns), source_slots)
    memory_target = jnp.concatenate(line_gather(memory_own), axis=1)

    self_ranges = key_ranges(target_lengths[0], target_lengths[0], tok_rows)
    cross_ranges = key_ranges(target_lengths[0], memory_lengths[0], tok_rows)

    self_query = matmul(layer_input, self_full[0])
    self_key = matmul(layer_input, self_full[1])
    self_value = matmul(layer_input, self_full[2])
    self_out, self_totals = attend(self_query, self_key, self_value, self_ranges, HD)
    self_mix = matmul(self_out, self_full[3].T)
    first_norm, first_back = jax.vjp(layer_norm, layer_input + self_mix, full_vectors[0], full_vectors[3])
    cross_query = matmul(first_norm, cross_full[0])
    cross_key = matmul(memory_target, cross_full[1])
    cross_value = matmul(memory_target, cross_full[2])
    cross_out, cross_totals = attend(cross_query, cross_key, cross_value, cross_ranges, HD)
    cross_mix = matmul(cross_out, cross_full[3].T)
    second_norm, second_back = jax.vjp(layer_norm, first_norm + cross_mix, full_vectors[1], full_vectors[4])
    expand_pre = matmul(second_norm, expand_full) + full_bias
    expanded, gelu_back = jax.vjp(apply_gelu, expand_pre)
    reduced = matmul(expanded, reduce_turned.T)
    layer_output, third_back = jax.vjp(
        layer_norm, second_norm + reduced + full_vectors[6], full_vectors[2], full_vectors[5]
    )

    def mine(value, size):
        return lax.dynamic_slice_in_dim(value, model * size, size, axis=1)

    def blocks(value):
        return value.reshape(data_count, rows, value.shape[1])

    resid_three_grad, gain_three, shift_three = third_back(output_grad)
    reduce_bias_grad = jnp.sum(resid_three_grad, axis=0)
    (pre_grad,) = gelu_back(matmul(resid_three_grad, reduce_turned))
    second_grad = resid_three_grad + matmul(pre_grad, expand_full.T)
    grad_reduce = matmul(resid_three_grad.T, mine(expanded, units))
    grad_expand = matmul(second_norm.T, mine(pre_grad, units))
    grad_bias = jnp.sum(mine(pre_grad, units), axis=0)
    grad_wide = lax.psum_scatter(
        blocks(jnp.concatenate([grad_expand, grad_reduce], axis=1)), "dp", scatter_dimension=0, tiled=False
    )
    resid_two_grad, gain_two, shift_two = second_back(second_grad)
    cross_out_grad = matmul(resid_two_grad, cross_full[3])
    cross_query_grad, cross_key_grad, cross_value_grad = attend_back(
        cross_query, cross_key, cross_value, cross_out, cross_totals, cross_out_grad, cross_ranges, HD
    )
    memory_columns = lambda matrix: lax.dynamic_slice_in_dim(matrix, model * columns, columns, axis=0)
    first_grad = resid_two_grad + matmul(cross_query_grad, cross_full[0].T)
    memory_grad_own = matmul(cross_key_grad, memory_columns(cross_full[1]).T) + matmul(
        cross_value_grad, memory_columns(cross_full[2]).T
    )
    returned = lax.all_to_all(
        place_back(memory_grad_own, source_slots, data_count * slot_cap).reshape(
            data_count, slot_cap, columns
        ),
        "dp",
        split_axis=0,
        concat_axis=0,
        tiled=True,
    )
    memory_grad = return_rows(returned, my_starts, tok_rows)
    grad_cross = jnp.concatenate(
        [
            matmul(first_norm.T, mine(cross_query_grad, columns)),
            matmul(memory_target.T, mine(cross_key_grad, columns)),
            matmul(memory_target.T, mine(cross_value_grad, columns)),
            matmul(resid_two_grad.T, mine(cross_out, columns)),
        ],
        axis=1,
    )
    grad_cross = lax.psum_scatter(blocks(grad_cross), "dp", scatter_dimension=0, tiled=False)
    resid_one_grad, gain_one, shift_one = first_back(first_grad)
    self_out_grad = matmul(resid_one_grad, self_full[3])
    self_query_grad, self_key_grad, self_value_grad = attend_back(
        self_query, self_key, self_value, self_out, self_totals, self_out_grad, self_ranges, HD
    )
    grad_self = jnp.concatenate(
        [
            matmul(layer_input.T, mine(self_query_grad, columns)),
            matmul(layer_input.T, mine(self_key_grad, columns)),
            matmul(layer_input.T, mine(self_value_grad, columns)),
            matmul(resid_one_grad.T, mine(self_out, columns)),
        ],
        axis=1,
    )
    grad_self = cube_scatter(blocks(grad_self))
    input_grad = (
        resid_one_grad
        + matmul(self_query_grad, self_full[0].T)
        + matmul(self_key_grad, self_full[1].T)
        + matmul(self_value_grad, self_full[2].T)
    )
    grad_vectors = jnp.stack(
        [gain_one, gain_two, gain_three, shift_one, shift_two, shift_three, reduce_bias_grad]
    )
    grad_vectors = jnp.concatenate(
        [
            grad_vectors.reshape(7, data_count, rows).transpose(1, 0, 2),
            jnp.pad(grad_bias.reshape(data_count, 1, bias_rows), ((0, 0), (0, 0), (0, rows - bias_rows))),
        ],
        axis=1,
    )
    grad_vectors = cube_scatter(grad_vectors)

    def third(value, which):
        return value[:, which * columns : (which + 1) * columns]

    grad_shards = (
        jnp.stack([third(grad_self, i) for i in range(3)] + [third(grad_cross, i) for i in range(3)]),
        jnp.stack([third(grad_self, 3).T, third(grad_cross, 3).T]),
        grad_wide[:, :units],
        grad_wide[:, units:].T,
        grad_vectors[:7],
        grad_vectors[7, :bias_rows],
    )
    firsts = (
        attend_input_first,
        attend_output_first,
        expand_weight_first,
        reduce_weight_first,
        norm_vectors_first,
        expand_bias_first,
    )
    seconds = (
        attend_input_second,
        attend_output_second,
        expand_weight_second,
        reduce_weight_second,
        norm_vectors_second,
        expand_bias_second,
    )
    weight_square = small_total(part_squares(weights, model_count))
    total_square = small_total(jnp.sum(part_squares(grad_shards, model_count))[None])[0]
    grad_norm = jnp.sqrt(total_square)
    clip_factor = jnp.minimum(1.0, clip_norm / grad_norm)
    steps_done = jnp.float32(STEP_NUM)
    step_rate = peak_rate * jnp.minimum(steps_done / warm_steps, jnp.sqrt(warm_steps / steps_done))
    first_fix = 1.0 - first_decay**steps_done
    second_fix = 1.0 - second_decay**steps_done
    new_firsts = []
    new_seconds = []
    updates = []
    for number in range(6):
        clipped = grad_shards[number] * clip_factor
        moment_one = first_decay * firsts[number] + (1.0 - first_decay) * clipped
        moment_two = second_decay * seconds[number] + (1.0 - second_decay) * clipped * clipped
        decay_rate = matrix_decay if number < 4 else 0.0
        updates.append(
            moment_one / first_fix / (jnp.sqrt(moment_two / second_fix) + adam_eps)
            + decay_rate * weights[number]
        )
        new_firsts.append(moment_one)
        new_seconds.append(moment_two)
    update_square = small_total(part_squares(updates, model_count))
    ratios = spread_parts(jnp.sqrt(weight_square) / jnp.sqrt(update_square))
    new_weights = [
        weights[number] - step_rate * ratios[number] * updates[number] for number in range(6)
    ]
    matrix_norms = jnp.stack([jnp.sqrt(weight_square[:10]), jnp.sqrt(update_square[:10])])
    return (
        layer_output,
        input_grad,
        memory_grad,
        grad_norm[None],
        *new_weights,
        *[value.astype(bf16) for value in new_weights[:4]],
        new_firsts[0],
        new_seconds[0],
        new_firsts[1],
        new_seconds[1],
        new_firsts[2],
        new_seconds[2],
        new_firsts[3],
        new_seconds[3],
        new_firsts[4],
        new_seconds[4],
        new_firsts[5],
        new_seconds[5],
        matrix_norms,
    )


def solution(mesh):
    in_specs = (
        P("dp", None),
        P("dp", "mp"),
        P("dp", None),
        P("dp", None),
        P("dp", None),
        P("dp"),
        P(),
        P(None, "dp", "mp"),
        P(None, "mp", "dp"),
        P("dp", "mp"),
        P("mp", "dp"),
        P(None, "dp"),
        P(("mp", "dp")),
        P(None, "dp", "mp"),
        P(None, "dp", "mp"),
        P(None, "mp", "dp"),
        P(None, "mp", "dp"),
        P("dp", "mp"),
        P("dp", "mp"),
        P("mp", "dp"),
        P("mp", "dp"),
        P(None, "dp"),
        P(None, "dp"),
        P(("mp", "dp")),
        P(("mp", "dp")),
    )
    out_specs = (
        P("dp", None),
        P("dp", None),
        P("dp", "mp"),
        P(),
        P(None, "dp", "mp"),
        P(None, "mp", "dp"),
        P("dp", "mp"),
        P("mp", "dp"),
        P(None, "dp"),
        P(("mp", "dp")),
        P(None, "dp", "mp"),
        P(None, "mp", "dp"),
        P("dp", "mp"),
        P("mp", "dp"),
        P(None, "dp", "mp"),
        P(None, "dp", "mp"),
        P(None, "mp", "dp"),
        P(None, "mp", "dp"),
        P("dp", "mp"),
        P("dp", "mp"),
        P("mp", "dp"),
        P("mp", "dp"),
        P(None, "dp"),
        P(None, "dp"),
        P(("mp", "dp")),
        P(("mp", "dp")),
        P(),
    )
    return jax.shard_map(shards, mesh=mesh, in_specs=in_specs, out_specs=out_specs, check_vma=False)
```

time: 1060 us -> 566 us (0.53)
  waiting for transfers between devices: 478 us -> 69.8 us
  blocking collectives: 185 us -> 0 us
  Pallas kernels: 0 us -> 140 us
  matrix products: 216 us -> 127 us
  starting transfers between devices: 9.23 us -> 97.4 us
  other arithmetic: 86.1 us -> 35.2 us
  local copies, waits for them, and re-layouts: 50.1 us -> 62.5 us
    psum x6 -> x0, waiting for transfers between devices: 346 us -> none  [the longest x3 188 us: branch_total(): return lax.psum(partial_sum, 'mp')]
    pallas_call x0 -> x10, Pallas kernels: none -> 140 us  [the longest x2 69.6 us: attend_back(): pl.pallas_call(functools.partial(attend_back_kernel, unroll, head_size **...]
    dot_general x54 -> x30, matrix products: 216 us -> 127 us  [matmul(): jnp.dot(left_side, right_side, precision=lax.Precision.HIGH, preferred_el...]
    ppermute x0 -> x61, starting transfers between devices: none -> 88.8 us  [the longest x43 55.4 us: flip(): return lax.ppermute(value, axis, pairs)]
    psum x2 -> x0, blocking collectives: 86.5 us -> none  [the longest x1 43.3 us: shards(): update_square = lax.psum(part_squares(updates, model_count), ('dp', 'mp'))]
    ppermute x0 -> x61, waiting for transfers between devices: none -> 55.2 us  [the longest x43 29.6 us: flip(): return lax.ppermute(value, axis, pairs)]
    all_gather x4 -> x1, waiting for transfers between devices: 55 us -> 0.02 us  [shards(): all_wide = lax.all_gather(own_wide, ('dp', 'mp'))]
    all_gather x2 -> x0, blocking collectives: 52.8 us -> none  [the longest x1 38.2 us: shards(): lax.all_gather(norm_vectors, 'dp', axis=1, tiled=True)]
  transfers between devices with their start and end apart: 18 -> 66, of which waited for: 12 -> 18; matrix products, arithmetic and copies ran while one was open for 24% -> 17% of each run, Pallas kernels for 0% -> 19%
where the time goes in v1:
time: 566 us; the launch traced here: 559 us
  Pallas kernels  140 us (25%)
  matrix products  127 us (22%)
  starting transfers between devices  97.4 us (17%)
  waiting for transfers between devices  69.8 us (12%)
  local copies, waits for them, and re-layouts  62.5 us (11%)
  other arithmetic  35.2 us (6%)
  between operations  27.1 us (5%)
    dot_general x30, matrix products, matmul(): jnp.dot(left_side, right_side, precision=lax.Precision.HIGH, preferred_el...  127 us
    pallas_call x2, Pallas kernels, attend_back(): pl.pallas_call(functools.partial(attend_back_kernel, unroll, head_size **...  69.6 us
    ppermute x43, starting transfers between devices, flip(): return lax.ppermute(value, axis, pairs)  55.4 us
    pallas_call x2, Pallas kernels, attend(): pl.pallas_call(functools.partial(attend_kernel, unroll, head_size ** (-0....  54.9 us
    ppermute x43, waiting for transfers between devices, flip(): return lax.ppermute(value, axis, pairs)  29.6 us
    ppermute x9, waiting for transfers between devices, line_gather(): lax.ppermute(right[-1], 'mp', [(i, i - 1) for i in range(count - step, 0,...  25.6 us
    unnamed x165, local copies, waits for them, and re-layouts  23.8 us
    ppermute x9, starting transfers between devices, line_gather(): lax.ppermute(left[-1], 'mp', [(i, i + 1) for i in range(step - 1, count -...  21.9 us
  transfers between devices with their start and end apart: 66, of which 18 were waited for; matrix products, arithmetic and copies ran while one was open for 17% of the time, Pallas kernels for 19%

profile of v1, /device:TPU:0, one launch (start us, length us, event | category | flops | bytes accessed | tf_op | source)
XLA Modules:
  0.0 559.3 jit_solution(17425285729009881513)
XLA Ops:
  12.7 5.6 collective-permute-start
  23.2 8.2 %collective-permute-start.13 = (f32[264,128]{1,0:T(8,128)S(1)}, f32[264,128]{1,0:T(8,128)S(1)}, u32[]{:S(2)}, u32[]{:S(2)}) collective-permute-start(f32[264,128]{1,0:T(8,128)S(1)} %get-tuple-element.231), channel_id=1, source_target_pairs={{0,1},{1,2},{2,3},{4,5},{5,6},{6,7},{8,9},{9,10},{10,11},{12,13},{... | collective-permute-start | bytes 405512 | tf_op jit(solution)/shard_map/ppermute | solution.py:328
  37.5 4.2 all-to-all-start
  47.4 5.4 collective-permute-done.17
  54.7 8.8 %collective-permute-done.18 = f32[264,128]{1,0:T(8,128)S(1)} collective-permute-done((f32[264,128]{1,0:T(8,128)S(1)}, f32[264,128]{1,0:T(8,128)S(1)}, u32[]{:S(2)}, u32[]{:S(2)}) %collective-permute-start.18) | collective-permute-done | bytes 135200 | tf_op jit(solution)/shard_map/ppermute | solution.py:329
  66.7 3.7 collective-permute-done.7.refs_2_
  71.9 3.3 unpack_rows.1
  76.5 2.9 copy.122
  81.6 6.9 %collective-permute-done.22.refs_4_ = f32[4,264,128]{2,1,0:T(8,128)S(1)} collective-permute-done((f32[4,264,128]{2,1,0:T(8,128)S(1)}, f32[4,264,128]{2,1,0:T(8,128)S(1)}, u32[]{:S(2)}, u32[]{:S(2)}) %collective-permute-start.22) | collective-permute-done | bytes 540704 | tf_op jit(solution)/shard_map/ppermute | solution.py:306
  88.5 2.5 collective-permute-start.26
  93.1 2.2 collective-permute-done.29
  96.8 8.8 %collective-permute-done.11.refs_6_ = f32[4,264,128]{2,1,0:T(8,128)} collective-permute-done((f32[4,264,128]{2,1,0:T(8,128)}, f32[4,264,128]{2,1,0:T(8,128)}, u32[]{:S(2)}, u32[]{:S(2)}) %collective-permute-start.11) | collective-permute-done | bytes 540704 | tf_op jit(solution)/shard_map/ppermute | solution.py:306
  110.3 2.9 copy.117
  117.9 2.4 place.2
  123.0 7.5 %collective-permute-done.30 = f32[1024,128]{1,0:T(8,128)} collective-permute-done((f32[1024,128]{1,0:T(8,128)}, f32[1024,128]{1,0:T(8,128)}, u32[]{:S(2)}, u32[]{:S(2)}) %collective-permute-start.30) | collective-permute-done | bytes 524320 | tf_op jit(solution)/shard_map/ppermute | solution.py:329
  133.2 2.7 place.3
  135.9 6.3 %convolution_bitcast_fusion.v_ref = f32[1024,512]{1,0:T(8,128)} fusion(f32[1024,512]{1,0:T(8,128)} %param.25, f32[4,512,512]{2,1,0:T(8,128)S(1)} %copy-done.1), kind=kOutput, calls=%fused_computation.49 | convolution fusion | flops 1610612736 | bytes 5242880 | tf_op jit(solution)/shard_map/dot_general | solution.py:286
  142.2 3.2 convolution_bitcast_fusion.1.k_ref
  147.2 23.5 %attend.2 = (f32[1024,512]{1,0:T(8,128)S(1)}, f32[1024,128]{1,0:T(8,128)S(1)}) custom-call(s32[8]{0:T(128)S(1)} %get-tuple-element.200.block_low, s32[8]{0:T(128)S(1)} %get-tuple-element.199.block_count, f32[1024,512]{1,0:T(8,128)S(1)} %convolution_bitcast_fusion.2.q_ref, f32[1024,512]{1,0:T(8,128)} %convolution_bitcast_fusion.1.k_ref, ...), custom_call_target="tpu_custom_call" | custom-call | flops 1610612736 | bytes 8388608 | tf_op jit(solution)/shard_map/attend/pallas_call | solution.py:241
  170.7 4.4 fusion.154
  179.2 2.6 select_select_fusion.3
  181.8 3.1 fusion.27.v_ref
  185.0 3.1 fusion.29.k_ref
  188.2 31.4 %attend.3 = (f32[1024,512]{1,0:T(8,128)S(1)}, f32[1024,128]{1,0:T(8,128)S(1)}) custom-call(s32[8]{0:T(128)S(1)} %get-tuple-element.202.block_low, s32[8]{0:T(128)S(1)} %get-tuple-element.201.block_count, f32[1024,512]{1,0:T(8,128)S(1)} %fusion.23.q_ref, f32[1024,512]{1,0:T(8,128)} %fusion.29.k_ref, f32[1024,512]{1,0:T(8,128)} %fusion.27.v_ref, ...), custom_call_target="tpu_custom_call" | custom-call | flops 1610612736 | bytes 8388608 | tf_op jit(solution)/shard_map/attend/pallas_call | solution.py:241
  223.3 12.2 %copy.159 = f32[8,4,2,64,512]{4,1,3,0,2:T(4,128)} copy(f32[8,4,2,64,512]{4,3,2,1,0:T(8,128)} %bitcast.256) | data formatting | bytes 16777216 | tf_op jit(solution)/shard_map/reshape | solution.py:567
  235.5 5.2 fusion.150
  242.7 2.4 copy.156
  245.1 11.6 %add_multiply_fusion = (f32[1024,2048]{1,0:T(8,128)S(1)}, f32[1024,2048]{1,0:T(8,128)}) fusion(f32[2048]{0:T(1024)S(1)} %add.367, f32[512,2048]{1,0:T(8,128)S(1)} %bitcast.258, f32[1024,512]{0,1:T(8,128)S(1)} %copy-done.26, f32[512]{0:T(512)S(1)} %add.364, f32[512]{0:T(512)S(1)} %mul.514, f32[1024]{0:T(1024)S(1)} %fusion.125, ...), kind=kOutput, calls=%fused_computation.10 | convolution fusion | flops 6463422464 | bytes 23089152 | tf_op jit(solution)/shard_map/dot_general | solution.py:286
  256.7 6.9 %fusion.156 = (f32[1024]{0:T(1024)S(1)}, f32[1024,512]{0,1:T(8,128)S(1)}) fusion(f32[512]{0:T(512)S(1)} %add.373, f32[1024,2048]{1,0:T(8,128)S(1)} %get-tuple-element.241, f32[512,2048]{1,0:T(8,128)S(1)} %bitcast.260, f32[512]{0:T(512)S(1)} %add.364, f32[512]{0:T(512)S(1)} %mul.514, f32[1024]{0:T(1024)S(1)} %fusion.125, f32[1024,512]{0,1:T(8,128)S(1)} %copy-done.26, ...), kind=kOutput, calls=%fused_computation.342 | convolution fusion | flops 6446119936 | bytes 16795648 | tf_op jit(solution)/shard_map/dot_general | solution.py:286
  265.9 2.2 fusion.147
  270.3 15.5 %fusion.2 = f32[1024,2048]{1,0:T(8,128)S(1)} fusion(f32[1024,2048]{1,0:T(8,128)} %get-tuple-element.242, f32[2048]{0:T(1024)S(1)} %add.367, f32[512,2048]{1,0:T(8,128)S(1)} %bitcast.261, f32[1024,512]{0,1:T(8,128)S(1)} %get-tuple-element.198, f32[1024]{0:T(1024)S(1)} %negate_multiply_fusion.2), kind=kOutput, calls=%fused_computation.6 | convolution fusion | flops 6493306880 | bytes 23080960 | tf_op jit(solution)/shard_map/dot_general | solution.py:286
  285.8 7.3 %multiply_reduce_fusion.1 = (f32[512]{0:T(512)S(1)}, f32[1024]{0:T(1024)S(1)}, f32[512]{0:T(512)S(1)}, f32[1024,512]{0,1:T(8,128)S(1)}) fusion(f32[1024,512]{0,1:T(8,128)S(1)} %copy-done.26, f32[1024]{0:T(1024)S(1)} %fusion.125, f32[1024]{0:T(1024)S(1)} %broadcast_multiply_fusion.1, f32[512]{0:T(512)S(1)} %mul.514, f32[1024,2048]{1,0:T(8,128)S(1)} %fusion.2, ...), kind=kOutput, calls=%fused_computation.17 | convolution fusion | flops 6447691776 | bytes 18896896 | tf_op jit(solution)/shard_map/dot_general | solution.py:286
  293.1 3.1 fusion.7
  297.0 2.4 copy-done.3
  299.3 3.4 fusion.15.g_ref
  302.7 2.2 fusion.13
  304.9 34.7 %attend_back.2 = (f32[1024,512]{1,0:T(8,128)}, f32[1024,512]{1,0:T(8,128)}, f32[1024,512]{1,0:T(8,128)}) custom-call(s32[8]{0:T(128)} %copy-done.15, s32[8]{0:T(128)} %copy-done.14, f32[1024,512]{1,0:T(8,128)} %copy-done.5, f32[1024,512]{1,0:T(8,128)} %fusion.29.k_ref, f32[1024,512]{1,0:T(8,128)} %fusion.27.v_ref, f32[1024,512]{1,0:T(8,128)} %copy-done.7, ...), custom_call_target="tpu_custom_call" | custom-call | flops 4026531840 | bytes 16777216 | tf_op jit(solution)/shard_map/attend_back/pallas_call | solution.py:260
  339.7 6.6 %multiply_reduce_fusion.2 = (f32[512]{0:T(512)S(1)}, f32[1024]{0:T(1024)S(1)}, f32[512]{0:T(512)S(1)}, f32[1024,512]{0,1:T(8,128)}) fusion(f32[1024,512]{0,1:T(8,128)} %copy-done.19, f32[1024]{0:T(1024)S(1)} %fusion.124, f32[1024]{0:T(1024)S(1)} %broadcast_multiply_fusion.2, f32[512]{0:T(512)S(1)} %mul.507, f32[1024,512]{1,0:T(8,128)} %get-tuple-element.46, ...), kind=kOutput, calls=%fused_computation.18 | convolution fusion | flops 1615853568 | bytes 9459712 | tf_op jit(solution)/shard_map/dot_general | solution.py:286
  346.3 3.3 fusion.22
  351.1 3.4 copy.138
  354.9 2.2 fusion.82
  357.1 2.8 fusion.90
  363.3 4.1 fusion.145
  367.7 4.3 collective-permute-start.36
  372.0 3.4 convolution_add_fusion.2.grads_ref
  375.4 3.3 place_back.1
  378.7 4.2 all-to-all-start.1
  383.0 5.1 fusion.11.g_ref
  388.1 34.9 %attend_back.3 = (f32[1024,512]{1,0:T(8,128)}, f32[1024,512]{1,0:T(8,128)}, f32[1024,512]{1,0:T(8,128)}) custom-call(s32[8]{0:T(128)} %copy-done.13, s32[8]{0:T(128)} %copy-done.12, f32[1024,512]{1,0:T(8,128)} %copy-done.4, f32[1024,512]{1,0:T(8,128)} %convolution_bitcast_fusion.1.k_ref, f32[1024,512]{1,0:T(8,128)} %convolution_bitcast_fusion.v_ref, ...), custom_call_target="tpu_custom_call" | custom-call | flops 4026531840 | bytes 16777216 | tf_op jit(solution)/shard_map/attend_back/pallas_call | solution.py:260
  428.5 2.2 fusion.9
  431.1 5.2 fusion.40
  436.3 4.4 fusion.37
  441.9 2.7 collective-permute-start.39
  445.6 6.5 %add_add_fusion.3 = f32[1024,512]{0,1:T(8,128)} fusion(f32[1024,512]{0,1:T(8,128)} %fusion.37, f32[1024,512]{0,1:T(8,128)} %fusion.40, f32[1024,512]{0,1:T(8,128)S(1)} %copy-done.24, f32[1024,512]{1,0:T(8,128)} %get-tuple-element.50, f32[1024]{0:T(1024)S(1)} %negate_multiply_fusion, f32[4,512,512]{2,1,0:T(8,128)} %copy-done), kind=kOutput, calls=%fused_computation.21 | convolution fusion | flops 1612709888 | bytes 11538432 | tf_op jit(solution)/shard_map/dot_general | solution.py:286
  452.1 3.1 copy.145
  458.5 2.6 collective-permute-start.35
  463.3 2.3 return_rows.1
  473.3 14.5 %reduce-scatter.5.cloned.1.call-done = f32[1,64,1024]{2,1,0:T(8,128)} async-done(((f32[8,64,1024]{2,1,0:T(8,128)}), f32[1,64,1024]{2,1,0:T(8,128)}) %reduce-scatter.5.cloned.1.call-update) | async-done | bytes 262160 | tf_op jit(solution)/shard_map/reduce_scatter | solution.py:618
  493.9 2.8 collective-permute-start.43
  496.7 2.7 collective-permute-start.42
  504.9 4.7 collective-permute-start.46
  510.9 2.4 collective-permute-start.44
  532.5 2.4 collective-permute-start.60
  537.0 2.4 collective-permute-start.53
  (399 shorter events, 128.8 us)
Async XLA Ops:
  7.2 216.1 %all-gather.3.cloned.1.call-start = ((), (), s32[]{:S(2)}) async-start(), calls=%async_computation.6 | async-start | bytes 8650752 | tf_op jit(solution)/shard_map/all_gather | solution.py:564
  11.4 8.5 %collective-permute-start.3 = (f32[264,128]{1,0:T(8,128)S(1)}, f32[264,128]{1,0:T(8,128)S(1)}, u32[]{:S(2)}, u32[]{:S(2)}) collective-permute-start(f32[264,128]{1,0:T(8,128)S(1)} %get-tuple-element.232), channel_id=1, source_target_pairs={{3,2},{2,1},{1,0},{7,6},{6,5},{5,4},{11,10},{10,9},{9,8},{15,14},{... | collective-permute-start | bytes 405512 | tf_op jit(solution)/shard_map/ppermute | solution.py:329
  12.7 8.5 %collective-permute-start = (f32[264,128]{1,0:T(8,128)S(1)}, f32[264,128]{1,0:T(8,128)S(1)}, u32[]{:S(2)}, u32[]{:S(2)}) collective-permute-start(f32[264,128]{1,0:T(8,128)S(1)} %get-tuple-element.232), channel_id=1, source_target_pairs={{0,1},{1,2},{2,3},{4,5},{5,6},{6,7},{8,9},{9,10},{10,11},{12,13},{... | collective-permute-start | bytes 405512 | tf_op jit(solution)/shard_map/ppermute | solution.py:328
  19.9 12.3 %collective-permute-start.4 = (f32[264,128]{1,0:T(8,128)S(1)}, f32[264,128]{1,0:T(8,128)S(1)}, u32[]{:S(2)}, u32[]{:S(2)}) collective-permute-start(f32[264,128]{1,0:T(8,128)S(1)} %collective-permute-done.3), channel_id=1, source_target_pairs={{2,1},{1,0},{6,5},{5,4},{10,9},{9,8},{14,13},{13,12},{18,17},{17,1... | collective-permute-start | bytes 405512 | tf_op jit(solution)/shard_map/ppermute | solution.py:329
  21.2 12.3 %collective-permute-start.1 = (f32[264,128]{1,0:T(8,128)S(1)}, f32[264,128]{1,0:T(8,128)S(1)}, u32[]{:S(2)}, u32[]{:S(2)}) collective-permute-start(f32[264,128]{1,0:T(8,128)S(1)} %collective-permute-done), channel_id=1, source_target_pairs={{1,2},{2,3},{5,6},{6,7},{9,10},{10,11},{13,14},{14,15},{17,18},{18... | collective-permute-start | bytes 405512 | tf_op jit(solution)/shard_map/ppermute | solution.py:328
  21.9 19.9 %collective-permute-start.16 = (f32[264,128]{1,0:T(8,128)S(1)}, f32[264,128]{1,0:T(8,128)S(1)}, u32[]{:S(2)}, u32[]{:S(2)}) collective-permute-start(f32[264,128]{1,0:T(8,128)S(1)} %get-tuple-element.231), channel_id=1, source_target_pairs={{3,2},{2,1},{1,0},{7,6},{6,5},{5,4},{11,10},{10,9},{9,8},{15,14},{... | collective-permute-start | bytes 405512 | tf_op jit(solution)/shard_map/ppermute | solution.py:329
  23.2 19.9 %collective-permute-start.13 = (f32[264,128]{1,0:T(8,128)S(1)}, f32[264,128]{1,0:T(8,128)S(1)}, u32[]{:S(2)}, u32[]{:S(2)}) collective-permute-start(f32[264,128]{1,0:T(8,128)S(1)} %get-tuple-element.231), channel_id=1, source_target_pairs={{0,1},{1,2},{2,3},{4,5},{5,6},{6,7},{8,9},{9,10},{10,11},{12,13},{... | collective-permute-start | bytes 405512 | tf_op jit(solution)/shard_map/ppermute | solution.py:328
  32.3 11.5 %collective-permute-start.5 = (f32[264,128]{1,0:T(8,128)S(1)}, f32[264,128]{1,0:T(8,128)S(1)}, u32[]{:S(2)}, u32[]{:S(2)}) collective-permute-start(f32[264,128]{1,0:T(8,128)S(1)} %collective-permute-done.4), channel_id=1, source_target_pairs={{1,0},{5,4},{9,8},{13,12},{17,16},{21,20},{25,24},{29,28}} | collective-permute-start | bytes 405512 | tf_op jit(solution)/shard_map/ppermute | solution.py:329
  33.6 10.2 %collective-permute-start.2 = (f32[264,128]{1,0:T(8,128)S(1)}, f32[264,128]{1,0:T(8,128)S(1)}, u32[]{:S(2)}, u32[]{:S(2)}) collective-permute-start(f32[264,128]{1,0:T(8,128)S(1)} %collective-permute-done.1), channel_id=1, source_target_pairs={{2,3},{6,7},{10,11},{14,15},{18,19},{22,23},{26,27},{30,31}} | collective-permute-start | bytes 405512 | tf_op jit(solution)/shard_map/ppermute | solution.py:328
  37.5 34.4 %all-to-all-start = ((f32[8,176,128]{2,1,0:T(8,128)}), f32[8,176,128]{2,1,0:T(8,128)}, u32[]{:S(2)}, u32[]{:S(2)}) async-start(f32[8,176,128]{2,1,0:T(8,128)} %pack_rows.1), calls=%async_computation | async-start | bytes 1441792 | tf_op jit(solution)/shard_map/all_to_all | solution.py:577
  41.7 426.0 %reduce-scatter.3.cloned.1.call-start = ((), (), s32[]{:S(2)}) async-start(), calls=%async_computation.4 | async-start | bytes 1179648 | tf_op jit(solution)/shard_map/reduce_scatter | solution.py:650
  41.8 11.0 %collective-permute-start.17 = (f32[264,128]{1,0:T(8,128)S(1)}, f32[264,128]{1,0:T(8,128)S(1)}, u32[]{:S(2)}, u32[]{:S(2)}) collective-permute-start(f32[264,128]{1,0:T(8,128)S(1)} %collective-permute-done.16), channel_id=1, source_target_pairs={{2,1},{1,0},{6,5},{5,4},{10,9},{9,8},{14,13},{13,12},{18,17},{17,1... | collective-permute-start | bytes 405512 | tf_op jit(solution)/shard_map/ppermute | solution.py:329
  43.1 11.0 %collective-permute-start.14 = (f32[264,128]{1,0:T(8,128)S(1)}, f32[264,128]{1,0:T(8,128)S(1)}, u32[]{:S(2)}, u32[]{:S(2)}) collective-permute-start(f32[264,128]{1,0:T(8,128)S(1)} %collective-permute-done.13), channel_id=1, source_target_pairs={{1,2},{2,3},{5,6},{6,7},{9,10},{10,11},{13,14},{14,15},{17,18},{18... | collective-permute-start | bytes 405512 | tf_op jit(solution)/shard_map/ppermute | solution.py:328
  44.0 22.7 %collective-permute-start.9 = (f32[4,264,128]{2,1,0:T(8,128)S(1)}, f32[4,264,128]{2,1,0:T(8,128)S(1)}, u32[]{:S(2)}, u32[]{:S(2)}) collective-permute-start(f32[4,264,128]{2,1,0:T(8,128)S(1)} %pad_maximum_fusion.4.refs_0_), channel_id=1, source_target_pairs={{0,16},{4,20},{8,24},{12,28},{16,0},{20,4},{24,8},{28,12},{1,17},{... | collective-permute-start | bytes 1622024 | tf_op jit(solution)/shard_map/ppermute | solution.py:306
  45.9 24.5 %collective-permute-start.7 = (f32[4,264,128]{2,1,0:T(8,128)S(1)}, f32[4,264,128]{2,1,0:T(8,128)}, u32[]{:S(2)}, u32[]{:S(2)}) collective-permute-start(f32[4,264,128]{2,1,0:T(8,128)S(1)} %pad_maximum_fusion.4.refs_0_), channel_id=1, source_target_pairs={{0,8},{4,12},{8,0},{12,4},{16,24},{20,28},{24,16},{28,20},{1,9},{5... | collective-permute-start | bytes 1622024 | tf_op jit(solution)/shard_map/ppermute | solution.py:306
  47.3 27.9 %collective-permute-start.6 = (f32[4,264,128]{2,1,0:T(8,128)S(1)}, f32[4,264,128]{2,1,0:T(8,128)}, u32[]{:S(2)}, u32[]{:S(2)}) collective-permute-start(f32[4,264,128]{2,1,0:T(8,128)S(1)} %pad_maximum_fusion.4.refs_0_), channel_id=1, source_target_pairs={{0,4},{4,0},{8,12},{12,8},{16,20},{20,16},{24,28},{28,24},{1,5},{5... | collective-permute-start | bytes 1622024 | tf_op jit(solution)/shard_map/ppermute | solution.py:306
  52.8 10.8 %collective-permute-start.18 = (f32[264,128]{1,0:T(8,128)S(1)}, f32[264,128]{1,0:T(8,128)S(1)}, u32[]{:S(2)}, u32[]{:S(2)}) collective-permute-start(f32[264,128]{1,0:T(8,128)S(1)} %collective-permute-done.17), channel_id=1, source_target_pairs={{1,0},{5,4},{9,8},{13,12},{17,16},{21,20},{25,24},{29,28}} | collective-permute-start | bytes 405512 | tf_op jit(solution)/shard_map/ppermute | solution.py:329
  54.1 9.5 %collective-permute-start.15 = (f32[264,128]{1,0:T(8,128)S(1)}, f32[264,128]{1,0:T(8,128)S(1)}, u32[]{:S(2)}, u32[]{:S(2)}) collective-permute-start(f32[264,128]{1,0:T(8,128)S(1)} %collective-permute-done.14), channel_id=1, source_target_pairs={{2,3},{6,7},{10,11},{14,15},{18,19},{22,23},{26,27},{30,31}} | collective-permute-start | bytes 405512 | tf_op jit(solution)/shard_map/ppermute | solution.py:328
  63.7 24.7 %collective-permute-start.22 = (f32[4,264,128]{2,1,0:T(8,128)S(1)}, f32[4,264,128]{2,1,0:T(8,128)S(1)}, u32[]{:S(2)}, u32[]{:S(2)}) collective-permute-start(f32[4,264,128]{2,1,0:T(8,128)S(1)} %pad_maximum_fusion.5.refs_0_), channel_id=1, source_target_pairs={{0,16},{4,20},{8,24},{12,28},{16,0},{20,4},{24,8},{28,12},{1,17},{... | collective-permute-start | bytes 1622024 | tf_op jit(solution)/shard_map/ppermute | solution.py:306
  65.9 26.7 %collective-permute-start.20 = (f32[4,264,128]{2,1,0:T(8,128)S(1)}, f32[4,264,128]{2,1,0:T(8,128)S(1)}, u32[]{:S(2)}, u32[]{:S(2)}) collective-permute-start(f32[4,264,128]{2,1,0:T(8,128)S(1)} %pad_maximum_fusion.5.refs_0_), channel_id=1, source_target_pairs={{0,8},{4,12},{8,0},{12,4},{16,24},{20,28},{24,16},{28,20},{1,9},{5... | collective-permute-start | bytes 1622024 | tf_op jit(solution)/shard_map/ppermute | solution.py:306
  66.6 26.0 %collective-permute-start.19 = (f32[4,264,128]{2,1,0:T(8,128)S(1)}, f32[4,264,128]{2,1,0:T(8,128)S(1)}, u32[]{:S(2)}, u32[]{:S(2)}) collective-permute-start(f32[4,264,128]{2,1,0:T(8,128)S(1)} %pad_maximum_fusion.5.refs_0_), channel_id=1, source_target_pairs={{0,4},{4,0},{8,12},{12,8},{16,20},{20,16},{24,28},{28,24},{1,5},{5... | collective-permute-start | bytes 1622024 | tf_op jit(solution)/shard_map/ppermute | solution.py:306
  70.4 35.2 %collective-permute-start.11 = (f32[4,264,128]{2,1,0:T(8,128)}, f32[4,264,128]{2,1,0:T(8,128)}, u32[]{:S(2)}, u32[]{:S(2)}) collective-permute-start(f32[4,264,128]{2,1,0:T(8,128)} %collective-permute-done.7.refs_2_), channel_id=1, source_target_pairs={{0,16},{4,20},{8,24},{12,28},{16,0},{20,4},{24,8},{28,12},{1,17},{... | collective-permute-start | bytes 1622024 | tf_op jit(solution)/shard_map/ppermute | solution.py:306
  75.2 20.1 %collective-permute-start.29 = (f32[1024,128]{1,0:T(8,128)}, f32[1024,128]{1,0:T(8,128)}, u32[]{:S(2)}, u32[]{:S(2)}) collective-permute-start(f32[1024,128]{1,0:T(8,128)} %unpack_rows.1), channel_id=1, source_target_pairs={{3,2},{2,1},{1,0},{7,6},{6,5},{5,4},{11,10},{10,9},{9,8},{15,14},{... | collective-permute-start | bytes 1572872 | tf_op jit(solution)/shard_map/ppermute | solution.py:329
  88.5 24.8 %collective-permute-start.26 = (f32[1024,128]{1,0:T(8,128)}, f32[1024,128]{1,0:T(8,128)}, u32[]{:S(2)}, u32[]{:S(2)}) collective-permute-start(f32[1024,128]{1,0:T(8,128)} %unpack_rows.1), channel_id=1, source_target_pairs={{0,1},{1,2},{2,3},{4,5},{5,6},{6,7},{8,9},{9,10},{10,11},{12,13},{... | collective-permute-start | bytes 1572872 | tf_op jit(solution)/shard_map/ppermute | solution.py:328
  92.6 21.3 %collective-permute-start.8 = (f32[4,264,128]{2,1,0:T(8,128)}, f32[4,264,128]{2,1,0:T(8,128)}, u32[]{:S(2)}, u32[]{:S(2)}) collective-permute-start(f32[4,264,128]{2,1,0:T(8,128)} %collective-permute-done.7.refs_2_), channel_id=1, source_target_pairs={{0,4},{4,0},{8,12},{12,8},{16,20},{20,16},{24,28},{28,24},{1,5},{5... | collective-permute-start | bytes 1622024 | tf_op jit(solution)/shard_map/ppermute | solution.py:306
  92.6 21.2 %collective-permute-start.10 = (f32[4,264,128]{2,1,0:T(8,128)S(1)}, f32[4,264,128]{2,1,0:T(8,128)}, u32[]{:S(2)}, u32[]{:S(2)}) collective-permute-start(f32[4,264,128]{2,1,0:T(8,128)S(1)} %collective-permute-done.9.refs_4_), channel_id=1, source_target_pairs={{0,4},{4,0},{8,12},{12,8},{16,20},{20,16},{24,28},{28,24},{1,5},{5... | collective-permute-start | bytes 1622024 | tf_op jit(solution)/shard_map/ppermute | solution.py:306
  95.3 21.0 %collective-permute-start.24 = (f32[4,264,128]{2,1,0:T(8,128)S(1)}, f32[4,264,128]{2,1,0:T(8,128)}, u32[]{:S(2)}, u32[]{:S(2)}) collective-permute-start(f32[4,264,128]{2,1,0:T(8,128)S(1)} %collective-permute-done.20.refs_2_), channel_id=1, source_target_pairs={{0,16},{4,20},{8,24},{12,28},{16,0},{20,4},{24,8},{28,12},{1,17},{... | collective-permute-start | bytes 1622024 | tf_op jit(solution)/shard_map/ppermute | solution.py:306
  105.6 12.2 %collective-permute-start.12 = (f32[4,264,128]{2,1,0:T(8,128)}, f32[4,264,128]{2,1,0:T(8,128)}, u32[]{:S(2)}, u32[]{:S(2)}) collective-permute-start(f32[4,264,128]{2,1,0:T(8,128)} %collective-permute-done.11.refs_6_), channel_id=1, source_target_pairs={{0,4},{4,0},{8,12},{12,8},{16,20},{20,16},{24,28},{28,24},{1,5},{5... | collective-permute-start | bytes 1622024 | tf_op jit(solution)/shard_map/ppermute | solution.py:306
  113.3 20.0 %collective-permute-start.21 = (f32[4,264,128]{2,1,0:T(8,128)S(1)}, f32[4,264,128]{2,1,0:T(8,128)}, u32[]{:S(2)}, u32[]{:S(2)}) collective-permute-start(f32[4,264,128]{2,1,0:T(8,128)S(1)} %collective-permute-done.20.refs_2_), channel_id=1, source_target_pairs={{0,4},{4,0},{8,12},{12,8},{16,20},{20,16},{24,28},{28,24},{1,5},{5... | collective-permute-start | bytes 1622024 | tf_op jit(solution)/shard_map/ppermute | solution.py:306
  113.9 19.3 %collective-permute-start.23 = (f32[4,264,128]{2,1,0:T(8,128)S(1)}, f32[4,264,128]{2,1,0:T(8,128)}, u32[]{:S(2)}, u32[]{:S(2)}) collective-permute-start(f32[4,264,128]{2,1,0:T(8,128)S(1)} %collective-permute-done.22.refs_4_), channel_id=1, source_target_pairs={{0,4},{4,0},{8,12},{12,8},{16,20},{20,16},{24,28},{28,24},{1,5},{5... | collective-permute-start | bytes 1622024 | tf_op jit(solution)/shard_map/ppermute | solution.py:306
  114.0 16.5 %collective-permute-start.30 = (f32[1024,128]{1,0:T(8,128)}, f32[1024,128]{1,0:T(8,128)}, u32[]{:S(2)}, u32[]{:S(2)}) collective-permute-start(f32[1024,128]{1,0:T(8,128)} %collective-permute-done.29), channel_id=1, source_target_pairs={{2,1},{1,0},{6,5},{5,4},{10,9},{9,8},{14,13},{13,12},{18,17},{17,1... | collective-permute-start | bytes 1572872 | tf_op jit(solution)/shard_map/ppermute | solution.py:329
  116.3 15.4 %collective-permute-start.27 = (f32[1024,128]{1,0:T(8,128)}, f32[1024,128]{1,0:T(8,128)}, u32[]{:S(2)}, u32[]{:S(2)}) collective-permute-start(f32[1024,128]{1,0:T(8,128)} %collective-permute-done.26), channel_id=1, source_target_pairs={{1,2},{2,3},{5,6},{6,7},{9,10},{10,11},{13,14},{14,15},{17,18},{18... | collective-permute-start | bytes 1572872 | tf_op jit(solution)/shard_map/ppermute | solution.py:328
  117.8 15.4 %collective-permute-start.25 = (f32[4,264,128]{2,1,0:T(8,128)}, f32[4,264,128]{2,1,0:T(8,128)}, u32[]{:S(2)}, u32[]{:S(2)}) collective-permute-start(f32[4,264,128]{2,1,0:T(8,128)} %collective-permute-done.24.refs_6_), channel_id=1, source_target_pairs={{0,4},{4,0},{8,12},{12,8},{16,20},{20,16},{24,28},{28,24},{1,5},{5... | collective-permute-start | bytes 1622024 | tf_op jit(solution)/shard_map/ppermute | solution.py:306
  130.4 48.7 %collective-permute-start.31 = (f32[1024,128]{1,0:T(8,128)}, f32[1024,128]{1,0:T(8,128)}, u32[]{:S(2)}, u32[]{:S(2)}) collective-permute-start(f32[1024,128]{1,0:T(8,128)} %collective-permute-done.30), channel_id=1, source_target_pairs={{1,0},{5,4},{9,8},{13,12},{17,16},{21,20},{25,24},{29,28}} | collective-permute-start | bytes 1572872 | tf_op jit(solution)/shard_map/ppermute | solution.py:329
  131.7 47.4 %collective-permute-start.28 = (f32[1024,128]{1,0:T(8,128)}, f32[1024,128]{1,0:T(8,128)}, u32[]{:S(2)}, u32[]{:S(2)}) collective-permute-start(f32[1024,128]{1,0:T(8,128)} %collective-permute-done.27), channel_id=1, source_target_pairs={{2,3},{6,7},{10,11},{14,15},{18,19},{22,23},{26,27},{30,31}} | collective-permute-start | bytes 1572872 | tf_op jit(solution)/shard_map/ppermute | solution.py:328
  367.7 74.2 %collective-permute-start.36 = (f32[4,8,64]{2,0,1:T(4,128)S(1)}, f32[4,8,64]{2,0,1:T(4,128)S(1)}, u32[]{:S(2)}, u32[]{:S(2)}) collective-permute-start(f32[4,8,64]{2,0,1:T(4,128)S(1)} %bitcast.282), channel_id=1, source_target_pairs={{0,4},{4,0},{8,12},{12,8},{16,20},{20,16},{24,28},{28,24},{1,5},{5... | collective-permute-start | bytes 24584 | tf_op jit(solution)/shard_map/ppermute | solution.py:306
  378.7 84.6 %all-to-all-start.1 = ((f32[8,176,128]{2,1,0:T(8,128)}), f32[8,176,128]{2,1,0:T(8,128)}, u32[]{:S(2)}, u32[]{:S(2)}) async-start(f32[8,176,128]{2,1,0:T(8,128)} %bitcast.263), calls=%async_computation.1 | async-start | bytes 1441792 | tf_op jit(solution)/shard_map/all_to_all | solution.py:631
  382.9 104.9 %reduce-scatter.5.cloned.1.call-start = ((), (), s32[]{:S(2)}) async-start(), calls=%async_computation.5 | async-start | bytes 2359296 | tf_op jit(solution)/shard_map/reduce_scatter | solution.py:618
  441.5 15.6 %collective-permute-start.32 = (f32[4,64,512]{2,1,0:T(8,128)}, f32[4,64,512]{2,1,0:T(8,128)}, u32[]{:S(2)}, u32[]{:S(2)}) collective-permute-start(f32[4,64,512]{2,1,0:T(8,128)} %select_bitcast_fusion), channel_id=1, source_target_pairs={{0,4},{4,0},{8,12},{12,8},{16,20},{20,16},{24,28},{28,24},{1,5},{5... | collective-permute-start | bytes 1572872 | tf_op jit(solution)/shard_map/ppermute | solution.py:306
  441.9 15.1 %collective-permute-start.39 = (f32[8,64]{1,0:T(8,128)S(1)}, f32[8,64]{1,0:T(8,128)S(1)}, u32[]{:S(2)}, u32[]{:S(2)}) collective-permute-start(f32[8,64]{1,0:T(8,128)S(1)} %bitcast.287), channel_id=1, source_target_pairs={{0,24},{4,28},{8,16},{12,20},{16,8},{20,12},{24,0},{28,4},{1,25},{... | collective-permute-start | bytes 6152 | tf_op jit(solution)/shard_map/ppermute | solution.py:306
  444.7 12.3 %collective-permute-start.37 = (f32[8,64]{1,0:T(8,128)S(1)}, f32[8,64]{1,0:T(8,128)S(1)}, u32[]{:S(2)}, u32[]{:S(2)}) collective-permute-start(f32[8,64]{1,0:T(8,128)S(1)} %bitcast.286), channel_id=1, source_target_pairs={{0,8},{4,12},{8,0},{12,4},{16,24},{20,28},{24,16},{28,20},{1,9},{5... | collective-permute-start | bytes 6152 | tf_op jit(solution)/shard_map/ppermute | solution.py:306
  445.2 11.8 %collective-permute-start.38 = (f32[8,64]{1,0:T(8,128)S(1)}, f32[8,64]{1,0:T(8,128)S(1)}, u32[]{:S(2)}, u32[]{:S(2)}) collective-permute-start(f32[8,64]{1,0:T(8,128)S(1)} %bitcast.285), channel_id=1, source_target_pairs={{0,16},{4,20},{8,24},{12,28},{16,0},{20,4},{24,8},{28,12},{1,17},{... | collective-permute-start | bytes 6152 | tf_op jit(solution)/shard_map/ppermute | solution.py:306
  458.5 7.1 %collective-permute-start.35 = (f32[64,512]{1,0:T(8,128)S(1)}, f32[64,512]{1,0:T(8,128)S(1)}, u32[]{:S(2)}, u32[]{:S(2)}) collective-permute-start(f32[64,512]{1,0:T(8,128)S(1)} %get-tuple-element.212), channel_id=1, source_target_pairs={{0,24},{4,28},{8,16},{12,20},{16,8},{20,12},{24,0},{28,4},{1,25},{... | collective-permute-start | bytes 393224 | tf_op jit(solution)/shard_map/ppermute | solution.py:306
  461.1 6.1 %collective-permute-start.34 = (f32[64,512]{1,0:T(8,128)S(1)}, f32[64,512]{1,0:T(8,128)S(1)}, u32[]{:S(2)}, u32[]{:S(2)}) collective-permute-start(f32[64,512]{1,0:T(8,128)S(1)} %get-tuple-element.213), channel_id=1, source_target_pairs={{0,16},{4,20},{8,24},{12,28},{16,0},{20,4},{24,8},{28,12},{1,17},{... | collective-permute-start | bytes 393224 | tf_op jit(solution)/shard_map/ppermute | solution.py:306
  462.0 5.5 collective-permute-start.33
  493.9 9.7 %collective-permute-start.43 = (f32[1]{0:T(128)}, f32[1]{0:T(128)}, u32[]{:S(2)}, u32[]{:S(2)}) collective-permute-start(f32[1]{0:T(128)} %add.401), channel_id=1, source_target_pairs={{0,24},{4,28},{8,16},{12,20},{16,8},{20,12},{24,0},{28,4},{1,25},{... | collective-permute-start | bytes 20 | tf_op jit(solution)/shard_map/ppermute | solution.py:306
  496.7 6.9 %collective-permute-start.42 = (f32[1]{0:T(128)}, f32[1]{0:T(128)}, u32[]{:S(2)}, u32[]{:S(2)}) collective-permute-start(f32[1]{0:T(128)} %add.401), channel_id=1, source_target_pairs={{0,16},{4,20},{8,24},{12,28},{16,0},{20,4},{24,8},{28,12},{1,17},{... | collective-permute-start | bytes 20 | tf_op jit(solution)/shard_map/ppermute | solution.py:306
  499.5 3.5 collective-permute-start.41
  504.9 10.1 %collective-permute-start.46 = (f32[1]{0:T(128)}, f32[1]{0:T(128)}, u32[]{:S(2)}, u32[]{:S(2)}) collective-permute-start(f32[1]{0:T(128)} %add.404), channel_id=1, source_target_pairs={{0,3},{1,2},{2,1},{3,0},{4,7},{5,6},{6,5},{7,4},{8,11},{9,10},{10,... | collective-permute-start | bytes 20 | tf_op jit(solution)/shard_map/ppermute | solution.py:306
  509.6 5.4 collective-permute-start.45
  510.9 3.5 collective-permute-start.44
  525.0 4.0 collective-permute-start.47
  525.5 5.6 collective-permute-start.57
  527.0 5.5 collective-permute-start.56
  527.5 4.9 collective-permute-start.55
  529.0 6.6 %collective-permute-start.50 = (f32[18]{0:T(128)S(1)}, f32[18]{0:T(128)S(1)}, u32[]{:S(2)}, u32[]{:S(2)}) collective-permute-start(f32[18]{0:T(128)S(1)} %add.408), channel_id=1, source_target_pairs={{0,24},{4,28},{8,16},{12,20},{16,8},{20,12},{24,0},{28,4},{1,25},{... | collective-permute-start | bytes 224 | tf_op jit(solution)/shard_map/ppermute | solution.py:306
  530.4 6.5 %collective-permute-start.49 = (f32[18]{0:T(128)S(1)}, f32[18]{0:T(128)S(1)}, u32[]{:S(2)}, u32[]{:S(2)}) collective-permute-start(f32[18]{0:T(128)S(1)} %add.408), channel_id=1, source_target_pairs={{0,16},{4,20},{8,24},{12,28},{16,0},{20,4},{24,8},{28,12},{1,17},{... | collective-permute-start | bytes 224 | tf_op jit(solution)/shard_map/ppermute | solution.py:306
  531.0 5.9 %collective-permute-start.48 = (f32[18]{0:T(128)S(1)}, f32[18]{0:T(128)S(1)}, u32[]{:S(2)}, u32[]{:S(2)}) collective-permute-start(f32[18]{0:T(128)S(1)} %add.408), channel_id=1, source_target_pairs={{0,8},{4,12},{8,0},{12,4},{16,24},{20,28},{24,16},{28,20},{1,9},{5... | collective-permute-start | bytes 224 | tf_op jit(solution)/shard_map/ppermute | solution.py:306
  532.5 6.9 %collective-permute-start.60 = (f32[18]{0:T(128)S(1)}, f32[18]{0:T(128)S(1)}, u32[]{:S(2)}, u32[]{:S(2)}) collective-permute-start(f32[18]{0:T(128)S(1)} %add_add_fusion.9), channel_id=1, source_target_pairs={{0,3},{1,2},{2,1},{3,0},{4,7},{5,6},{6,5},{7,4},{8,11},{9,10},{10,... | collective-permute-start | bytes 224 | tf_op jit(solution)/shard_map/ppermute | solution.py:306
  534.9 6.5 %collective-permute-start.59 = (f32[18]{0:T(128)S(1)}, f32[18]{0:T(128)S(1)}, u32[]{:S(2)}, u32[]{:S(2)}) collective-permute-start(f32[18]{0:T(128)S(1)} %add_add_fusion.9), channel_id=1, source_target_pairs={{0,2},{1,3},{2,0},{3,1},{4,6},{5,7},{6,4},{7,5},{8,10},{9,11},{10,... | collective-permute-start | bytes 224 | tf_op jit(solution)/shard_map/ppermute | solution.py:306
  535.5 5.9 %collective-permute-start.58 = (f32[18]{0:T(128)S(1)}, f32[18]{0:T(128)S(1)}, u32[]{:S(2)}, u32[]{:S(2)}) collective-permute-start(f32[18]{0:T(128)S(1)} %add_add_fusion.9), channel_id=1, source_target_pairs={{0,1},{1,0},{2,3},{3,2},{4,5},{5,4},{6,7},{7,6},{8,9},{9,8},{10,11... | collective-permute-start | bytes 224 | tf_op jit(solution)/shard_map/ppermute | solution.py:306
  537.0 5.4 collective-permute-start.53
  539.4 4.4 collective-permute-start.52
  539.4 4.4 collective-permute-start.51
  (76 other events, 1903.5 us)
Sparse Core Ops, SparseCore 0:
  11.0 102.8 all-gather.2
  367.6 42.9 reduce-scatter.2
  442.0 45.7 reduce-scatter.4

commit v2 on v1

v2 whole, which is shorter than its diff:
```python
import functools

import jax
import jax.numpy as jnp
from jax import lax
from jax.experimental import pallas as pl
from jax.experimental.pallas import tpu as pltpu
from jax.sharding import PartitionSpec as P

HD = 64
STEP_NUM = 6

norm_eps = 1e-05
adam_eps = 1e-06
first_decay = 0.5
second_decay = 0.5
matrix_decay = 0.01
peak_rate = 0.6
warm_steps = 8.0
clip_norm = 1.0

bf16 = jnp.bfloat16
f32 = jnp.float32
neg_large = -1e30
q_rows = 128
key_rows = 256
pair_lanes = 128


def split_two(values):
    high = values.astype(bf16)
    return high, (values - high.astype(f32)).astype(bf16)


def dot_nn(left_side, right_side):
    return lax.dot_general(left_side, right_side, (((1,), (0,)), ((), ())), preferred_element_type=f32)


def dot_nt(left_side, right_side):
    return lax.dot_general(left_side, right_side, (((1,), (1,)), ((), ())), preferred_element_type=f32)


def dot_tn(left_side, right_side):
    return lax.dot_general(left_side, right_side, (((0,), (0,)), ((), ())), preferred_element_type=f32)


def three(dot, left_pair, right_pair):
    return (
        dot(left_pair[0], right_pair[0])
        + dot(left_pair[1], right_pair[0])
        + dot(left_pair[0], right_pair[1])
    )


def swap_halves(tile):
    return pltpu.roll(tile, pair_lanes // 2, 1)


def parts_of(tile):
    high = tile.astype(bf16).astype(f32)
    return high, tile - high


def query_packs(tile, low_half):
    high, low = parts_of(tile)
    high_swap, low_swap = swap_halves(high), swap_halves(low)
    zero = jnp.zeros_like(tile)
    first = jnp.concatenate(
        [jnp.where(low_half, high, high_swap), jnp.where(low_half, low, zero)], axis=1
    )
    second = jnp.concatenate(
        [jnp.where(low_half, high_swap, high), jnp.where(low_half, low_swap, zero)], axis=1
    )
    return first.astype(bf16), second.astype(bf16)


def key_packs(tile, low_half):
    high, low = parts_of(tile)
    high_swap, low_swap = swap_halves(high), swap_halves(low)
    zero = jnp.zeros_like(tile)
    first = jnp.concatenate(
        [jnp.where(low_half, high, low_swap), jnp.where(low_half, high, zero)], axis=1
    )
    second = jnp.concatenate(
        [jnp.where(low_half, high_swap, low), jnp.where(low_half, high_swap, zero)], axis=1
    )
    return first.astype(bf16), second.astype(bf16)


def both_parts(tile):
    high, low = split_two(tile)
    return jnp.concatenate([high, low], axis=1)


def stack_heads(tile, low_half):
    return jnp.concatenate([jnp.where(low_half, tile, 0.0), jnp.where(low_half, 0.0, tile)], axis=0)


def merge_heads(stacked, low_half):
    return jnp.where(low_half, stacked[:q_rows], stacked[q_rows:])


def folded(dot, left_pair, right_both):
    wide = dot(left_pair[0], right_both)
    return wide[:, :pair_lanes] + wide[:, pair_lanes:] + dot(left_pair[1], right_both[:, :pair_lanes])


def prepare(source_ref, low_half, pack_ref, both_ref):
    rows, width = source_ref.shape

    def one(step, carry):
        at = pl.ds(pl.multiple_of(step * q_rows, q_rows), q_rows)
        for pair in range(width // pair_lanes):
            tile = source_ref[at, pair * pair_lanes : (pair + 1) * pair_lanes]
            if pack_ref is not None:
                first, second = key_packs(tile, low_half)
                pack_ref[2 * pair, at, :] = first
                pack_ref[2 * pair + 1, at, :] = second
            if both_ref is not None:
                both_ref[pair, at, :] = both_parts(tile)
        return carry

    lax.fori_loop(0, rows // q_rows, one, 0)
    for ref in (pack_ref, both_ref):
        if ref is not None:
            ref[:, rows:, :] = jnp.zeros((ref.shape[0], ref.shape[1] - rows, ref.shape[2]), bf16)


def attend_kernel(
    unroll, scale, block_low, block_count,
    q_ref, k_ref, v_ref, low_ref, high_ref,
    o_ref, total_ref,
    kp_ref, vb_ref,
):
    rows, width = q_ref.shape
    lanes = lax.broadcasted_iota(jnp.int32, (q_rows, pair_lanes), 1)
    low_half = lanes < pair_lanes // 2
    prepare(k_ref, low_half, kp_ref, None)
    prepare(v_ref, low_half, None, vb_ref)
    groups = width // pair_lanes // unroll
    key_iota = lax.broadcasted_iota(jnp.int32, (q_rows, key_rows), 1)

    def block(index, carry):
        at = pl.ds(pl.multiple_of(index * q_rows, q_rows), q_rows)
        first = low_ref[at, :]
        last = high_ref[at, :]
        for group in range(groups):
            pairs = [group * unroll + u for u in range(unroll)]
            queries = [
                query_packs(q_ref[at, p * pair_lanes : (p + 1) * pair_lanes] * scale, low_half)
                for p in pairs
            ]

            def chunk(step, state):
                start = pl.multiple_of(block_low[index] + step * key_rows, 16)
                here = pl.ds(start, key_rows)
                places = key_iota + start
                bias = jnp.where(jnp.logical_and(places >= first, places < last), 0.0, neg_large)
                bias = jnp.concatenate([bias, bias], axis=0)
                out = []
                found = [
                    jnp.concatenate(
                        [dot_nt(queries[u][h], kp_ref[2 * p + h, here, :]) for h in range(2)], axis=0
                    )
                    for u, p in enumerate(pairs)
                ]
                for u, p in enumerate(pairs):
                    scores = bias + found[u]
                    new_top = jnp.max(scores, axis=1, keepdims=True)
                    if state is not None:
                        top, total, held = state[u]
                        new_top = jnp.maximum(top, new_top)
                        shrink = jnp.exp(top - new_top)
                    weights = jnp.exp(scores - new_top)
                    new_total = jnp.sum(weights, axis=1, keepdims=True)
                    new_held = folded(dot_nn, split_two(weights), vb_ref[p, here, :])
                    if state is not None:
                        new_total = total * shrink + new_total
                        new_held = held * shrink + new_held
                    out.append((new_top, new_total, new_held))
                return tuple(out)

            def finish(state):
                tile = total_ref[at, :] if group else jnp.zeros((q_rows, pair_lanes), f32)
                for u, p in enumerate(pairs):
                    top, total, held = state[u]
                    o_ref[at, p * pair_lanes : (p + 1) * pair_lanes] = merge_heads(held / total, low_half)
                    logs = top + jnp.log(total)
                    tile = jnp.where(lanes == 2 * p, logs[:q_rows], tile)
                    tile = jnp.where(lanes == 2 * p + 1, logs[q_rows:], tile)
                total_ref[at, :] = tile

            @pl.when(block_count[index] == 1)
            def _():
                finish(chunk(0, None))

            @pl.when(block_count[index] > 1)
            def _():
                start_state = tuple(
                    (
                        jnp.full((2 * q_rows, 1), neg_large, f32),
                        jnp.zeros((2 * q_rows, 1), f32),
                        jnp.zeros((2 * q_rows, pair_lanes), f32),
                    )
                    for _ in range(unroll)
                )
                finish(lax.fori_loop(0, block_count[index], chunk, start_state))

        return carry

    lax.fori_loop(0, rows // q_rows, block, 0)


def attend_back_blocks(
    unroll, scale, block_low, block_count,
    q_ref, o_ref, g_ref, total_ref, low_ref, high_ref,
    dq_ref, kp_ref, vp_ref, kb_ref, dk_sum, dv_sum,
):
    rows, width = q_ref.shape
    lanes = lax.broadcasted_iota(jnp.int32, (q_rows, pair_lanes), 1)
    low_half = lanes < pair_lanes // 2
    groups = width // pair_lanes // unroll
    key_iota = lax.broadcasted_iota(jnp.int32, (q_rows, key_rows), 1)

    def block(index, carry):
        at = pl.ds(pl.multiple_of(index * q_rows, q_rows), q_rows)
        first = low_ref[at, :]
        last = high_ref[at, :]
        total_tile = total_ref[at, :]
        for group in range(groups):
            pairs = [group * unroll + u for u in range(unroll)]
            queries, query_both, grads, grad_both, logs, dots = [], [], [], [], [], []
            for p in pairs:
                lanes_of = slice(p * pair_lanes, (p + 1) * pair_lanes)
                tile = q_ref[at, lanes_of] * scale
                queries.append(query_packs(tile, low_half))
                query_both.append(both_parts(stack_heads(tile, low_half)))
                tile = g_ref[at, lanes_of]
                grads.append(query_packs(tile, low_half))
                grad_both.append(both_parts(stack_heads(tile, low_half)))
                product = tile * o_ref[at, lanes_of]
                column = lambda mask, value: jnp.sum(jnp.where(mask, value, 0.0), axis=1, keepdims=True)
                dots.append(
                    jnp.concatenate(
                        [column(low_half, product), column(jnp.logical_not(low_half), product)], axis=0
                    )
                )
                logs.append(
                    jnp.concatenate(
                        [column(lanes == 2 * p, total_tile), column(lanes == 2 * p + 1, total_tile)], axis=0
                    )
                )

            def chunk(step, state):
                start = pl.multiple_of(block_low[index] + step * key_rows, 16)
                here = pl.ds(start, key_rows)
                places = key_iota + start
                bias = jnp.where(jnp.logical_and(places >= first, places < last), 0.0, neg_large)
                bias = jnp.concatenate([bias, bias], axis=0)
                out = []
                found = [
                    jnp.concatenate(
                        [dot_nt(queries[u][h], kp_ref[2 * p + h, here, :]) for h in range(2)], axis=0
                    )
                    for u, p in enumerate(pairs)
                ]
                found_grad = [
                    jnp.concatenate(
                        [dot_nt(grads[u][h], vp_ref[2 * p + h, here, :]) for h in range(2)], axis=0
                    )
                    for u, p in enumerate(pairs)
                ]
                for u, p in enumerate(pairs):
                    lanes_of = slice(p * pair_lanes, (p + 1) * pair_lanes)
                    scores = bias + found[u]
                    weights = jnp.exp(scores - logs[u])
                    grad_weights = found_grad[u]
                    grad_scores = split_two(weights * (grad_weights - dots[u]))
                    new_state = folded(dot_nn, grad_scores, kb_ref[p, here, :])
                    out.append(new_state if state is None else state[u] + new_state)
                    dk_sum[here, lanes_of] += folded(dot_tn, grad_scores, query_both[u])
                    dv_sum[here, lanes_of] += folded(dot_tn, split_two(weights), grad_both[u])
                return tuple(out)

            def finish(state):
                for u, p in enumerate(pairs):
                    dq_ref[at, p * pair_lanes : (p + 1) * pair_lanes] = merge_heads(state[u], low_half) * scale

            @pl.when(block_count[index] == 1)
            def _():
                finish(chunk(0, None))

            @pl.when(block_count[index] > 1)
            def _():
                start_state = tuple(jnp.zeros((2 * q_rows, pair_lanes), f32) for _ in range(unroll))
                finish(lax.fori_loop(0, block_count[index], chunk, start_state))

        return carry

    lax.fori_loop(0, rows // q_rows, block, 0)


def own_lanes(ref, at, model, columns):
    if columns % pair_lanes == 0:
        return ref[at, pl.ds(pl.multiple_of(model * columns, pair_lanes), columns)]
    start = model * columns
    base = pl.multiple_of(start // pair_lanes * pair_lanes, pair_lanes)
    tile = ref[at, pl.ds(base, pair_lanes)]
    return pltpu.roll(tile, lax.rem(pair_lanes - lax.rem(start, pair_lanes), pair_lanes), 1)[:, :columns]


def norm_parts(values):
    centred = values - jnp.mean(values, axis=1, keepdims=True)
    scale = lax.rsqrt(jnp.mean(centred * centred, axis=1, keepdims=True) + norm_eps)
    return centred * scale, scale


def norm_back(grad, normal, scale, gain):
    inner = grad * gain
    return (
        inner
        - jnp.mean(inner, axis=1, keepdims=True)
        - normal * jnp.mean(inner * normal, axis=1, keepdims=True)
    ) * scale


def column_sum(value):
    return jnp.sum(value, axis=0, keepdims=True)


def chunks(rows, size, body):
    lax.fori_loop(0, rows // size, lambda step, carry: (body(pl.ds(pl.multiple_of(step * size, size), size)), carry)[1], 0)


def hand_out(index_ref, grads_ref, keep_ref, send_ref, rows, extra_ref=None):
    me = index_ref[0]
    odd = lax.rem(me, 2)
    for r in range(keep_ref.shape[0]):
        pair = 2 * ((me // 2) ^ r)
        for ref, which in ((keep_ref, pair + odd), (send_ref, pair + 1 - odd)):
            ref[r, :rows, :] = grads_ref[pl.ds(pl.multiple_of(which * rows, rows), rows), :]
            if extra_ref is not None:
                ref[r, rows:, :] = extra_ref[pl.ds(which, 1)][0]


def cross_back_kernel(
    unroll, scale, columns, rows_of, bias_rows, index_ref, block_low, block_count,
    g_ref, two_ref, one_ref, mem_ref, q_ref, k_ref, v_ref, o_ref, total_ref, low_ref, high_ref,
    w_ref, vec_ref, sums_ref, bias_ref,
    keep_ref, send_ref, resid_ref, mem_grad_ref,
    kp_ref, vp_ref, kb_ref, dk_sum, dv_sum, dq_ref, go_ref, two_grad_ref, woh, wol, wqh, wql, grads, totals, parts,
):
    rows, width = q_ref.shape
    model = index_ref[1]
    lanes = lax.broadcasted_iota(jnp.int32, (q_rows, pair_lanes), 1)
    low_half = lanes < pair_lanes // 2
    prepare(k_ref, low_half, kp_ref, kb_ref)
    prepare(v_ref, low_half, vp_ref, None)
    dk_sum[...] = jnp.zeros_like(dk_sum)
    dv_sum[...] = jnp.zeros_like(dv_sum)
    woh[...], wol[...] = split_two(w_ref[3])
    wqh[...], wql[...] = split_two(w_ref[0])
    totals[...] = sums_ref[...]
    grads[...] = jnp.zeros_like(grads)

    def before(at):
        normal, spread = norm_parts(two_ref[at, :])
        grad = g_ref[at, :]
        resid = norm_back(grad, normal, spread, vec_ref[0, 1:2, :])
        totals[1:2, :] += column_sum(grad * normal)
        totals[4:5, :] += column_sum(grad)
        two_grad_ref[at, :] = resid
        go_ref[at, :] = three(dot_nn, split_two(resid), (woh[...], wol[...]))

    chunks(rows, 256, before)
    attend_back_blocks(
        unroll, scale, block_low, block_count,
        q_ref, o_ref, go_ref, total_ref, low_ref, high_ref,
        dq_ref, kp_ref, vp_ref, kb_ref, dk_sum, dv_sum,
    )

    def after(at):
        resid = two_grad_ref[at, :]
        grad = resid + three(dot_nt, split_two(dq_ref[at, :]), (wqh[...], wql[...]))
        normal, spread = norm_parts(one_ref[at, :])
        gain = vec_ref[0, 0:1, :]
        resid_ref[at, :] = norm_back(grad, normal, spread, gain)
        totals[0:1, :] += column_sum(grad * normal)
        totals[3:4, :] += column_sum(grad)
        source = split_two(normal * gain + vec_ref[0, 3:4, :])
        memory = split_two(mem_ref[at, :])
        dk = dk_sum[at, :]
        dv = dv_sum[at, :]
        grads[:, :columns] += three(dot_tn, source, split_two(own_lanes(dq_ref, at, model, columns)))
        grads[:, columns : 2 * columns] += three(
            dot_tn, memory, split_two(own_lanes(dk_sum, at, model, columns))
        )
        grads[:, 2 * columns : 3 * columns] += three(
            dot_tn, memory, split_two(own_lanes(dv_sum, at, model, columns))
        )
        grads[:, 3 * columns :] += three(
            dot_tn, split_two(resid), split_two(own_lanes(o_ref, at, model, columns))
        )
        slice_of = pl.ds(pl.multiple_of(model * columns, columns), columns)
        mem_grad_ref[at, :] = three(dot_nt, split_two(dk), split_two(w_ref[1, slice_of, :])) + three(
            dot_nt, split_two(dv), split_two(w_ref[2, slice_of, :])
        )

    chunks(rows, 256, after)
    parts[...] = jnp.zeros_like(parts)
    for j in range(parts.shape[0]):
        parts[j, :, :rows_of] = totals[:, j * rows_of : (j + 1) * rows_of]
        parts[j, 7:8, :bias_rows] = bias_ref[:, j * bias_rows : (j + 1) * bias_rows]
    hand_out(index_ref, grads, keep_ref, send_ref, rows_of, parts)


def self_back_kernel(
    unroll, scale, columns, rows_of, index_ref, block_low, block_count,
    g_ref, x_ref, q_ref, k_ref, v_ref, o_ref, total_ref, low_ref, high_ref, w_ref,
    keep_ref, send_ref, dq_ref, dk_ref, dv_ref,
    kp_ref, vp_ref, kb_ref, dk_sum, dv_sum, go_ref, woh, wol, grads,
):
    rows, width = q_ref.shape
    model = index_ref[1]
    lanes = lax.broadcasted_iota(jnp.int32, (q_rows, pair_lanes), 1)
    low_half = lanes < pair_lanes // 2
    prepare(k_ref, low_half, kp_ref, kb_ref)
    prepare(v_ref, low_half, vp_ref, None)
    dk_sum[...] = jnp.zeros_like(dk_sum)
    dv_sum[...] = jnp.zeros_like(dv_sum)
    woh[...], wol[...] = split_two(w_ref[3])
    grads[...] = jnp.zeros_like(grads)

    def before(at):
        go_ref[at, :] = three(dot_nn, split_two(g_ref[at, :]), (woh[...], wol[...]))

    chunks(rows, 256, before)
    attend_back_blocks(
        unroll, scale, block_low, block_count,
        q_ref, o_ref, go_ref, total_ref, low_ref, high_ref,
        dq_ref, kp_ref, vp_ref, kb_ref, dk_sum, dv_sum,
    )

    def after(at):
        source = split_two(x_ref[at, :])
        dk_ref[at, :] = dk_sum[at, :]
        dv_ref[at, :] = dv_sum[at, :]
        for number, ref in enumerate((dq_ref, dk_sum, dv_sum)):
            grads[:, number * columns : (number + 1) * columns] += three(
                dot_tn, source, split_two(own_lanes(ref, at, model, columns))
            )
        grads[:, 3 * columns :] += three(
            dot_tn, split_two(g_ref[at, :]), split_two(own_lanes(o_ref, at, model, columns))
        )

    chunks(rows, 256, after)
    hand_out(index_ref, grads, keep_ref, send_ref, rows_of)


VM = functools.partial(pl.BlockSpec, memory_space=pltpu.VMEM)
SM = functools.partial(pl.BlockSpec, memory_space=pltpu.SMEM)


def attend(queries, keys_in, values_in, ranges, head_size, unroll=4):
    block_low, block_count, low, high = ranges
    rows, width = queries.shape
    pad_rows = keys_in.shape[0] + key_rows
    return pl.pallas_call(
        functools.partial(attend_kernel, unroll, head_size ** -0.5),
        out_shape=(
            jax.ShapeDtypeStruct((rows, width), f32),
            jax.ShapeDtypeStruct((rows, pair_lanes), f32),
        ),
        in_specs=[SM(), SM()] + [VM()] * 5,
        out_specs=(VM(), VM()),
        scratch_shapes=[
            pltpu.VMEM((width // 64, pad_rows, 2 * pair_lanes), bf16),
            pltpu.VMEM((width // pair_lanes, pad_rows, 2 * pair_lanes), bf16),
        ],
        compiler_params=pltpu.CompilerParams(vmem_limit_bytes=48 << 20),
        cost_estimate=pl.CostEstimate(flops=12 * rows * key_rows * width, bytes_accessed=16 * rows * width, transcendentals=rows * key_rows * 8),
        name="attend",
    )(block_low, block_count, queries, keys_in, values_in, low, high)


def back_scratch(rows, width):
    pad_rows = rows + key_rows
    return [
        pltpu.VMEM((width // 64, pad_rows, 2 * pair_lanes), bf16),
        pltpu.VMEM((width // 64, pad_rows, 2 * pair_lanes), bf16),
        pltpu.VMEM((width // pair_lanes, pad_rows, 2 * pair_lanes), bf16),
        pltpu.VMEM((pad_rows, width), f32),
        pltpu.VMEM((pad_rows, width), f32),
    ]


def cross_back(
    index, ranges, grad, two, one, memory, queries, keys_in, values_in, outputs, totals,
    matrices, vectors, sums, bias, head_size, columns, rows_of, bias_rows, unroll=4,
):
    block_low, block_count, low, high = ranges
    rows, width = queries.shape
    data = width // rows_of
    block = jax.ShapeDtypeStruct((data // 2, rows_of + 8, 4 * columns), f32)
    return pl.pallas_call(
        functools.partial(cross_back_kernel, unroll, head_size ** -0.5, columns, rows_of, bias_rows),
        out_shape=(
            block,
            block,
            jax.ShapeDtypeStruct((rows, width), f32),
            jax.ShapeDtypeStruct((rows, columns), f32),
        ),
        in_specs=[SM()] * 3 + [VM()] * 15,
        out_specs=(VM(),) * 4,
        scratch_shapes=back_scratch(rows, width)
        + [pltpu.VMEM((rows, width), f32)] * 3
        + [pltpu.VMEM((width, width), bf16)] * 4
        + [
            pltpu.VMEM((width, 4 * columns), f32),
            pltpu.VMEM((8, width), f32),
            pltpu.VMEM((data, 8, 4 * columns), f32),
        ],
        compiler_params=pltpu.CompilerParams(vmem_limit_bytes=60 << 20),
        cost_estimate=pl.CostEstimate(flops=30 << 30, bytes_accessed=30 << 20, transcendentals=rows * key_rows * 8),
        name="cross_back",
    )(
        index, block_low, block_count, grad, two, one, memory, queries, keys_in, values_in, outputs, totals,
        low, high, matrices, vectors, sums, bias,
    )


def self_back(
    index, ranges, grad, source, queries, keys_in, values_in, outputs, totals, matrices,
    head_size, columns, rows_of, unroll=4,
):
    block_low, block_count, low, high = ranges
    rows, width = queries.shape
    data = width // rows_of
    block = jax.ShapeDtypeStruct((data // 2, rows_of, 4 * columns), f32)
    return pl.pallas_call(
        functools.partial(self_back_kernel, unroll, head_size ** -0.5, columns, rows_of),
        out_shape=(block, block) + (jax.ShapeDtypeStruct((rows, width), f32),) * 3,
        in_specs=[SM()] * 3 + [VM()] * 10,
        out_specs=(VM(),) * 5,
        scratch_shapes=back_scratch(rows, width)
        + [pltpu.VMEM((rows, width), f32)]
        + [pltpu.VMEM((width, width), bf16)] * 2
        + [pltpu.VMEM((width, 4 * columns), f32)],
        compiler_params=pltpu.CompilerParams(vmem_limit_bytes=60 << 20),
        cost_estimate=pl.CostEstimate(flops=30 << 30, bytes_accessed=30 << 20, transcendentals=rows * key_rows * 8),
        name="self_back",
    )(
        index, block_low, block_count, grad, source, queries, keys_in, values_in, outputs, totals,
        low, high, matrices,
    )


def key_ranges(query_lengths, key_lengths, rows):
    query_ends = jnp.cumsum(query_lengths)
    query_starts = query_ends - query_lengths
    places = jnp.arange(rows, dtype=jnp.int32)
    low = jnp.sum(jnp.where(query_ends[None, :] <= places[:, None], key_lengths[None, :], 0), axis=1)
    high = jnp.sum(jnp.where(query_starts[None, :] <= places[:, None], key_lengths[None, :], 0), axis=1)
    block_low = low[::q_rows] // 16 * 16
    block_high = high[q_rows - 1 :: q_rows]
    block_count = (block_high - block_low + key_rows - 1) // key_rows
    return block_low, block_count, low[:, None], high[:, None]


def matmul(left_side, right_side):
    return jnp.dot(left_side, right_side, precision=lax.Precision.HIGH, preferred_element_type=f32)


def layer_norm(values, gain_row, shift_row):
    centre_mean = jnp.mean(values, axis=-1, keepdims=True)
    centred = values - centre_mean
    variance = jnp.mean(centred * centred, axis=-1, keepdims=True)
    return centred * lax.rsqrt(variance + norm_eps) * gain_row + shift_row


def flip(value, axis, distance):
    pairs = [(i, i ^ distance) for i in range(lax.axis_size(axis))]
    return lax.ppermute(value, axis, pairs)


def tree_total(pieces):
    while len(pieces) > 1:
        pieces = [pieces[i] + pieces[i + 1] for i in range(0, len(pieces), 2)]
    return pieces[0]


def small_total(value):
    value = value + flip(value, "dp", 1)
    others = lax.axis_size("dp") // 2
    value = tree_total([value] + [flip(value, "dp", 2 * r) for r in range(1, others)])
    models = lax.axis_size("mp")
    return tree_total([value] + [flip(value, "mp", r) for r in range(1, models)])


def ring_gather(own):
    count = lax.axis_size("mp")
    return [own] + [
        lax.ppermute(own, "mp", [(i, (i + step) % count) for i in range(count)])
        for step in range(1, count)
    ]


def ring_order(ring):
    count = len(ring)
    me = lax.axis_index("mp")
    found = []
    for place in range(count):
        value = ring[0]
        for step in range(1, count):
            value = jnp.where(me == (place + step) % count, ring[step], value)
        found.append(value)
    return found


def even_gather(own):
    return [own] + [flip(own, "dp", r) for r in range(2, lax.axis_size("dp"), 2)]


def odd_gather(even):
    odd = [flip(value, "dp", 1) for value in even]
    return [value for pair in zip(even, odd) for value in pair]


def place_kernel(parts, rows, columns, bias_rows, index_ref, *refs):
    pieces, (full_ref, vec_ref) = refs[:-2], refs[-2:]
    me, model = index_ref[0], index_ref[1]
    models = pieces[0].shape[0]
    width = vec_ref.shape[2]
    pad = jnp.zeros((8, width - columns), f32)
    bias_row = lax.broadcasted_iota(jnp.int32, (8, width), 0) == 7
    vec_ref[...] = jnp.zeros_like(vec_ref)
    for r, piece in enumerate(pieces):
        whose = me ^ r
        at = pl.ds(pl.multiple_of(whose * rows, rows), rows)
        for place in range(models):
            slot = lax.rem(model - place + models, models)
            for part in range(parts):
                full_ref[part, at, place * columns : (place + 1) * columns] = piece[
                    slot, part * rows : (part + 1) * rows, :
                ]
            values = jnp.concatenate([piece[slot, parts * rows :, :], pad], axis=1)
            moved = pltpu.roll(values, whose * rows, 1)
            if rows != bias_rows:
                moved = jnp.where(bias_row, pltpu.roll(values, whose * bias_rows, 1), moved)
            vec_ref[place] += moved


def place(pieces, index, parts, rows, columns, bias_rows):
    models, count = pieces[0].shape[0], len(pieces)
    return pl.pallas_call(
        functools.partial(place_kernel, parts, rows, columns, bias_rows),
        out_shape=(
            jax.ShapeDtypeStruct((parts, rows * count, columns * models), f32),
            jax.ShapeDtypeStruct((models, 8, columns * models), f32),
        ),
        in_specs=[SM()] + [VM()] * count,
        out_specs=(VM(), VM()),
        compiler_params=pltpu.CompilerParams(vmem_limit_bytes=40 << 20),
        name="place",
    )(index, *pieces)


def gelu_both(values):
    inner = 0.7978845608028654 * (values + 0.044715 * values * values * values)
    bent = jnp.tanh(inner)
    half = 0.5 * (1.0 + bent)
    slope = half + 0.5 * values * (1.0 - bent * bent) * (
        0.7978845608028654 * (1.0 + 3.0 * 0.044715 * values * values)
    )
    return values * half, slope


def wide_kernel(
    rows, model_ref, z_ref, g_ref, wide_ref, all_vec_ref,
    out_ref, second_ref, grads_ref, sums_ref, bias_grad_ref,
    eh_ref, el_ref, rh_ref, rl_ref, slope_ref, xh_ref, xl_ref,
):
    tokens, width = z_ref.shape
    data, models, _, units = wide_ref.shape
    model = model_ref[0]
    vec_ref = all_vec_ref.at[0]
    block = xh_ref.shape[0]

    def load(step, carry):
        which, part = step // models, step % models
        at = pl.ds(pl.multiple_of(which * rows, rows), rows)
        to = pl.ds(pl.multiple_of(part * units, units), units)
        eh_ref[at, to], el_ref[at, to] = split_two(wide_ref[which, part, :rows, :])
        rh_ref[at, to], rl_ref[at, to] = split_two(wide_ref[which, part, rows:, :])
        return carry

    lax.fori_loop(0, data * models, load, 0)
    sums_ref[...] = jnp.zeros_like(sums_ref)
    bias_grad_ref[...] = jnp.zeros_like(bias_grad_ref)
    grads_ref[...] = jnp.zeros_like(grads_ref)

    def chunk(step, carry):
        at = pl.ds(pl.multiple_of(step * block, block), block)
        source = z_ref[at, :]
        source_pair = split_two(source)

        def forward(part, reduced):
            to = pl.ds(pl.multiple_of(part * units, units), units)
            before = three(dot_nn, source_pair, (eh_ref[:, to], el_ref[:, to])) + all_vec_ref[part, 7:8, :units]
            value, slope = gelu_both(before)
            slope_ref[:, to] = slope
            high, low = split_two(value)
            xh_ref[:, to] = high
            xl_ref[:, to] = low
            return reduced + three(dot_nt, (high, low), (rh_ref[:, to], rl_ref[:, to]))

        reduced = lax.fori_loop(0, models, forward, source + vec_ref[6:7, :])
        normal, scale = norm_parts(reduced)
        gain = vec_ref[2:3, :]
        out_ref[at, :] = normal * gain + vec_ref[5:6, :]
        grad = g_ref[at, :]
        resid = norm_back(grad, normal, scale, gain)
        sums_ref[2:3, :] += column_sum(grad * normal)
        sums_ref[5:6, :] += column_sum(grad)
        sums_ref[6:7, :] += column_sum(resid)
        resid_pair = split_two(resid)

        def backward(part, second):
            to = pl.ds(pl.multiple_of(part * units, units), units)
            back = three(dot_nn, resid_pair, (rh_ref[:, to], rl_ref[:, to])) * slope_ref[:, to]
            back_pair = split_two(back)

            @pl.when(part == model)
            def _():
                bias_grad_ref[...] += jnp.sum(back, axis=0, keepdims=True)
                grads_ref[:, :units] += three(dot_tn, source_pair, back_pair)
                grads_ref[:, units:] += three(dot_tn, resid_pair, (xh_ref[:, to], xl_ref[:, to]))

            return second + three(dot_nt, back_pair, (eh_ref[:, to], el_ref[:, to]))

        second_ref[at, :] = lax.fori_loop(0, models, backward, resid)
        return carry

    lax.fori_loop(0, tokens // block, chunk, 0)


def feed_forward(model, source, grad, wide, vectors, rows):
    tokens, width = source.shape
    data, models, _, units = wide.shape
    block = min(512, tokens)
    return pl.pallas_call(
        functools.partial(wide_kernel, rows),
        out_shape=(
            jax.ShapeDtypeStruct((tokens, width), f32),
            jax.ShapeDtypeStruct((tokens, width), f32),
            jax.ShapeDtypeStruct((width, 2 * units), f32),
            jax.ShapeDtypeStruct((8, width), f32),
            jax.ShapeDtypeStruct((1, units), f32),
        ),
        in_specs=[SM()] + [VM()] * 4,
        out_specs=(VM(),) * 5,
        scratch_shapes=[pltpu.VMEM((width, models * units), bf16)] * 4
        + [
            pltpu.VMEM((block, models * units), f32),
            pltpu.VMEM((block, models * units), bf16),
            pltpu.VMEM((block, models * units), bf16),
        ],
        compiler_params=pltpu.CompilerParams(vmem_limit_bytes=60 << 20),
        cost_estimate=pl.CostEstimate(
            flops=27 * tokens * width * models * units, bytes_accessed=24 << 20, transcendentals=tokens * models * units
        ),
        name="feed_forward",
    )(model[None], source, grad, wide, vectors)


def cell(row, lane):
    return jnp.sum(
        jnp.where(lax.broadcasted_iota(jnp.int32, row.shape, 1) == lane, row, 0.0), axis=1, keepdims=True
    )


def total_of(value):
    return jnp.sum(jnp.sum(value, axis=1, keepdims=True), axis=0, keepdims=True)


def put(row, lane, value):
    return jnp.where(lax.broadcasted_iota(jnp.int32, row.shape, 1) == lane, value, row)


def part_row(pieces, divisor):
    row = jnp.zeros((1, 128), f32)
    for number, value in enumerate(pieces):
        total = total_of(value * value)
        row = put(row, number, total / divisor if 10 <= number < 17 else total)
    return row


def part_list(arrays):
    return (
        [arrays[0][i] for i in range(arrays[0].shape[0])]
        + [arrays[1][i] for i in range(arrays[1].shape[0])]
        + [arrays[2][...], arrays[3][...]]
        + [arrays[4][i : i + 1, :] for i in range(arrays[4].shape[0])]
        + [arrays[5][...]]
    )


def squares_kernel(divisor, count, *refs):
    self_pieces, cross_pieces, rest = refs[:count], refs[count : 2 * count], refs[2 * count :]
    wide, weights, (self_ref, cross_ref, vector_ref, row_ref) = rest[0][...], rest[1:-4], rest[-4:]
    rows = self_ref.shape[0]
    value = tree_total([piece[...] for piece in self_pieces])
    both = tree_total([piece[...] for piece in cross_pieces])
    cross, vectors = both[:rows], both[rows:, :rows]
    self_ref[...] = value
    cross_ref[...] = cross
    vector_ref[...] = vectors
    total = total_of(value * value) + total_of(cross * cross) + total_of(wide * wide)
    norms = vectors[:7]
    last = vectors[7:8]
    total = total + total_of(norms * norms) / divisor + total_of(last * last)
    row_ref[...] = put(part_row(part_list(weights), divisor), 18, total)


def moments_kernel(divisor, columns, row_ref, *refs):
    grads, rest = refs[:4], refs[4:]
    weights, firsts, seconds = rest[:6], rest[6:12], rest[12:18]
    new_firsts, new_seconds, updates, out_row = rest[18:24], rest[24:30], rest[30:36], rest[36]
    units = rest[2].shape[1]
    bias_rows = rest[5].shape[1]
    norm = jnp.sqrt(cell(row_ref[...], 18))
    clip = jnp.minimum(1.0, clip_norm / norm)
    first_fix = 1.0 - first_decay**STEP_NUM
    second_fix = 1.0 - second_decay**STEP_NUM

    def step(grad, weight, first, second, decay):
        clipped = grad * clip
        one = first_decay * first + (1.0 - first_decay) * clipped
        two = second_decay * second + (1.0 - second_decay) * clipped * clipped
        return one, two, one / first_fix / (jnp.sqrt(two / second_fix) + adam_eps) + decay * weight

    squares = []

    def store(number, at, grad, decay):
        one, two, update = step(
            grad, weights[number][at], firsts[number][at], seconds[number][at], decay
        )
        new_firsts[number][at] = one
        new_seconds[number][at] = two
        updates[number][at] = update
        return update

    for number in range(2):
        for which in range(3):
            store(0, 3 * number + which, grads[number][:, which * columns : (which + 1) * columns], matrix_decay)
    for number in range(2):
        store(1, number, grads[number][:, 3 * columns : 4 * columns], matrix_decay)
    store(2, slice(None), grads[2][:, :units], matrix_decay)
    store(3, slice(None), grads[2][:, units:], matrix_decay)
    store(4, slice(None), grads[3][:7, :], 0.0)
    store(5, slice(None), grads[3][7:8, :bias_rows], 0.0)
    out_row[...] = part_row(part_list(updates), divisor)


def apply_kernel(weight_row_ref, update_row_ref, *refs):
    weights, updates, new, copies = refs[:6], refs[6:12], refs[12:18], refs[18:22]
    norms_ref, grad_norm_ref = refs[22:]
    rate = peak_rate * min(STEP_NUM / warm_steps, (warm_steps / STEP_NUM) ** 0.5)
    weight_row, update_row = jnp.sqrt(weight_row_ref[...]), jnp.sqrt(update_row_ref[...])
    lanes = lax.broadcasted_iota(jnp.int32, weight_row.shape, 1)
    ratios = rate * (weight_row / jnp.where(lanes < 18, update_row, 1.0))

    def store(number, at, part):
        value = weights[number][at] - cell(ratios, part) * updates[number][at]
        new[number][at] = value
        if number < 4:
            copies[number][at] = value.astype(bf16)

    for which in range(6):
        store(0, which, which)
    for which in range(2):
        store(1, which, 6 + which)
    store(2, slice(None), 8)
    store(3, slice(None), 9)
    for which in range(7):
        store(4, slice(which, which + 1), 10 + which)
    store(5, slice(None), 17)
    norms_ref[0:1, :] = weight_row
    norms_ref[1:2, :] = update_row
    grad_norm_ref[...] = cell(weight_row, 18)


def same(arrays, dtype=f32):
    return tuple(jax.ShapeDtypeStruct(value.shape, dtype) for value in arrays)


def whole_call(kernel, name, out_shape, *arrays):
    return pl.pallas_call(
        kernel,
        out_shape=out_shape,
        in_specs=[VM()] * len(arrays),
        out_specs=jax.tree.map(lambda _: VM(), out_shape),
        compiler_params=pltpu.CompilerParams(vmem_limit_bytes=40 << 20),
        name=name,
    )(*arrays)


def pack_kernel(cap, starts_ref, source_ref, packed_ref, padded_ref):
    rows = source_ref.shape[0]
    padded_ref[:rows, :] = source_ref[...]
    padded_ref[rows:, :] = jnp.zeros((padded_ref.shape[0] - rows, source_ref.shape[1]), f32)

    def one(target, carry):
        packed_ref[pl.ds(target, 1)] = padded_ref[pl.ds(starts_ref[target], cap), :][None]
        return carry

    lax.fori_loop(0, packed_ref.shape[0], one, 0)


def pack_rows(source, starts, cap):
    rows, width = source.shape
    return pl.pallas_call(
        functools.partial(pack_kernel, cap),
        out_shape=jax.ShapeDtypeStruct((starts.shape[0], cap, width), f32),
        in_specs=[SM(), VM()],
        out_specs=VM(),
        scratch_shapes=[pltpu.VMEM((rows + cap, width), f32)],
        name="pack_rows",
    )(starts, source)


def unpack_kernel(slots_ref, arrived_ref, out_ref):
    def one(step, carry):
        for k in range(8):
            row = step * 8 + k
            out_ref[pl.ds(row, 1), :] = arrived_ref[pl.ds(slots_ref[row], 1), :]
        return carry

    lax.fori_loop(0, out_ref.shape[0] // 8, one, 0)


def unpack_rows(arrived, slots):
    return pl.pallas_call(
        unpack_kernel,
        out_shape=jax.ShapeDtypeStruct((slots.shape[0], arrived.shape[1]), f32),
        in_specs=[SM(), VM()],
        out_specs=VM(),
        name="unpack_rows",
    )(slots, arrived)


def place_back_kernel(slots_ref, grads_ref, out_ref):
    out_ref[...] = jnp.zeros_like(out_ref)

    def one(step, carry):
        for k in range(8):
            row = step * 8 + k
            out_ref[pl.ds(slots_ref[row], 1), :] = grads_ref[pl.ds(row, 1), :]
        return carry

    lax.fori_loop(0, grads_ref.shape[0] // 8, one, 0)


def place_back(grads_in, slots, total):
    return pl.pallas_call(
        place_back_kernel,
        out_shape=jax.ShapeDtypeStruct((total, grads_in.shape[1]), f32),
        in_specs=[SM(), VM()],
        out_specs=VM(),
        name="place_back",
    )(slots, grads_in)


def return_kernel(starts_ref, returned_ref, out_ref, padded_ref):
    cap = returned_ref.shape[1]

    def one(target, carry):
        padded_ref[pl.ds(starts_ref[target], cap), :] = returned_ref[pl.ds(target, 1)][0]
        return carry

    lax.fori_loop(0, returned_ref.shape[0], one, 0)
    out_ref[...] = padded_ref[: out_ref.shape[0], :]


def return_rows(returned, starts, rows):
    _, cap, width = returned.shape
    return pl.pallas_call(
        return_kernel,
        out_shape=jax.ShapeDtypeStruct((rows, width), f32),
        in_specs=[SM(), VM()],
        out_specs=VM(),
        scratch_shapes=[pltpu.VMEM((rows + cap, width), f32)],
        name="return_rows",
    )(starts, returned)


def cube_scatter(keep, send):
    both = keep + flip(send, "dp", 1)
    return [both[0]] + [flip(both[r], "dp", 2 * r) for r in range(1, both.shape[0])]


def shards(
    layer_input,
    encoder_memory,
    output_grad,
    target_lengths,
    memory_lengths,
    source_slots,
    pair_counts,
    attend_input,
    attend_output,
    expand_weight,
    reduce_weight,
    norm_vectors,
    expand_bias,
    attend_input_first,
    attend_input_second,
    attend_output_first,
    attend_output_second,
    expand_weight_first,
    expand_weight_second,
    reduce_weight_first,
    reduce_weight_second,
    norm_vectors_first,
    norm_vectors_second,
    expand_bias_first,
    expand_bias_second,
):
    data_count = lax.axis_size("dp")
    model_count = lax.axis_size("mp")
    me = lax.axis_index("dp")
    model = lax.axis_index("mp")
    tok_rows, width = layer_input.shape
    rows, columns = attend_input.shape[1:]
    units = expand_weight.shape[1]
    attend_output, attend_output_first, attend_output_second = [
        value.transpose(0, 2, 1) for value in (attend_output, attend_output_first, attend_output_second)
    ]
    reduce_weight, reduce_weight_first, reduce_weight_second = [
        value.T for value in (reduce_weight, reduce_weight_first, reduce_weight_second)
    ]
    weights = (attend_input, attend_output, expand_weight, reduce_weight, norm_vectors, expand_bias)

    extra_slots = tok_rows // 16
    slot_cap = (tok_rows - data_count // 4 * extra_slots) // data_count + extra_slots
    my_counts = lax.dynamic_index_in_dim(pair_counts, me, 0, keepdims=False)
    my_starts = jnp.cumsum(my_counts) - my_counts
    arrived = lax.all_to_all(
        pack_rows(encoder_memory, my_starts, slot_cap), "dp", split_axis=0, concat_axis=0, tiled=True
    )

    bias_rows = expand_bias.shape[0]
    vectors = jnp.concatenate(
        [
            jnp.pad(norm_vectors, ((0, 0), (0, columns - rows))),
            jnp.pad(expand_bias[None], ((0, 0), (0, columns - bias_rows))),
        ],
        axis=0,
    )
    own_self = jnp.concatenate(
        [attend_input[:3].reshape(3 * rows, columns), attend_output[0], vectors], axis=0
    )
    own_cross = jnp.concatenate(
        [attend_input[3:].reshape(3 * rows, columns), attend_output[1], vectors], axis=0
    )
    own_wide = jnp.concatenate([expand_weight, reduce_weight], axis=0)
    index = jnp.stack([me, model])
    together = lax.optimization_barrier
    memory_own = unpack_rows(arrived.reshape(data_count * slot_cap, columns), source_slots)
    self_ring, own_cross, memory_own = together((ring_gather(own_self), own_cross, memory_own))
    self_even, cross_ring = together((even_gather(jnp.stack(self_ring)), ring_gather(own_cross)))
    memory_ring = ring_gather(memory_own)
    memory_ring[1], own_wide = together((memory_ring[1], own_wide))
    all_wide = lax.all_gather(own_wide, ("dp", "mp"))
    self_pieces = odd_gather(self_even)
    cross_even = even_gather(jnp.stack(cross_ring))
    self_full, all_vectors = place(self_pieces, index, 4, rows, columns, bias_rows)
    all_wide = all_wide.reshape(data_count, model_count, 2 * rows, units)
    full_vectors = all_vectors[0]

    self_ranges = key_ranges(target_lengths[0], target_lengths[0], tok_rows)
    cross_ranges = key_ranges(target_lengths[0], memory_lengths[0], tok_rows)

    self_query = matmul(layer_input, self_full[0])
    self_key = matmul(layer_input, self_full[1])
    self_value = matmul(layer_input, self_full[2])
    self_out, self_totals = attend(self_query, self_key, self_value, self_ranges, HD)
    self_out, memory_ring, cross_even = together((self_out, memory_ring, cross_even))
    cross_full, _ = place(odd_gather(cross_even), index, 4, rows, columns, bias_rows)
    memory_target = jnp.concatenate(ring_order(memory_ring), axis=1)
    self_mix = matmul(self_out, self_full[3].T)
    first_sum = layer_input + self_mix
    first_norm = layer_norm(first_sum, full_vectors[0], full_vectors[3])
    cross_query = matmul(first_norm, cross_full[0])
    cross_key = matmul(memory_target, cross_full[1])
    cross_value = matmul(memory_target, cross_full[2])
    cross_out, cross_totals = attend(cross_query, cross_key, cross_value, cross_ranges, HD)
    cross_mix = matmul(cross_out, cross_full[3].T)
    second_sum = first_norm + cross_mix
    second_norm = layer_norm(second_sum, full_vectors[1], full_vectors[4])
    layer_output, second_grad, grad_wide, wide_sums, grad_bias = feed_forward(
        model,
        second_norm,
        output_grad,
        all_wide,
        all_vectors,
        rows,
    )

    grad_wide = lax.psum_scatter(
        grad_wide.reshape(data_count, rows, 2 * units), "dp", scatter_dimension=0, tiled=False
    )
    keep, send, resid_one_grad, memory_grad_own = cross_back(
        index,
        cross_ranges,
        second_grad,
        second_sum,
        first_sum,
        memory_target,
        cross_query,
        cross_key,
        cross_value,
        cross_out,
        cross_totals,
        cross_full,
        all_vectors,
        wide_sums,
        grad_bias,
        HD,
        columns,
        rows,
        bias_rows,
    )
    placed = place_back(memory_grad_own, source_slots, data_count * slot_cap)
    resid_one_grad, placed = together((resid_one_grad, placed))
    returned = lax.all_to_all(
        placed.reshape(data_count, slot_cap, columns), "dp", split_axis=0, concat_axis=0, tiled=True
    )
    grad_cross = cube_scatter(keep, send)
    keep, send, self_query_grad, self_key_grad, self_value_grad = self_back(
        index,
        self_ranges,
        resid_one_grad,
        layer_input,
        self_query,
        self_key,
        self_value,
        self_out,
        self_totals,
        self_full,
        HD,
        columns,
        rows,
    )
    grad_self = cube_scatter(keep, send)
    memory_grad = return_rows(returned, my_starts, tok_rows)
    input_grad = (
        resid_one_grad
        + matmul(self_query_grad, self_full[0].T)
        + matmul(self_key_grad, self_full[1].T)
        + matmul(self_value_grad, self_full[2].T)
    )

    weights = weights[:5] + (expand_bias[None],)
    firsts = (
        attend_input_first,
        attend_output_first,
        expand_weight_first,
        reduce_weight_first,
        norm_vectors_first,
        expand_bias_first[None],
    )
    seconds = (
        attend_input_second,
        attend_output_second,
        expand_weight_second,
        reduce_weight_second,
        norm_vectors_second,
        expand_bias_second[None],
    )
    row_shape = jax.ShapeDtypeStruct((1, 128), f32)
    grad_self, grad_cross, grad_vectors, row = whole_call(
        functools.partial(squares_kernel, model_count, len(grad_self)),
        "squares",
        same(grad_self[:1] * 2) + (jax.ShapeDtypeStruct((8, rows), f32), row_shape),
        *grad_self,
        *grad_cross,
        grad_wide,
        *weights,
    )
    row = small_total(row)
    moved = whole_call(
        functools.partial(moments_kernel, model_count, columns),
        "moments",
        same(weights) * 3 + (row_shape,),
        row,
        grad_self,
        grad_cross,
        grad_wide,
        grad_vectors,
        *weights,
        *firsts,
        *seconds,
    )
    new_firsts, new_seconds, updates = moved[:6], moved[6:12], moved[12:18]
    applied = whole_call(
        apply_kernel,
        "apply",
        same(weights)
        + same(weights[:4], bf16)
        + (jax.ShapeDtypeStruct((2, 128), f32), jax.ShapeDtypeStruct((1, 1), f32)),
        row,
        small_total(moved[18]),
        *weights,
        *updates,
    )
    new_weights = applied[:5] + (applied[5][0],)
    matrix_norms = applied[10][:, :10]

    def turned(values):
        return (values[0], values[1].transpose(0, 2, 1), values[2], values[3].T) + tuple(values[4:])

    new_weights, copies = turned(new_weights), turned(applied[6:10])
    new_firsts, new_seconds = turned(new_firsts), turned(new_seconds)
    return (
        layer_output,
        input_grad,
        memory_grad,
        applied[11][0],
        *new_weights,
        *copies,
        new_firsts[0],
        new_seconds[0],
        new_firsts[1],
        new_seconds[1],
        new_firsts[2],
        new_seconds[2],
        new_firsts[3],
        new_seconds[3],
        new_firsts[4],
        new_seconds[4],
        new_firsts[5][0],
        new_seconds[5][0],
        matrix_norms,
    )


def solution(mesh):
    in_specs = (
        P("dp", None),
        P("dp", "mp"),
        P("dp", None),
        P("dp", None),
        P("dp", None),
        P("dp"),
        P(),
        P(None, "dp", "mp"),
        P(None, "mp", "dp"),
        P("dp", "mp"),
        P("mp", "dp"),
        P(None, "dp"),
        P(("mp", "dp")),
        P(None, "dp", "mp"),
        P(None, "dp", "mp"),
        P(None, "mp", "dp"),
        P(None, "mp", "dp"),
        P("dp", "mp"),
        P("dp", "mp"),
        P("mp", "dp"),
        P("mp", "dp"),
        P(None, "dp"),
        P(None, "dp"),
        P(("mp", "dp")),
        P(("mp", "dp")),
    )
    out_specs = (
        P("dp", None),
        P("dp", None),
        P("dp", "mp"),
        P(),
        P(None, "dp", "mp"),
        P(None, "mp", "dp"),
        P("dp", "mp"),
        P("mp", "dp"),
        P(None, "dp"),
        P(("mp", "dp")),
        P(None, "dp", "mp"),
        P(None, "mp", "dp"),
        P("dp", "mp"),
        P("mp", "dp"),
        P(None, "dp", "mp"),
        P(None, "dp", "mp"),
        P(None, "mp", "dp"),
        P(None, "mp", "dp"),
        P("dp", "mp"),
        P("dp", "mp"),
        P("mp", "dp"),
        P("mp", "dp"),
        P(None, "dp"),
        P(None, "dp"),
        P(("mp", "dp")),
        P(("mp", "dp")),
        P(),
    )
    return jax.shard_map(shards, mesh=mesh, in_specs=in_specs, out_specs=out_specs, check_vma=False)
```

time: 566 us -> 392 us (0.69)
  matrix products: 127 us -> 36.7 us
  local copies, waits for them, and re-layouts: 62.5 us -> 9.27 us
  starting transfers between devices: 97.4 us -> 50.1 us
  Pallas kernels: 140 us -> 184 us
  other arithmetic: 35.2 us -> 10.3 us
  between operations: 27.1 us -> 15.5 us
  waiting for transfers between devices: 69.8 us -> 78.8 us
    dot_general x30 -> x11, matrix products: 127 us -> 36.7 us  [matmul(): jnp.dot(left_side, right_side, precision=lax.Precision.HIGH, preferred_el...]
    pallas_call x4 -> x8, Pallas kernels: 74.6 us -> 145 us  [the longest x1 52.2 us: feed_forward(): pl.pallas_call(functools.partial(wide_kernel, rows), out_shape=(jax.Shape...]
    pallas_call x2, Pallas kernels: 54.9 us -> 28.1 us  [attend(): pl.pallas_call(functools.partial(attend_kernel, unroll, head_size ** (-0....]
    ppermute x18 -> x9, starting transfers between devices: 33.4 us -> 7.66 us  [ring_gather(): lax.ppermute(own, 'mp', [(i, (i + step) % count) for i in range(count)])]
    ppermute x43 -> x36, starting transfers between devices: 55.4 us -> 33.2 us  [flip(): return lax.ppermute(value, axis, pairs)]
    unnamed x165 -> x106, local copies, waits for them, and re-layouts: 23.8 us -> 4.62 us
    reduce_sum x19 -> x0, other arithmetic: 18.3 us -> none  [the longest x3 6.93 us: layer_norm(): centred = values - centre_mean]
    ppermute x18 -> x9, waiting for transfers between devices: 25.6 us -> 42.8 us  [ring_gather(): lax.ppermute(own, 'mp', [(i, (i + step) % count) for i in range(count)])]
  transfers between devices with their start and end apart: 66 -> 49, of which waited for: 18 -> 19; matrix products, arithmetic and copies ran while one was open for 17% -> 13% of each run, Pallas kernels for 19% -> 33%
where the time goes in v2:
time: 392 us; the launch traced here: 384 us
  Pallas kernels  184 us (47%)
  waiting for transfers between devices  78.8 us (20%)
  starting transfers between devices  50.1 us (13%)
  matrix products  36.7 us (9%)
  between operations  15.5 us (4%)
  other arithmetic  10.3 us (3%)
  local copies, waits for them, and re-layouts  9.27 us (2%)
    pallas_call x1, Pallas kernels, feed_forward(): pl.pallas_call(functools.partial(wide_kernel, rows), out_shape=(jax.Shape...  52.2 us
    pallas_call x1, Pallas kernels, cross_back(): pl.pallas_call(functools.partial(cross_back_kernel, unroll, head_size **...  48.1 us
    ppermute x9, waiting for transfers between devices, ring_gather(): lax.ppermute(own, 'mp', [(i, (i + step) % count) for i in range(count)])  42.8 us
    pallas_call x1, Pallas kernels, self_back(): pl.pallas_call(functools.partial(self_back_kernel, unroll, head_size ** (...  38.5 us
    dot_general x11, matrix products, matmul(): jnp.dot(left_side, right_side, precision=lax.Precision.HIGH, preferred_el...  36.7 us
    ppermute x36, starting transfers between devices, flip(): return lax.ppermute(value, axis, pairs)  33.2 us
    ppermute x36, waiting for transfers between devices, flip(): return lax.ppermute(value, axis, pairs)  28.9 us
    pallas_call x2, Pallas kernels, attend(): pl.pallas_call(functools.partial(attend_kernel, unroll, head_size ** (-0....  28.1 us
  transfers between devices with their start and end apart: 49, of which 19 were waited for; matrix products, arithmetic and copies ran while one was open for 13% of the time, Pallas kernels for 33%

profile of v2, /device:TPU:0, one launch (start us, length us, event | category | flops | bytes accessed | tf_op | source)
XLA Modules:
  0.0 384.5 jit_solution(15626231454141207094)
XLA Ops:
  8.2 1.2 bitcast_subtract_fusion.1.starts_ref
  9.4 2.0 pack_rows.1
  11.4 5.3 %all-to-all-start = ((f32[8,176,128]{2,1,0:T(8,128)}), f32[8,176,128]{2,1,0:T(8,128)S(1)}, u32[]{:S(2)}, u32[]{:S(2)}) async-start(f32[8,176,128]{2,1,0:T(8,128)} %pack_rows.1), calls=%async_computation | async-start | bytes 1441792 | tf_op jit(solution)/shard_map/all_to_all | solution.py:1048
  16.9 3.7 collective-permute-start.2
  20.6 1.0 collective-permute-start
  21.6 7.1 %all-to-all-done = f32[8,176,128]{2,1,0:T(8,128)S(1)} async-done(((f32[8,176,128]{2,1,0:T(8,128)}), f32[8,176,128]{2,1,0:T(8,128)S(1)}, u32[]{:S(2)}, u32[]{:S(2)}) %all-to-all-start) | async-done | bytes 720928 | tf_op jit(solution)/shard_map/all_to_all | solution.py:1048
  29.5 3.3 unpack_rows.1
  32.9 1.5 collective-permute-start.13
  35.2 13.2 %collective-permute-done.13 = f32[1024,128]{1,0:T(8,128)S(1)} collective-permute-done((f32[1024,128]{1,0:T(8,128)}, f32[1024,128]{1,0:T(8,128)S(1)}, u32[]{:S(2)}, u32[]{:S(2)}) %collective-permute-start.13) | collective-permute-done | bytes 524320 | tf_op jit(solution)/shard_map/ppermute | solution.py:603
  49.3 2.5 collective-permute-start.5
  53.8 6.3 %collective-permute-done.8 = f32[264,128]{1,0:T(8,128)S(1)} collective-permute-done((f32[264,128]{1,0:T(8,128)S(1)}, f32[264,128]{1,0:T(8,128)S(1)}, u32[]{:S(2)}, u32[]{:S(2)}) %collective-permute-start.8) | collective-permute-done | bytes 135200 | tf_op jit(solution)/shard_map/ppermute | solution.py:603
  60.7 1.1 copy.80.high_ref
  61.8 1.0 copy.79.low_ref
  63.0 1.0 copy.77.high_ref
  64.2 6.0 %collective-permute-done.7 = f32[264,128]{1,0:T(8,128)} collective-permute-done((f32[264,128]{1,0:T(8,128)S(1)}, f32[264,128]{1,0:T(8,128)}, u32[]{:S(2)}, u32[]{:S(2)}) %collective-permute-start.7) | collective-permute-done | bytes 135200 | tf_op jit(solution)/shard_map/ppermute | solution.py:603
  70.1 6.4 %collective-permute-done.4.refs_4_ = f32[4,264,128]{2,1,0:T(8,128)S(1)} collective-permute-done((f32[4,264,128]{2,1,0:T(8,128)S(1)}, f32[4,264,128]{2,1,0:T(8,128)S(1)}, u32[]{:S(2)}, u32[]{:S(2)}) %collective-permute-start.4) | collective-permute-done | bytes 540704 | tf_op jit(solution)/shard_map/ppermute | solution.py:583
  78.5 1.0 pad_maximum_fusion.2.refs_0_
  80.1 2.3 collective-permute-start.18
  83.6 1.7 place.2
  85.3 3.2 convolution_bitcast_fusion.v_ref
  88.4 3.2 convolution_bitcast_fusion.1.k_ref
  91.6 1.9 convolution_bitcast_fusion.2.q_ref
  93.5 13.2 %attend.2 = (f32[1024,512]{1,0:T(8,128)S(1)}, f32[1024,128]{1,0:T(8,128)S(1)}) custom-call(s32[8]{0:T(128)S(1)} %get-tuple-element.198.block_low, s32[8]{0:T(128)S(1)} %get-tuple-element.197.block_count, f32[1024,512]{1,0:T(8,128)S(1)} %convolution_bitcast_fusion.2.q_ref, f32[1024,512]{1,0:T(8,128)} %convolution_bitcast_fusion.1.k_ref, ...), custom_call_target="tpu_custom_call" | custom-call | flops 1610612736 | bytes 8388608 | tf_op jit(solution)/shard_map/attend/pallas_call | solution.py:468
  106.8 17.2 %collective-permute-done.14 = f32[1024,128]{1,0:T(8,128)} collective-permute-done((f32[1024,128]{1,0:T(8,128)S(1)}, f32[1024,128]{1,0:T(8,128)}, u32[]{:S(2)}, u32[]{:S(2)}) %collective-permute-start.14) | collective-permute-done | bytes 524320 | tf_op jit(solution)/shard_map/ppermute | solution.py:603
  125.1 4.2 %fusion.44 = (f32[1024]{0:T(1024)S(1)}, f32[1024,512]{1,0:T(8,128)S(1)}) fusion(f32[1024,512]{1,0:T(8,128)} %x_ref.1, f32[1024,512]{1,0:T(8,128)S(1)} %get-tuple-element.127.o_ref, f32[4,512,512]{2,1,0:T(8,128)S(1)} %get-tuple-element.119.w_ref), kind=kOutput, calls=%fused_computation.109 | convolution fusion | flops 1611660288 | bytes 7344128 | tf_op jit(solution)/shard_map/dot_general | solution.py:571
  129.8 1.0 copy-done.49
  130.8 1.5 select_select_fusion.3
  132.2 1.4 pad_maximum_fusion.mem_ref
  133.7 1.8 place.3
  135.5 3.2 fusion.2.v_ref
  138.7 3.3 fusion.4.k_ref
  142.0 1.9 fusion.q_ref
  144.0 14.9 %attend.3 = (f32[1024,512]{1,0:T(8,128)S(1)}, f32[1024,128]{1,0:T(8,128)S(1)}) custom-call(s32[8]{0:T(128)S(1)} %get-tuple-element.200.block_low, s32[8]{0:T(128)S(1)} %get-tuple-element.199.block_count, f32[1024,512]{1,0:T(8,128)S(1)} %fusion.q_ref, f32[1024,512]{1,0:T(8,128)} %fusion.4.k_ref, f32[1024,512]{1,0:T(8,128)} %fusion.2.v_ref, ...), custom_call_target="tpu_custom_call" | custom-call | flops 1610612736 | bytes 8388608 | tf_op jit(solution)/shard_map/attend/pallas_call | solution.py:468
  158.9 2.3 fusion.45
  161.7 1.7 multiply_add_fusion.z_ref
  163.4 52.2 %feed_forward.1 = (f32[1024,512]{1,0:T(8,128)}, f32[1024,512]{1,0:T(8,128)}, f32[512,1024]{1,0:T(8,128)}, f32[8,512]{1,0:T(8,128)}, f32[1,512]{1,0:T(1,128)}) custom-call(s32[1]{0:T(128)} %bitcast.model_ref, f32[1024,512]{1,0:T(8,128)} %multiply_add_fusion.z_ref, f32[1024,512]{1,0:T(8,128)} %g_ref.1, f32[8,4,128,512]{3,2,1,0:T(8,128)} %bitcast.173, ...), custom_call_target="tpu_custom_call" | custom-call | flops 28991029248 | bytes 25165824 | tf_op jit(solution)/shard_map/feed_forward/pallas_call | solution.py:751
  215.6 48.1 %cross_back.1 = (f32[4,72,512]{2,1,0:T(8,128)}, f32[4,72,512]{2,1,0:T(8,128)}, f32[1024,512]{1,0:T(8,128)}, f32[1024,128]{1,0:T(8,128)}) custom-call(s32[2]{0:T(128)} %copy-done.28, s32[8]{0:T(128)} %copy-done.32, s32[8]{0:T(128)} %copy-done.31, f32[1024,512]{1,0:T(8,128)} %get-tuple-element.141.g_ref, f32[1024,512]{1,0:T(8,128)} %copy-done.40, ...), custom_call_target="tpu_custom_call" | custom-call | flops 32212254720 | bytes 31457280 | tf_op jit(solution)/shard_map/cross_back/pallas_call | solution.py:505
  263.7 3.3 place_back.1
  267.0 38.5 %self_back.1 = (f32[4,64,512]{2,1,0:T(8,128)}, f32[4,64,512]{2,1,0:T(8,128)}, f32[1024,512]{1,0:T(8,128)}, f32[1024,512]{1,0:T(8,128)}, f32[1024,512]{1,0:T(8,128)}) custom-call(s32[2]{0:T(128)} %copy-done.28, s32[8]{0:T(128)} %copy-done.30, s32[8]{0:T(128)} %copy-done.29, f32[1024,512]{1,0:T(8,128)} %get-tuple-element.147.g_ref, f32[1024,512]{1,0:T(8,128)} %x_ref.1, ...), custom_call_target="tpu_custom_call" | custom-call | flops 32212254720 | bytes 31457280 | tf_op jit(solution)/shard_map/self_back/pallas_call | solution.py:540
  306.1 1.6 collective-permute-done.23
  307.7 1.1 add.135
  309.8 2.4 collective-permute-start.30
  313.4 1.8 collective-permute-start.25
  315.2 1.1 collective-permute-done.26.refs_3_
  317.2 7.3 %collective-permute-done.25.refs_2_ = f32[64,512]{1,0:T(8,128)S(1)} collective-permute-done((f32[64,512]{1,0:T(8,128)S(1)}, f32[64,512]{1,0:T(8,128)S(1)}, u32[]{:S(2)}, u32[]{:S(2)}) %collective-permute-start.25) | collective-permute-done | bytes 131104 | tf_op jit(solution)/shard_map/ppermute | solution.py:583
  325.8 1.1 collective-permute-done.31
  327.0 1.0 collective-permute-start.34
  327.9 1.4 collective-permute-start.33
  329.4 1.1 collective-permute-start.32
  330.4 0.9 collective-permute-done.34
  331.5 1.4 collective-permute-done.32
  332.9 4.3 %collective-permute-start.37 = (f32[1,128]{1,0:T(1,128)S(1)}, f32[1,128]{1,0:T(1,128)S(1)}, u32[]{:S(2)}, u32[]{:S(2)}) collective-permute-start(f32[1,128]{1,0:T(1,128)S(1)} %add_add_fusion.4), channel_id=1, source_target_pairs={{0,3},{1,2},{2,1},{3,0},{4,7},{5,6},{6,5},{7,4},{8,11},{9,10},{10,... | collective-permute-start | bytes 1544 | tf_op jit(solution)/shard_map/ppermute | solution.py:583
  338.7 2.9 collective-permute-done.36
  341.8 1.5 moments.1
  343.3 4.4 %fusion.13 = f32[1024,512]{1,0:T(8,128)} fusion(f32[1024,512]{1,0:T(8,128)S(1)} %copy-done.44, f32[4,512,512]{2,1,0:T(8,128)} %copy-done), kind=kOutput, calls=%fused_computation.24 | convolution fusion | flops 1610612736 | bytes 5242880 | tf_op jit(solution)/shard_map/dot_general | solution.py:571
  347.7 3.8 all-to-all-start.1
  351.5 3.0 collective-permute-start.41
  355.1 3.9 %fusion.10 = f32[1024,512]{1,0:T(8,128)S(1)} fusion(f32[1024,512]{1,0:T(8,128)} %get-tuple-element.150, f32[4,512,512]{2,1,0:T(8,128)} %copy-done), kind=kOutput, calls=%fused_computation.21 | convolution fusion | flops 1610612736 | bytes 5242880 | tf_op jit(solution)/shard_map/dot_general | solution.py:571
  359.0 4.4 %collective-permute-done.41 = f32[1,128]{1,0:T(1,128)S(1)} collective-permute-done((f32[1,128]{1,0:T(1,128)S(1)}, f32[1,128]{1,0:T(1,128)S(1)}, u32[]{:S(2)}, u32[]{:S(2)}) %collective-permute-start.41) | collective-permute-done | bytes 544 | tf_op jit(solution)/shard_map/ppermute | solution.py:583
  363.4 1.5 collective-permute-start.44
  365.6 2.3 collective-permute-start.42
  367.9 5.3 %add_add_fusion = f32[1024,512]{1,0:T(8,128)} fusion(f32[1024,512]{1,0:T(8,128)S(1)} %fusion.10, f32[1024,512]{1,0:T(8,128)S(1)} %copy-done.45, f32[1024,512]{1,0:T(8,128)S(1)} %copy-done.41, f32[1024,512]{1,0:T(8,128)} %get-tuple-element.151, f32[4,512,512]{2,1,0:T(8,128)} %copy-done), kind=kOutput, calls=%fused_computation.1 | convolution fusion | flops 1612185600 | bytes 11534336 | tf_op jit(solution)/shard_map/dot_general | solution.py:571
  374.1 2.0 return_rows.1
  376.1 1.0 apply.1
  (212 shorter events, 20.9 us)
Async XLA Ops:
  11.4 17.2 %all-to-all-start = ((f32[8,176,128]{2,1,0:T(8,128)}), f32[8,176,128]{2,1,0:T(8,128)S(1)}, u32[]{:S(2)}, u32[]{:S(2)}) async-start(f32[8,176,128]{2,1,0:T(8,128)} %pack_rows.1), calls=%async_computation | async-start | bytes 1441792 | tf_op jit(solution)/shard_map/all_to_all | solution.py:1048
  16.7 146.6 %all-gather.3.cloned.1.call-start = ((), (), s32[]{:S(2)}) async-start(), calls=%async_computation.4 | async-start | bytes 8650752 | tf_op jit(solution)/shard_map/all_gather | solution.py:1074
  16.8 36.0 %copy-start.50 = (s32[1,32]{1,0:T(1,128)S(1)}, s32[1,32]{1,0:T(1,128)}, u32[]{:S(2)}) copy-start(s32[1,32]{1,0:T(1,128)} %param.28) | copy-start | bytes 388
  16.8 43.4 %copy-start.51 = (s32[1,32]{1,0:T(1,128)S(1)}, s32[1,32]{1,0:T(1,128)}, u32[]{:S(2)}) copy-start(s32[1,32]{1,0:T(1,128)} %param.29) | copy-start | bytes 388
  16.9 15.9 %collective-permute-start.2 = (f32[264,128]{1,0:T(8,128)S(1)}, f32[264,128]{1,0:T(8,128)S(1)}, u32[]{:S(2)}, u32[]{:S(2)}) collective-permute-start(f32[264,128]{1,0:T(8,128)S(1)} %get-tuple-element.110), channel_id=1, source_target_pairs={{0,3},{1,0},{2,1},{3,2},{4,7},{5,4},{6,5},{7,6},{8,11},{9,8},{10,9... | collective-permute-start | bytes 405512 | tf_op jit(solution)/shard_map/ppermute | solution.py:603
  20.6 12.4 %collective-permute-start.1 = (f32[264,128]{1,0:T(8,128)S(1)}, f32[264,128]{1,0:T(8,128)S(1)}, u32[]{:S(2)}, u32[]{:S(2)}) collective-permute-start(f32[264,128]{1,0:T(8,128)S(1)} %get-tuple-element.110), channel_id=1, source_target_pairs={{0,2},{1,3},{2,0},{3,1},{4,6},{5,7},{6,4},{7,5},{8,10},{9,11},{10,... | collective-permute-start | bytes 405512 | tf_op jit(solution)/shard_map/ppermute | solution.py:603
  20.6 12.4 %collective-permute-start = (f32[264,128]{1,0:T(8,128)S(1)}, f32[264,128]{1,0:T(8,128)S(1)}, u32[]{:S(2)}, u32[]{:S(2)}) collective-permute-start(f32[264,128]{1,0:T(8,128)S(1)} %get-tuple-element.110), channel_id=1, source_target_pairs={{0,1},{1,2},{2,3},{3,0},{4,5},{5,6},{6,7},{7,4},{8,9},{9,10},{10,1... | collective-permute-start | bytes 405512 | tf_op jit(solution)/shard_map/ppermute | solution.py:603
  32.8 45.0 %copy-start.46 = (f32[1024,128]{1,0:T(8,128)S(1)}, f32[1024,128]{1,0:T(8,128)}, u32[]{:S(2)}) copy-start(f32[1024,128]{1,0:T(8,128)} %unpack_rows.1) | copy-start | bytes 1572868
  32.9 15.5 %collective-permute-start.13 = (f32[1024,128]{1,0:T(8,128)}, f32[1024,128]{1,0:T(8,128)S(1)}, u32[]{:S(2)}, u32[]{:S(2)}) collective-permute-start(f32[1024,128]{1,0:T(8,128)} %unpack_rows.1), channel_id=1, source_target_pairs={{0,1},{1,2},{2,3},{3,0},{4,5},{5,6},{6,7},{7,4},{8,9},{9,10},{10,1... | collective-permute-start | bytes 1572872 | tf_op jit(solution)/shard_map/ppermute | solution.py:603
  48.4 276.1 %reduce-scatter.2.cloned.1.call-start = ((), (), s32[]{:S(2)}) async-start(), calls=%async_computation.3 | async-start | bytes 2359296 | tf_op jit(solution)/shard_map/reduce_scatter | solution.py:1110
  49.3 20.9 %collective-permute-start.5 = (f32[4,264,128]{2,1,0:T(8,128)S(1)}, f32[4,264,128]{2,1,0:T(8,128)S(1)}, u32[]{:S(2)}, u32[]{:S(2)}) collective-permute-start(f32[4,264,128]{2,1,0:T(8,128)S(1)} %pad_maximum_fusion.1.refs_0_), channel_id=1, source_target_pairs={{0,24},{4,28},{8,16},{12,20},{16,8},{20,12},{24,0},{28,4},{1,25},{... | collective-permute-start | bytes 1622024 | tf_op jit(solution)/shard_map/ppermute | solution.py:583
  51.8 24.8 %collective-permute-start.4 = (f32[4,264,128]{2,1,0:T(8,128)S(1)}, f32[4,264,128]{2,1,0:T(8,128)S(1)}, u32[]{:S(2)}, u32[]{:S(2)}) collective-permute-start(f32[4,264,128]{2,1,0:T(8,128)S(1)} %pad_maximum_fusion.1.refs_0_), channel_id=1, source_target_pairs={{0,16},{4,20},{8,24},{12,28},{16,0},{20,4},{24,8},{28,12},{1,17},{... | collective-permute-start | bytes 1622024 | tf_op jit(solution)/shard_map/ppermute | solution.py:583
  52.3 24.4 %collective-permute-start.3 = (f32[4,264,128]{2,1,0:T(8,128)S(1)}, f32[4,264,128]{2,1,0:T(8,128)}, u32[]{:S(2)}, u32[]{:S(2)}) collective-permute-start(f32[4,264,128]{2,1,0:T(8,128)S(1)} %pad_maximum_fusion.1.refs_0_), channel_id=1, source_target_pairs={{0,8},{4,12},{8,0},{12,4},{16,24},{20,28},{24,16},{28,20},{1,9},{5... | collective-permute-start | bytes 1622024 | tf_op jit(solution)/shard_map/ppermute | solution.py:583
  53.1 7.1 %collective-permute-start.8 = (f32[264,128]{1,0:T(8,128)S(1)}, f32[264,128]{1,0:T(8,128)S(1)}, u32[]{:S(2)}, u32[]{:S(2)}) collective-permute-start(f32[264,128]{1,0:T(8,128)S(1)} %get-tuple-element.123), channel_id=1, source_target_pairs={{0,3},{1,0},{2,1},{3,2},{4,7},{5,4},{6,5},{7,6},{8,11},{9,8},{10,9... | collective-permute-start | bytes 405512 | tf_op jit(solution)/shard_map/ppermute | solution.py:603
  53.8 16.3 %collective-permute-start.7 = (f32[264,128]{1,0:T(8,128)S(1)}, f32[264,128]{1,0:T(8,128)}, u32[]{:S(2)}, u32[]{:S(2)}) collective-permute-start(f32[264,128]{1,0:T(8,128)S(1)} %get-tuple-element.123), channel_id=1, source_target_pairs={{0,2},{1,3},{2,0},{3,1},{4,6},{5,7},{6,4},{7,5},{8,10},{9,11},{10,... | collective-permute-start | bytes 405512 | tf_op jit(solution)/shard_map/ppermute | solution.py:603
  60.2 10.0 %collective-permute-start.6 = (f32[264,128]{1,0:T(8,128)S(1)}, f32[264,128]{1,0:T(8,128)}, u32[]{:S(2)}, u32[]{:S(2)}) collective-permute-start(f32[264,128]{1,0:T(8,128)S(1)} %get-tuple-element.123), channel_id=1, source_target_pairs={{0,1},{1,2},{2,3},{3,0},{4,5},{5,6},{6,7},{7,4},{8,9},{9,10},{10,1... | collective-permute-start | bytes 405512 | tf_op jit(solution)/shard_map/ppermute | solution.py:603
  64.1 69.6 %copy-start.28 = (s32[2]{0:T(128)}, s32[2]{0:T(128)S(1)}, u32[]{:S(2)}) copy-start(s32[2]{0:T(128)S(1)} %pad_add_fusion.index_ref) | copy-start | bytes 28
  76.8 2.8 collective-permute-start.9
  76.8 3.3 collective-permute-start.10
  77.3 5.1 %collective-permute-start.11 = (f32[4,264,128]{2,1,0:T(8,128)S(1)}, f32[4,264,128]{2,1,0:T(8,128)S(1)}, u32[]{:S(2)}, u32[]{:S(2)}) collective-permute-start(f32[4,264,128]{2,1,0:T(8,128)S(1)} %collective-permute-done.4.refs_4_), channel_id=1, source_target_pairs={{0,4},{4,0},{8,12},{12,8},{16,20},{20,16},{24,28},{28,24},{1,5},{5... | collective-permute-start | bytes 1622024 | tf_op jit(solution)/shard_map/ppermute | solution.py:583
  77.3 5.8 %collective-permute-start.12 = (f32[4,264,128]{2,1,0:T(8,128)S(1)}, f32[4,264,128]{2,1,0:T(8,128)S(1)}, u32[]{:S(2)}, u32[]{:S(2)}) collective-permute-start(f32[4,264,128]{2,1,0:T(8,128)S(1)} %collective-permute-done.5.refs_6_), channel_id=1, source_target_pairs={{0,4},{4,0},{8,12},{12,8},{16,20},{20,16},{24,28},{28,24},{1,5},{5... | collective-permute-start | bytes 1622024 | tf_op jit(solution)/shard_map/ppermute | solution.py:583
  77.9 66.1 %copy-start.31 = (s32[8]{0:T(128)}, s32[8]{0:T(128)S(1)}, u32[]{:S(2)}) copy-start(s32[8]{0:T(128)S(1)} %get-tuple-element.199.block_count) | copy-start | bytes 100
  77.9 66.1 %copy-start.32 = (s32[8]{0:T(128)}, s32[8]{0:T(128)S(1)}, u32[]{:S(2)}) copy-start(s32[8]{0:T(128)S(1)} %get-tuple-element.200.block_low) | copy-start | bytes 100
  77.9 28.9 %collective-permute-start.15 = (f32[1024,128]{1,0:T(8,128)S(1)}, f32[1024,128]{1,0:T(8,128)}, u32[]{:S(2)}, u32[]{:S(2)}) collective-permute-start(f32[1024,128]{1,0:T(8,128)S(1)} %copy-done.46), channel_id=1, source_target_pairs={{0,3},{1,0},{2,1},{3,2},{4,7},{5,4},{6,5},{7,6},{8,11},{9,8},{10,9... | collective-permute-start | bytes 1572872 | tf_op jit(solution)/shard_map/ppermute | solution.py:603
  79.5 44.4 %collective-permute-start.14 = (f32[1024,128]{1,0:T(8,128)S(1)}, f32[1024,128]{1,0:T(8,128)}, u32[]{:S(2)}, u32[]{:S(2)}) collective-permute-start(f32[1024,128]{1,0:T(8,128)S(1)} %copy-done.46), channel_id=1, source_target_pairs={{0,2},{1,3},{2,0},{3,1},{4,6},{5,7},{6,4},{7,5},{8,10},{9,11},{10,... | collective-permute-start | bytes 1572872 | tf_op jit(solution)/shard_map/ppermute | solution.py:603
  80.1 43.9 %collective-permute-start.18 = (f32[4,264,128]{2,1,0:T(8,128)S(1)}, f32[4,264,128]{2,1,0:T(8,128)S(1)}, u32[]{:S(2)}, u32[]{:S(2)}) collective-permute-start(f32[4,264,128]{2,1,0:T(8,128)S(1)} %pad_maximum_fusion.2.refs_0_), channel_id=1, source_target_pairs={{0,24},{4,28},{8,16},{12,20},{16,8},{20,12},{24,0},{28,4},{1,25},{... | collective-permute-start | bytes 1622024 | tf_op jit(solution)/shard_map/ppermute | solution.py:583
  82.3 41.6 %collective-permute-start.17 = (f32[4,264,128]{2,1,0:T(8,128)S(1)}, f32[4,264,128]{2,1,0:T(8,128)S(1)}, u32[]{:S(2)}, u32[]{:S(2)}) collective-permute-start(f32[4,264,128]{2,1,0:T(8,128)S(1)} %pad_maximum_fusion.2.refs_0_), channel_id=1, source_target_pairs={{0,16},{4,20},{8,24},{12,28},{16,0},{20,4},{24,8},{28,12},{1,17},{... | collective-permute-start | bytes 1622024 | tf_op jit(solution)/shard_map/ppermute | solution.py:583
  83.0 40.9 %collective-permute-start.16 = (f32[4,264,128]{2,1,0:T(8,128)S(1)}, f32[4,264,128]{2,1,0:T(8,128)S(1)}, u32[]{:S(2)}, u32[]{:S(2)}) collective-permute-start(f32[4,264,128]{2,1,0:T(8,128)S(1)} %pad_maximum_fusion.2.refs_0_), channel_id=1, source_target_pairs={{0,8},{4,12},{8,0},{12,4},{16,24},{20,28},{24,16},{28,20},{1,9},{5... | collective-permute-start | bytes 1622024 | tf_op jit(solution)/shard_map/ppermute | solution.py:583
  85.3 39.8 %copy-start = (f32[4,512,512]{2,1,0:T(8,128)}, f32[4,512,512]{2,1,0:T(8,128)S(1)}, u32[]{:S(2)}) copy-start(f32[4,512,512]{2,1,0:T(8,128)S(1)} %get-tuple-element.119.w_ref) | copy-start | bytes 12582916
  85.3 48.4 %copy-start.33 = (f32[4,8,512]{2,1,0:T(8,128)}, f32[4,8,512]{2,1,0:T(8,128)S(1)}, u32[]{:S(2)}) copy-start(f32[4,8,512]{2,1,0:T(8,128)S(1)} %get-tuple-element.128.all_vec_ref.vec_ref) | copy-start | bytes 196612
  124.0 9.7 %collective-permute-start.19 = (f32[4,264,128]{2,1,0:T(8,128)S(1)}, f32[4,264,128]{2,1,0:T(8,128)S(1)}, u32[]{:S(2)}, u32[]{:S(2)}) collective-permute-start(f32[4,264,128]{2,1,0:T(8,128)S(1)} %pad_maximum_fusion.2.refs_0_), channel_id=1, source_target_pairs={{0,4},{4,0},{8,12},{12,8},{16,20},{20,16},{24,28},{28,24},{1,5},{5... | collective-permute-start | bytes 1622024 | tf_op jit(solution)/shard_map/ppermute | solution.py:583
  124.0 9.7 %collective-permute-start.20 = (f32[4,264,128]{2,1,0:T(8,128)S(1)}, f32[4,264,128]{2,1,0:T(8,128)S(1)}, u32[]{:S(2)}, u32[]{:S(2)}) collective-permute-start(f32[4,264,128]{2,1,0:T(8,128)S(1)} %collective-permute-done.16.refs_2_), channel_id=1, source_target_pairs={{0,4},{4,0},{8,12},{12,8},{16,20},{20,16},{24,28},{28,24},{1,5},{5... | collective-permute-start | bytes 1622024 | tf_op jit(solution)/shard_map/ppermute | solution.py:583
  124.5 9.2 %collective-permute-start.21 = (f32[4,264,128]{2,1,0:T(8,128)S(1)}, f32[4,264,128]{2,1,0:T(8,128)S(1)}, u32[]{:S(2)}, u32[]{:S(2)}) collective-permute-start(f32[4,264,128]{2,1,0:T(8,128)S(1)} %collective-permute-done.17.refs_4_), channel_id=1, source_target_pairs={{0,4},{4,0},{8,12},{12,8},{16,20},{20,16},{24,28},{28,24},{1,5},{5... | collective-permute-start | bytes 1622024 | tf_op jit(solution)/shard_map/ppermute | solution.py:583
  124.6 9.1 %collective-permute-start.22 = (f32[4,264,128]{2,1,0:T(8,128)S(1)}, f32[4,264,128]{2,1,0:T(8,128)S(1)}, u32[]{:S(2)}, u32[]{:S(2)}) collective-permute-start(f32[4,264,128]{2,1,0:T(8,128)S(1)} %collective-permute-done.18.refs_6_), channel_id=1, source_target_pairs={{0,4},{4,0},{8,12},{12,8},{16,20},{20,16},{24,28},{28,24},{1,5},{5... | collective-permute-start | bytes 1622024 | tf_op jit(solution)/shard_map/ppermute | solution.py:583
  267.0 38.6 %copy-start.52 = (f32[4,72,512]{2,1,0:T(8,128)S(1)}, f32[4,72,512]{2,1,0:T(8,128)}, u32[]{:S(2)}) copy-start(f32[4,72,512]{2,1,0:T(8,128)} %get-tuple-element.156) | copy-start | bytes 1769476
  305.5 2.2 collective-permute-start.23
  305.6 3.9 %collective-permute-start.27 = (f32[4,72,512]{2,1,0:T(8,128)S(1)}, f32[4,72,512]{2,1,0:T(8,128)S(1)}, u32[]{:S(2)}, u32[]{:S(2)}) collective-permute-start(f32[4,72,512]{2,1,0:T(8,128)S(1)} %copy-done.52), channel_id=1, source_target_pairs={{0,4},{4,0},{8,12},{12,8},{16,20},{20,16},{24,28},{28,24},{1,5},{5... | collective-permute-start | bytes 1769480 | tf_op jit(solution)/shard_map/ppermute | solution.py:583
  308.9 7.4 %collective-permute-start.26 = (f32[64,512]{1,0:T(8,128)S(1)}, f32[64,512]{1,0:T(8,128)S(1)}, u32[]{:S(2)}, u32[]{:S(2)}) collective-permute-start(f32[64,512]{1,0:T(8,128)S(1)} %get-tuple-element.209), channel_id=1, source_target_pairs={{0,24},{4,28},{8,16},{12,20},{16,8},{20,12},{24,0},{28,4},{1,25},{... | collective-permute-start | bytes 393224 | tf_op jit(solution)/shard_map/ppermute | solution.py:583
  309.5 32.1 %copy-start.17 = (f32[6,64,128]{2,1,0:T(8,128)S(1)}, f32[6,64,128]{2,1,0:T(8,128)}, u32[]{:S(2)}) copy-start(f32[6,64,128]{2,1,0:T(8,128)} %refs_16_.1) | copy-start | bytes 589828
  309.5 32.1 %copy-start.18 = (f32[64,512]{1,0:T(8,128)S(1)}, f32[64,512]{1,0:T(8,128)}, u32[]{:S(2)}) copy-start(f32[64,512]{1,0:T(8,128)} %refs_12_.1) | copy-start | bytes 393220
  309.6 32.1 %copy-start.19 = (f32[512,64]{0,1:T(8,128)S(1)}, f32[512,64]{0,1:T(8,128)}, u32[]{:S(2)}) copy-start(f32[512,64]{0,1:T(8,128)} %param.44) | copy-start | bytes 393220
  309.6 32.1 %copy-start.20 = (f32[64,512]{1,0:T(8,128)S(1)}, f32[64,512]{1,0:T(8,128)}, u32[]{:S(2)}) copy-start(f32[64,512]{1,0:T(8,128)} %refs_18_.1) | copy-start | bytes 393220
  309.6 32.1 %copy-start.21 = (f32[512,64]{0,1:T(8,128)S(1)}, f32[512,64]{0,1:T(8,128)}, u32[]{:S(2)}) copy-start(f32[512,64]{0,1:T(8,128)} %param.45) | copy-start | bytes 393220
  309.6 32.1 %copy-start.23 = (f32[2,128,64]{1,2,0:T(8,128)S(1)}, f32[2,128,64]{1,2,0:T(8,128)}, u32[]{:S(2)}) copy-start(f32[2,128,64]{1,2,0:T(8,128)} %param.40) | copy-start | bytes 196612
  309.8 14.7 %collective-permute-start.30 = (f32[72,512]{1,0:T(8,128)S(1)}, f32[72,512]{1,0:T(8,128)S(1)}, u32[]{:S(2)}, u32[]{:S(2)}) collective-permute-start(f32[72,512]{1,0:T(8,128)S(1)} %get-tuple-element.205), channel_id=1, source_target_pairs={{0,24},{4,28},{8,16},{12,20},{16,8},{20,12},{24,0},{28,4},{1,25},{... | collective-permute-start | bytes 442376 | tf_op jit(solution)/shard_map/ppermute | solution.py:583
  312.2 12.3 %collective-permute-start.29 = (f32[72,512]{1,0:T(8,128)S(1)}, f32[72,512]{1,0:T(8,128)S(1)}, u32[]{:S(2)}, u32[]{:S(2)}) collective-permute-start(f32[72,512]{1,0:T(8,128)S(1)} %get-tuple-element.206), channel_id=1, source_target_pairs={{0,16},{4,20},{8,24},{12,28},{16,0},{20,4},{24,8},{28,12},{1,17},{... | collective-permute-start | bytes 442376 | tf_op jit(solution)/shard_map/ppermute | solution.py:583
  312.6 11.9 %collective-permute-start.28 = (f32[72,512]{1,0:T(8,128)S(1)}, f32[72,512]{1,0:T(8,128)S(1)}, u32[]{:S(2)}, u32[]{:S(2)}) collective-permute-start(f32[72,512]{1,0:T(8,128)S(1)} %get-tuple-element.207), channel_id=1, source_target_pairs={{0,8},{4,12},{8,0},{12,4},{16,24},{20,28},{24,16},{28,20},{1,9},{5... | collective-permute-start | bytes 442376 | tf_op jit(solution)/shard_map/ppermute | solution.py:583
  313.4 11.1 %collective-permute-start.25 = (f32[64,512]{1,0:T(8,128)S(1)}, f32[64,512]{1,0:T(8,128)S(1)}, u32[]{:S(2)}, u32[]{:S(2)}) collective-permute-start(f32[64,512]{1,0:T(8,128)S(1)} %get-tuple-element.210), channel_id=1, source_target_pairs={{0,16},{4,20},{8,24},{12,28},{16,0},{20,4},{24,8},{28,12},{1,17},{... | collective-permute-start | bytes 393224 | tf_op jit(solution)/shard_map/ppermute | solution.py:583
  316.3 8.2 %collective-permute-start.24 = (f32[64,512]{1,0:T(8,128)S(1)}, f32[64,512]{1,0:T(8,128)S(1)}, u32[]{:S(2)}, u32[]{:S(2)}) collective-permute-start(f32[64,512]{1,0:T(8,128)S(1)} %get-tuple-element.211), channel_id=1, source_target_pairs={{0,8},{4,12},{8,0},{12,4},{16,24},{20,28},{24,16},{28,20},{1,9},{5... | collective-permute-start | bytes 393224 | tf_op jit(solution)/shard_map/ppermute | solution.py:583
  325.8 1.2 collective-permute-start.31
  327.0 4.4 %collective-permute-start.34 = (f32[1,128]{1,0:T(1,128)S(1)}, f32[1,128]{1,0:T(1,128)S(1)}, u32[]{:S(2)}, u32[]{:S(2)}) collective-permute-start(f32[1,128]{1,0:T(1,128)S(1)} %add.137), channel_id=1, source_target_pairs={{0,24},{4,28},{8,16},{12,20},{16,8},{20,12},{24,0},{28,4},{1,25},{... | collective-permute-start | bytes 1544 | tf_op jit(solution)/shard_map/ppermute | solution.py:583
  327.9 3.5 collective-permute-start.33
  329.4 3.5 collective-permute-start.32
  332.9 5.8 %collective-permute-start.37 = (f32[1,128]{1,0:T(1,128)S(1)}, f32[1,128]{1,0:T(1,128)S(1)}, u32[]{:S(2)}, u32[]{:S(2)}) collective-permute-start(f32[1,128]{1,0:T(1,128)S(1)} %add_add_fusion.4), channel_id=1, source_target_pairs={{0,3},{1,2},{2,1},{3,0},{4,7},{5,6},{6,5},{7,4},{8,11},{9,10},{10,... | collective-permute-start | bytes 1544 | tf_op jit(solution)/shard_map/ppermute | solution.py:583
  337.2 4.4 %collective-permute-start.36 = (f32[1,128]{1,0:T(1,128)S(1)}, f32[1,128]{1,0:T(1,128)S(1)}, u32[]{:S(2)}, u32[]{:S(2)}) collective-permute-start(f32[1,128]{1,0:T(1,128)S(1)} %add_add_fusion.4), channel_id=1, source_target_pairs={{0,2},{1,3},{2,0},{3,1},{4,6},{5,7},{6,4},{7,5},{8,10},{9,11},{10,... | collective-permute-start | bytes 1544 | tf_op jit(solution)/shard_map/ppermute | solution.py:583
  337.2 4.4 %collective-permute-start.35 = (f32[1,128]{1,0:T(1,128)S(1)}, f32[1,128]{1,0:T(1,128)S(1)}, u32[]{:S(2)}, u32[]{:S(2)}) collective-permute-start(f32[1,128]{1,0:T(1,128)S(1)} %add_add_fusion.4), channel_id=1, source_target_pairs={{0,1},{1,0},{2,3},{3,2},{4,5},{5,4},{6,7},{7,6},{8,9},{9,8},{10,11... | collective-permute-start | bytes 1544 | tf_op jit(solution)/shard_map/ppermute | solution.py:583
  343.3 8.2 %collective-permute-start.38 = (f32[1,128]{1,0:T(1,128)S(1)}, f32[1,128]{1,0:T(1,128)S(1)}, u32[]{:S(2)}, u32[]{:S(2)}) collective-permute-start(f32[1,128]{1,0:T(1,128)S(1)} %get-tuple-element.162), channel_id=1, source_target_pairs={{0,4},{4,0},{8,12},{12,8},{16,20},{20,16},{24,28},{28,24},{1,5},{5... | collective-permute-start | bytes 1544 | tf_op jit(solution)/shard_map/ppermute | solution.py:583
  347.7 25.5 %all-to-all-start.1 = ((f32[8,176,128]{2,1,0:T(8,128)}), f32[8,176,128]{2,1,0:T(8,128)S(1)}, u32[]{:S(2)}, u32[]{:S(2)}) async-start(f32[8,176,128]{2,1,0:T(8,128)} %bitcast.45), calls=%async_computation.1 | async-start | bytes 1441792 | tf_op jit(solution)/shard_map/all_to_all | solution.py:1136
  351.5 11.9 %collective-permute-start.41 = (f32[1,128]{1,0:T(1,128)S(1)}, f32[1,128]{1,0:T(1,128)S(1)}, u32[]{:S(2)}, u32[]{:S(2)}) collective-permute-start(f32[1,128]{1,0:T(1,128)S(1)} %add.144), channel_id=1, source_target_pairs={{0,24},{4,28},{8,16},{12,20},{16,8},{20,12},{24,0},{28,4},{1,25},{... | collective-permute-start | bytes 1544 | tf_op jit(solution)/shard_map/ppermute | solution.py:583
  354.5 8.9 %collective-permute-start.40 = (f32[1,128]{1,0:T(1,128)S(1)}, f32[1,128]{1,0:T(1,128)S(1)}, u32[]{:S(2)}, u32[]{:S(2)}) collective-permute-start(f32[1,128]{1,0:T(1,128)S(1)} %add.144), channel_id=1, source_target_pairs={{0,16},{4,20},{8,24},{12,28},{16,0},{20,4},{24,8},{28,12},{1,17},{... | collective-permute-start | bytes 1544 | tf_op jit(solution)/shard_map/ppermute | solution.py:583
  355.0 8.4 %collective-permute-start.39 = (f32[1,128]{1,0:T(1,128)S(1)}, f32[1,128]{1,0:T(1,128)S(1)}, u32[]{:S(2)}, u32[]{:S(2)}) collective-permute-start(f32[1,128]{1,0:T(1,128)S(1)} %add.144), channel_id=1, source_target_pairs={{0,8},{4,12},{8,0},{12,4},{16,24},{20,28},{24,16},{28,20},{1,9},{5... | collective-permute-start | bytes 1544 | tf_op jit(solution)/shard_map/ppermute | solution.py:583
  363.4 12.7 %collective-permute-start.44 = (f32[1,128]{1,0:T(1,128)S(1)}, f32[1,128]{1,0:T(1,128)S(1)}, u32[]{:S(2)}, u32[]{:S(2)}) collective-permute-start(f32[1,128]{1,0:T(1,128)S(1)} %add_add_fusion.2), channel_id=1, source_target_pairs={{0,3},{1,2},{2,1},{3,0},{4,7},{5,6},{6,5},{7,4},{8,11},{9,10},{10,... | collective-permute-start | bytes 1544 | tf_op jit(solution)/shard_map/ppermute | solution.py:583
  364.9 11.2 %collective-permute-start.43 = (f32[1,128]{1,0:T(1,128)S(1)}, f32[1,128]{1,0:T(1,128)S(1)}, u32[]{:S(2)}, u32[]{:S(2)}) collective-permute-start(f32[1,128]{1,0:T(1,128)S(1)} %add_add_fusion.2), channel_id=1, source_target_pairs={{0,2},{1,3},{2,0},{3,1},{4,6},{5,7},{6,4},{7,5},{8,10},{9,11},{10,... | collective-permute-start | bytes 1544 | tf_op jit(solution)/shard_map/ppermute | solution.py:583
  365.6 10.5 %collective-permute-start.42 = (f32[1,128]{1,0:T(1,128)S(1)}, f32[1,128]{1,0:T(1,128)S(1)}, u32[]{:S(2)}, u32[]{:S(2)}) collective-permute-start(f32[1,128]{1,0:T(1,128)S(1)} %add_add_fusion.2), channel_id=1, source_target_pairs={{0,1},{1,0},{2,3},{3,2},{4,5},{5,4},{6,7},{7,6},{8,9},{9,8},{10,11... | collective-permute-start | bytes 1544 | tf_op jit(solution)/shard_map/ppermute | solution.py:583
  (38 other events, 552.2 us)
Sparse Core Ops, SparseCore 0:
  48.5 106.9 all-gather.2
  215.7 42.5 reduce-scatter.1

commit v3 on v2

--- a/solution.py
+++ b/solution.py
@@ -105,25 +105,32 @@
     return wide[:, :pair_lanes] + wide[:, pair_lanes:] + dot(left_pair[1], right_both[:, :pair_lanes])
 
 
-def prepare(source_ref, low_half, pack_ref, both_ref):
-    rows, width = source_ref.shape
-
+def prepare_rows(at, source_ref, low_half, pack_ref, both_ref):
+    for pair in range(source_ref.shape[1] // pair_lanes):
+        tile = source_ref[at, pair * pair_lanes : (pair + 1) * pair_lanes]
+        if pack_ref is not None:
+            first, second = key_packs(tile, low_half)
+            pack_ref[2 * pair, at, :] = first
+            pack_ref[2 * pair + 1, at, :] = second
+        if both_ref is not None:
+            both_ref[pair, at, :] = both_parts(tile)
+
+
+def clear_pad(rows, *refs):
+    for ref in refs:
+        ref[:, rows:, :] = jnp.zeros((ref.shape[0], ref.shape[1] - rows, ref.shape[2]), bf16)
+
+
+def half_mask(rows):
+    return lax.broadcasted_iota(jnp.int32, (rows, pair_lanes), 1) < pair_lanes // 2
+
+
+def chunks(rows, size, body):
     def one(step, carry):
-        at = pl.ds(pl.multiple_of(step * q_rows, q_rows), q_rows)
-        for pair in range(width // pair_lanes):
-            tile = source_ref[at, pair * pair_lanes : (pair + 1) * pair_lanes]
-            if pack_ref is not None:
-                first, second = key_packs(tile, low_half)
-                pack_ref[2 * pair, at, :] = first
-                pack_ref[2 * pair + 1, at, :] = second
-            if both_ref is not None:
-                both_ref[pair, at, :] = both_parts(tile)
+        body(pl.ds(pl.multiple_of(step * size, size), size))
         return carry
 
-    lax.fori_loop(0, rows // q_rows, one, 0)
-    for ref in (pack_ref, both_ref):
-        if ref is not None:
-            ref[:, rows:, :] = jnp.zeros((ref.shape[0], ref.shape[1] - rows, ref.shape[2]), bf16)
+    lax.fori_loop(0, rows // size, one, 0)
 
 
 def attend_kernel(
@@ -135,8 +142,13 @@
     rows, width = q_ref.shape
     lanes = lax.broadcasted_iota(jnp.int32, (q_rows, pair_lanes), 1)
     low_half = lanes < pair_lanes // 2
-    prepare(k_ref, low_half, kp_ref, None)
-    prepare(v_ref, low_half, None, vb_ref)
+    clear_pad(rows, kp_ref, vb_ref)
+
+    def before(at):
+        prepare_rows(at, k_ref, low_half, kp_ref, None)
+        prepare_rows(at, v_ref, low_half, None, vb_ref)
+
+    chunks(rows, q_rows, before)
     groups = width // pair_lanes // unroll
     key_iota = lax.broadcasted_iota(jnp.int32, (q_rows, key_rows), 1)
 
@@ -146,24 +158,25 @@
         last = high_ref[at, :]
         for group in range(groups):
             pairs = [group * unroll + u for u in range(unroll)]
-            queries = [
-                query_packs(q_ref[at, p * pair_lanes : (p + 1) * pair_lanes] * scale, low_half)
-                for p in pairs
-            ]
-
-            def chunk(step, state):
+
+            def load(u):
+                lanes_of = slice(pairs[u] * pair_lanes, (pairs[u] + 1) * pair_lanes)
+                return query_packs(q_ref[at, lanes_of] * scale, low_half)
+
+            def chunk(step, state, held_packs=None):
                 start = pl.multiple_of(block_low[index] + step * key_rows, 16)
                 here = pl.ds(start, key_rows)
                 places = key_iota + start
                 bias = jnp.where(jnp.logical_and(places >= first, places < last), 0.0, neg_large)
                 bias = jnp.concatenate([bias, bias], axis=0)
-                out = []
-                found = [
-                    jnp.concatenate(
-                        [dot_nt(queries[u][h], kp_ref[2 * p + h, here, :]) for h in range(2)], axis=0
+                out, found = [], []
+                for u, p in enumerate(pairs):
+                    query = load(u) if held_packs is None else held_packs[u]
+                    found.append(
+                        jnp.concatenate(
+                            [dot_nt(query[h], kp_ref[2 * p + h, here, :]) for h in range(2)], axis=0
+                        )
                     )
-                    for u, p in enumerate(pairs)
-                ]
                 for u, p in enumerate(pairs):
                     scores = bias + found[u]
                     new_top = jnp.max(scores, axis=1, keepdims=True)
@@ -204,7 +217,9 @@
                     )
                     for _ in range(unroll)
                 )
-                finish(lax.fori_loop(0, block_count[index], chunk, start_state))
+                packs = [load(u) for u in range(unroll)]
+                step = lambda number, state: chunk(number, state, packs)
+                finish(lax.fori_loop(0, block_count[index], step, start_state))
 
         return carry
 
@@ -229,57 +244,53 @@
         total_tile = total_ref[at, :]
         for group in range(groups):
             pairs = [group * unroll + u for u in range(unroll)]
-            queries, query_both, grads, grad_both, logs, dots = [], [], [], [], [], []
-            for p in pairs:
+
+            def column(mask, value):
+                return jnp.sum(jnp.where(mask, value, 0.0), axis=1, keepdims=True)
+
+            def load(u):
+                p = pairs[u]
                 lanes_of = slice(p * pair_lanes, (p + 1) * pair_lanes)
-                tile = q_ref[at, lanes_of] * scale
-                queries.append(query_packs(tile, low_half))
-                query_both.append(both_parts(stack_heads(tile, low_half)))
-                tile = g_ref[at, lanes_of]
-                grads.append(query_packs(tile, low_half))
-                grad_both.append(both_parts(stack_heads(tile, low_half)))
-                product = tile * o_ref[at, lanes_of]
-                column = lambda mask, value: jnp.sum(jnp.where(mask, value, 0.0), axis=1, keepdims=True)
-                dots.append(
-                    jnp.concatenate(
-                        [column(low_half, product), column(jnp.logical_not(low_half), product)], axis=0
-                    )
+                query = q_ref[at, lanes_of] * scale
+                grad = g_ref[at, lanes_of]
+                product = grad * o_ref[at, lanes_of]
+                dots = [column(low_half, product), column(jnp.logical_not(low_half), product)]
+                logs = [column(lanes == 2 * p, total_tile), column(lanes == 2 * p + 1, total_tile)]
+                return (
+                    query_packs(query, low_half),
+                    query_packs(grad, low_half),
+                    both_parts(stack_heads(query, low_half)),
+                    both_parts(stack_heads(grad, low_half)),
+                    jnp.concatenate(logs, axis=0),
+                    jnp.concatenate(dots, axis=0),
                 )
-                logs.append(
-                    jnp.concatenate(
-                        [column(lanes == 2 * p, total_tile), column(lanes == 2 * p + 1, total_tile)], axis=0
-                    )
-                )
-
-            def chunk(step, state):
+
+            def chunk(step, state, held_packs=None):
                 start = pl.multiple_of(block_low[index] + step * key_rows, 16)
                 here = pl.ds(start, key_rows)
                 places = key_iota + start
                 bias = jnp.where(jnp.logical_and(places >= first, places < last), 0.0, neg_large)
                 bias = jnp.concatenate([bias, bias], axis=0)
-                out = []
-                found = [
-                    jnp.concatenate(
-                        [dot_nt(queries[u][h], kp_ref[2 * p + h, here, :]) for h in range(2)], axis=0
+                out, packs, found = [], [], []
+                for u, p in enumerate(pairs):
+                    packs.append(load(u) if held_packs is None else held_packs[u])
+                    found.append(
+                        [
+                            jnp.concatenate(
+                                [dot_nt(packs[u][k][h], ref[2 * p + h, here, :]) for h in range(2)], axis=0
+                            )
+                            for k, ref in enumerate((kp_ref, vp_ref))
+                        ]
                     )
-                    for u, p in enumerate(pairs)
-                ]
-                found_grad = [
-                    jnp.concatenate(
-                        [dot_nt(grads[u][h], vp_ref[2 * p + h, here, :]) for h in range(2)], axis=0
-                    )
-                    for u, p in enumerate(pairs)
-                ]
                 for u, p in enumerate(pairs):
                     lanes_of = slice(p * pair_lanes, (p + 1) * pair_lanes)
-                    scores = bias + found[u]
-                    weights = jnp.exp(scores - logs[u])
-                    grad_weights = found_grad[u]
-                    grad_scores = split_two(weights * (grad_weights - dots[u]))
+                    _, _, query_both, grad_both, logs, dots = packs[u]
+                    weights = jnp.exp(bias + found[u][0] - logs)
+                    grad_scores = split_two(weights * (found[u][1] - dots))
                     new_state = folded(dot_nn, grad_scores, kb_ref[p, here, :])
                     out.append(new_state if state is None else state[u] + new_state)
-                    dk_sum[here, lanes_of] += folded(dot_tn, grad_scores, query_both[u])
-                    dv_sum[here, lanes_of] += folded(dot_tn, split_two(weights), grad_both[u])
+                    dk_sum[here, lanes_of] += folded(dot_tn, grad_scores, query_both)
+                    dv_sum[here, lanes_of] += folded(dot_tn, split_two(weights), grad_both)
                 return tuple(out)
 
             def finish(state):
@@ -293,7 +304,9 @@
             @pl.when(block_count[index] > 1)
             def _():
                 start_state = tuple(jnp.zeros((2 * q_rows, pair_lanes), f32) for _ in range(unroll))
-                finish(lax.fori_loop(0, block_count[index], chunk, start_state))
+                packs = [load(u) for u in range(unroll)]
+                step = lambda number, state: chunk(number, state, packs)
+                finish(lax.fori_loop(0, block_count[index], step, start_state))
 
         return carry
 
@@ -326,10 +339,6 @@
 
 def column_sum(value):
     return jnp.sum(value, axis=0, keepdims=True)
-
-
-def chunks(rows, size, body):
-    lax.fori_loop(0, rows // size, lambda step, carry: (body(pl.ds(pl.multiple_of(step * size, size), size)), carry)[1], 0)
 
 
 def hand_out(index_ref, grads_ref, keep_ref, send_ref, rows, extra_ref=None):
@@ -352,10 +361,8 @@
 ):
     rows, width = q_ref.shape
     model = index_ref[1]
-    lanes = lax.broadcasted_iota(jnp.int32, (q_rows, pair_lanes), 1)
-    low_half = lanes < pair_lanes // 2
-    prepare(k_ref, low_half, kp_ref, kb_ref)
-    prepare(v_ref, low_half, vp_ref, None)
+    mask = half_mask(256)
+    clear_pad(rows, kp_ref, vp_ref, kb_ref)
     dk_sum[...] = jnp.zeros_like(dk_sum)
     dv_sum[...] = jnp.zeros_like(dv_sum)
     woh[...], wol[...] = split_two(w_ref[3])
@@ -371,6 +378,8 @@
         totals[4:5, :] += column_sum(grad)
         two_grad_ref[at, :] = resid
         go_ref[at, :] = three(dot_nn, split_two(resid), (woh[...], wol[...]))
+        prepare_rows(at, k_ref, mask, kp_ref, kb_ref)
+        prepare_rows(at, v_ref, mask, vp_ref, None)
 
     chunks(rows, 256, before)
     attend_back_blocks(
@@ -392,12 +401,8 @@
         dk = dk_sum[at, :]
         dv = dv_sum[at, :]
         grads[:, :columns] += three(dot_tn, source, split_two(own_lanes(dq_ref, at, model, columns)))
-        grads[:, columns : 2 * columns] += three(
-            dot_tn, memory, split_two(own_lanes(dk_sum, at, model, columns))
-        )
-        grads[:, 2 * columns : 3 * columns] += three(
-            dot_tn, memory, split_two(own_lanes(dv_sum, at, model, columns))
-        )
+        both = jnp.concatenate([own_lanes(ref, at, model, columns) for ref in (dk_sum, dv_sum)], axis=1)
+        grads[:, columns : 3 * columns] += three(dot_tn, memory, split_two(both))
         grads[:, 3 * columns :] += three(
             dot_tn, split_two(resid), split_two(own_lanes(o_ref, at, model, columns))
         )
@@ -422,10 +427,8 @@
 ):
     rows, width = q_ref.shape
     model = index_ref[1]
-    lanes = lax.broadcasted_iota(jnp.int32, (q_rows, pair_lanes), 1)
-    low_half = lanes < pair_lanes // 2
-    prepare(k_ref, low_half, kp_ref, kb_ref)
-    prepare(v_ref, low_half, vp_ref, None)
+    mask = half_mask(256)
+    clear_pad(rows, kp_ref, vp_ref, kb_ref)
     dk_sum[...] = jnp.zeros_like(dk_sum)
     dv_sum[...] = jnp.zeros_like(dv_sum)
     woh[...], wol[...] = split_two(w_ref[3])
@@ -433,6 +436,8 @@
 
     def before(at):
         go_ref[at, :] = three(dot_nn, split_two(g_ref[at, :]), (woh[...], wol[...]))
+        prepare_rows(at, k_ref, mask, kp_ref, kb_ref)
+        prepare_rows(at, v_ref, mask, vp_ref, None)
 
     chunks(rows, 256, before)
     attend_back_blocks(
@@ -445,10 +450,8 @@
         source = split_two(x_ref[at, :])
         dk_ref[at, :] = dk_sum[at, :]
         dv_ref[at, :] = dv_sum[at, :]
-        for number, ref in enumerate((dq_ref, dk_sum, dv_sum)):
-            grads[:, number * columns : (number + 1) * columns] += three(
-                dot_tn, source, split_two(own_lanes(ref, at, model, columns))
-            )
+        every = [own_lanes(ref, at, model, columns) for ref in (dq_ref, dk_sum, dv_sum)]
+        grads[:, : 3 * columns] += three(dot_tn, source, split_two(jnp.concatenate(every, axis=1)))
         grads[:, 3 * columns :] += three(
             dot_tn, split_two(g_ref[at, :]), split_two(own_lanes(o_ref, at, model, columns))
         )
@@ -678,7 +681,7 @@
 def wide_kernel(
     rows, model_ref, z_ref, g_ref, wide_ref, all_vec_ref,
     out_ref, second_ref, grads_ref, sums_ref, bias_grad_ref,
-    eh_ref, el_ref, rh_ref, rl_ref, slope_ref, xh_ref, xl_ref,
+    eh_ref, el_ref, rh_ref, rl_ref, slope_ref, xh_ref, xl_ref, bh_ref, bl_ref,
 ):
     tokens, width = z_ref.shape
     data, models, _, units = wide_ref.shape
@@ -699,46 +702,75 @@
     bias_grad_ref[...] = jnp.zeros_like(bias_grad_ref)
     grads_ref[...] = jnp.zeros_like(grads_ref)
 
+    gain = vec_ref[2:3, :]
+    half = block // 2
+    halves = [slice(0, half), slice(half, block)]
+
     def chunk(step, carry):
-        at = pl.ds(pl.multiple_of(step * block, block), block)
-        source = z_ref[at, :]
-        source_pair = split_two(source)
-
-        def forward(part, reduced):
-            to = pl.ds(pl.multiple_of(part * units, units), units)
-            before = three(dot_nn, source_pair, (eh_ref[:, to], el_ref[:, to])) + all_vec_ref[part, 7:8, :units]
-            value, slope = gelu_both(before)
-            slope_ref[:, to] = slope
-            high, low = split_two(value)
-            xh_ref[:, to] = high
-            xl_ref[:, to] = low
-            return reduced + three(dot_nt, (high, low), (rh_ref[:, to], rl_ref[:, to]))
-
-        reduced = lax.fori_loop(0, models, forward, source + vec_ref[6:7, :])
-        normal, scale = norm_parts(reduced)
-        gain = vec_ref[2:3, :]
-        out_ref[at, :] = normal * gain + vec_ref[5:6, :]
-        grad = g_ref[at, :]
-        resid = norm_back(grad, normal, scale, gain)
-        sums_ref[2:3, :] += column_sum(grad * normal)
-        sums_ref[5:6, :] += column_sum(grad)
-        sums_ref[6:7, :] += column_sum(resid)
-        resid_pair = split_two(resid)
-
-        def backward(part, second):
-            to = pl.ds(pl.multiple_of(part * units, units), units)
-            back = three(dot_nn, resid_pair, (rh_ref[:, to], rl_ref[:, to])) * slope_ref[:, to]
-            back_pair = split_two(back)
-
-            @pl.when(part == model)
-            def _():
-                bias_grad_ref[...] += jnp.sum(back, axis=0, keepdims=True)
-                grads_ref[:, :units] += three(dot_tn, source_pair, back_pair)
-                grads_ref[:, units:] += three(dot_tn, resid_pair, (xh_ref[:, to], xl_ref[:, to]))
-
-            return second + three(dot_nt, back_pair, (eh_ref[:, to], el_ref[:, to]))
-
-        second_ref[at, :] = lax.fori_loop(0, models, backward, resid)
+        whole = pl.ds(pl.multiple_of(step * block, block), block)
+        ats = [pl.ds(pl.multiple_of(step * block + h * half, half), half) for h in range(2)]
+        products, resids, reduced = [None] * 2, [None] * 2, [None] * 2
+
+        def enter(h):
+            products[h] = three(dot_nn, split_two(z_ref[ats[h], :]), (eh_ref[...], el_ref[...]))
+
+        def bend(h):
+            for part in range(models):
+                to = slice(part * units, (part + 1) * units)
+                value, slope = gelu_both(products[h][:, to] + all_vec_ref[part, 7:8, :units])
+                slope_ref[halves[h], to] = slope
+                xh_ref[halves[h], to], xl_ref[halves[h], to] = split_two(value)
+
+        def leave(h):
+            reduced[h] = three(
+                dot_nt, (xh_ref[halves[h], :], xl_ref[halves[h], :]), (rh_ref[...], rl_ref[...])
+            )
+
+        def turn(h):
+            at = ats[h]
+            normal, scale = norm_parts(z_ref[at, :] + vec_ref[6:7, :] + reduced[h])
+            out_ref[at, :] = normal * gain + vec_ref[5:6, :]
+            grad = g_ref[at, :]
+            resids[h] = norm_back(grad, normal, scale, gain)
+            sums_ref[2:3, :] += column_sum(grad * normal)
+            sums_ref[5:6, :] += column_sum(grad)
+            sums_ref[6:7, :] += column_sum(resids[h])
+
+        def reenter(h):
+            products[h] = three(dot_nn, split_two(resids[h]), (rh_ref[...], rl_ref[...]))
+
+        def unbend(h):
+            for part in range(models):
+                to = slice(part * units, (part + 1) * units)
+                back = products[h][:, to] * slope_ref[halves[h], to]
+                slope_ref[halves[h], to] = back
+                bh_ref[halves[h], to], bl_ref[halves[h], to] = split_two(back)
+
+        def finish(h):
+            return three(dot_nt, (bh_ref[halves[h], :], bl_ref[halves[h], :]), (eh_ref[...], el_ref[...]))
+
+        enter(0)
+        enter(1)
+        bend(0)
+        leave(0)
+        bend(1)
+        leave(1)
+        turn(0)
+        reenter(0)
+        turn(1)
+        reenter(1)
+        unbend(0)
+        more = finish(0)
+        unbend(1)
+        last = finish(1)
+        second_ref[ats[0], :] = resids[0] + more
+        second_ref[ats[1], :] = resids[1] + last
+        to = pl.ds(pl.multiple_of(model * units, units), units)
+        bias_grad_ref[...] += column_sum(slope_ref[:, to])
+        grads_ref[:, :units] += three(dot_tn, split_two(z_ref[whole, :]), (bh_ref[:, to], bl_ref[:, to]))
+        grads_ref[:, units:] += three(
+            dot_tn, split_two(jnp.concatenate(resids, axis=0)), (xh_ref[:, to], xl_ref[:, to])
+        )
         return carry
 
     lax.fori_loop(0, tokens // block, chunk, 0)
@@ -762,9 +794,8 @@
         scratch_shapes=[pltpu.VMEM((width, models * units), bf16)] * 4
         + [
             pltpu.VMEM((block, models * units), f32),
-            pltpu.VMEM((block, models * units), bf16),
-            pltpu.VMEM((block, models * units), bf16),
-        ],
+        ]
+        + [pltpu.VMEM((block, models * units), bf16)] * 4,
         compiler_params=pltpu.CompilerParams(vmem_limit_bytes=60 << 20),
         cost_estimate=pl.CostEstimate(
             flops=27 * tokens * width * models * units, bytes_accessed=24 << 20, transcendentals=tokens * models * units
@@ -994,8 +1025,7 @@
     )(starts, returned)
 
 
-def cube_scatter(keep, send):
-    both = keep + flip(send, "dp", 1)
+def cube_scatter(both):
     return [both[0]] + [flip(both[r], "dp", 2 * r) for r in range(1, both.shape[0])]
 
 
@@ -1132,11 +1162,11 @@
         bias_rows,
     )
     placed = place_back(memory_grad_own, source_slots, data_count * slot_cap)
-    resid_one_grad, placed = together((resid_one_grad, placed))
+    resid_one_grad, placed, both = together((resid_one_grad, placed, keep + flip(send, "dp", 1)))
     returned = lax.all_to_all(
         placed.reshape(data_count, slot_cap, columns), "dp", split_axis=0, concat_axis=0, tiled=True
     )
-    grad_cross = cube_scatter(keep, send)
+    grad_cross = cube_scatter(both)
     keep, send, self_query_grad, self_key_grad, self_value_grad = self_back(
         index,
         self_ranges,
@@ -1152,7 +1182,8 @@
         columns,
         rows,
     )
-    grad_self = cube_scatter(keep, send)
+    keep, send, returned, grad_cross = together((keep, send, returned, grad_cross))
+    grad_self = cube_scatter(keep + flip(send, "dp", 1))
     memory_grad = return_rows(returned, my_starts, tok_rows)
     input_grad = (
         resid_one_grad
@@ -1188,7 +1219,7 @@
         grad_wide,
         *weights,
     )
-    row = small_total(row)
+    row, input_grad = together((small_total(row), input_grad))
     moved = whole_call(
         functools.partial(moments_kernel, model_count, columns),
         "moments",

time: 392 us -> 357 us (0.911)
  Pallas kernels: 184 us -> 156 us
  starting transfers between devices: 50.1 us -> 58.4 us
  waiting for transfers between devices: 78.8 us -> 72.4 us
  matrix products: 36.7 us -> 32.3 us
    pallas_call x1, Pallas kernels: 52.2 us -> 41.2 us  [feed_forward(): pl.pallas_call(functools.partial(wide_kernel, rows), out_shape=(jax.Shape...]
    all_to_all x1, starting transfers between devices: 3.84 us -> 11.8 us  [shards(): lax.all_to_all(placed.reshape(data_count, slot_cap, columns), 'dp', split...]
    pallas_call x1, Pallas kernels: 48.1 us -> 40.2 us  [cross_back(): pl.pallas_call(functools.partial(cross_back_kernel, unroll, head_size **...]
    ppermute x36, waiting for transfers between devices: 28.9 us -> 21.4 us  [flip(): return lax.ppermute(value, axis, pairs)]
    pallas_call x1, Pallas kernels: 38.5 us -> 33.5 us  [self_back(): pl.pallas_call(functools.partial(self_back_kernel, unroll, head_size ** (...]
    dot_general x11, matrix products: 36.7 us -> 32.3 us  [matmul(): jnp.dot(left_side, right_side, precision=lax.Precision.HIGH, preferred_el...]
    pallas_call x2, Pallas kernels: 28.1 us -> 23.9 us  [attend(): pl.pallas_call(functools.partial(attend_kernel, unroll, head_size ** (-0....]
  transfers between devices with their start and end apart: 49 -> 49, of which waited for: 19 -> 20; matrix products, arithmetic and copies ran while one was open for 13% -> 13% of each run, Pallas kernels for 33% -> 20%
where the time goes in v3:
time: 357 us; the launch traced here: 353 us
  Pallas kernels  156 us (44%)
  waiting for transfers between devices  72.4 us (20%)
  starting transfers between devices  58.4 us (16%)
  matrix products  32.3 us (9%)
  between operations  15.2 us (4%)
  other arithmetic  10.3 us (3%)
  local copies, waits for them, and re-layouts  8.38 us (2%)
    ppermute x9, waiting for transfers between devices, ring_gather(): lax.ppermute(own, 'mp', [(i, (i + step) % count) for i in range(count)])  43.9 us
    pallas_call x1, Pallas kernels, feed_forward(): pl.pallas_call(functools.partial(wide_kernel, rows), out_shape=(jax.Shape...  41.2 us
    pallas_call x1, Pallas kernels, cross_back(): pl.pallas_call(functools.partial(cross_back_kernel, unroll, head_size **...  40.2 us
    ppermute x36, starting transfers between devices, flip(): return lax.ppermute(value, axis, pairs)  33.5 us
    pallas_call x1, Pallas kernels, self_back(): pl.pallas_call(functools.partial(self_back_kernel, unroll, head_size ** (...  33.5 us
    dot_general x11, matrix products, matmul(): jnp.dot(left_side, right_side, precision=lax.Precision.HIGH, preferred_el...  32.3 us
    pallas_call x2, Pallas kernels, attend(): pl.pallas_call(functools.partial(attend_kernel, unroll, head_size ** (-0....  23.9 us
    ppermute x36, waiting for transfers between devices, flip(): return lax.ppermute(value, axis, pairs)  21.4 us
  transfers between devices with their start and end apart: 49, of which 20 were waited for; matrix products, arithmetic and copies ran while one was open for 13% of the time, Pallas kernels for 20%

profile of v3, /device:TPU:0, one launch (start us, length us, event | category | flops | bytes accessed | tf_op | source)
XLA Modules:
  0.0 352.8 jit_solution(10727626685667623482)
XLA Ops:
  8.2 1.2 bitcast_subtract_fusion.1.starts_ref
  9.4 2.0 pack_rows.1
  11.4 5.3 %all-to-all-start = ((f32[8,176,128]{2,1,0:T(8,128)}), f32[8,176,128]{2,1,0:T(8,128)S(1)}, u32[]{:S(2)}, u32[]{:S(2)}) async-start(f32[8,176,128]{2,1,0:T(8,128)} %pack_rows.1), calls=%async_computation | async-start | bytes 1441792 | tf_op jit(solution)/shard_map/all_to_all | solution.py:1078
  16.9 3.7 %collective-permute-start.2 = (f32[264,128]{1,0:T(8,128)S(1)}, f32[264,128]{1,0:T(8,128)S(1)}, u32[]{:S(2)}, u32[]{:S(2)}) collective-permute-start(f32[264,128]{1,0:T(8,128)S(1)} %get-tuple-element.120), channel_id=1, source_target_pairs={{0,3},{1,0},{2,1},{3,2},{4,7},{5,4},{6,5},{7,6},{8,11},{9,8},{10,9... | collective-permute-start | bytes 405512 | tf_op jit(solution)/shard_map/ppermute | solution.py:606
  20.6 1.0 collective-permute-start
  21.6 7.1 %all-to-all-done = f32[8,176,128]{2,1,0:T(8,128)S(1)} async-done(((f32[8,176,128]{2,1,0:T(8,128)}), f32[8,176,128]{2,1,0:T(8,128)S(1)}, u32[]{:S(2)}, u32[]{:S(2)}) %all-to-all-start) | async-done | bytes 720928 | tf_op jit(solution)/shard_map/all_to_all | solution.py:1078
  28.6 0.9 copy-done.42
  29.5 3.3 unpack_rows.1
  32.9 1.5 collective-permute-start.13
  35.2 13.2 %collective-permute-done.13 = f32[1024,128]{1,0:T(8,128)S(1)} collective-permute-done((f32[1024,128]{1,0:T(8,128)}, f32[1024,128]{1,0:T(8,128)S(1)}, u32[]{:S(2)}, u32[]{:S(2)}) %collective-permute-start.13) | collective-permute-done | bytes 524320 | tf_op jit(solution)/shard_map/ppermute | solution.py:606
  49.2 2.5 collective-permute-start.5
  53.8 6.3 %collective-permute-done.8 = f32[264,128]{1,0:T(8,128)S(1)} collective-permute-done((f32[264,128]{1,0:T(8,128)S(1)}, f32[264,128]{1,0:T(8,128)S(1)}, u32[]{:S(2)}, u32[]{:S(2)}) %collective-permute-start.8) | collective-permute-done | bytes 135200 | tf_op jit(solution)/shard_map/ppermute | solution.py:606
  60.7 1.1 copy.80.high_ref
  61.7 1.0 copy.79.low_ref
  63.0 1.0 copy.77.high_ref
  64.1 6.0 %collective-permute-done.7 = f32[264,128]{1,0:T(8,128)} collective-permute-done((f32[264,128]{1,0:T(8,128)S(1)}, f32[264,128]{1,0:T(8,128)}, u32[]{:S(2)}, u32[]{:S(2)}) %collective-permute-start.7) | collective-permute-done | bytes 135200 | tf_op jit(solution)/shard_map/ppermute | solution.py:606
  70.1 6.4 %collective-permute-done.4.refs_4_ = f32[4,264,128]{2,1,0:T(8,128)S(1)} collective-permute-done((f32[4,264,128]{2,1,0:T(8,128)S(1)}, f32[4,264,128]{2,1,0:T(8,128)S(1)}, u32[]{:S(2)}, u32[]{:S(2)}) %collective-permute-start.4) | collective-permute-done | bytes 540704 | tf_op jit(solution)/shard_map/ppermute | solution.py:586
  78.5 1.0 pad_maximum_fusion.2.refs_0_
  80.1 2.3 collective-permute-start.18
  83.6 1.7 place.2
  85.3 3.2 convolution_bitcast_fusion.v_ref
  88.4 3.2 convolution_bitcast_fusion.1.k_ref
  91.6 1.9 convolution_bitcast_fusion.2.q_ref
  93.5 12.1 %attend.2 = (f32[1024,512]{1,0:T(8,128)S(1)}, f32[1024,128]{1,0:T(8,128)S(1)}) custom-call(s32[8]{0:T(128)S(1)} %get-tuple-element.218.block_low, s32[8]{0:T(128)S(1)} %get-tuple-element.217.block_count, f32[1024,512]{1,0:T(8,128)S(1)} %convolution_bitcast_fusion.2.q_ref, f32[1024,512]{1,0:T(8,128)} %convolution_bitcast_fusion.1.k_ref, ...), custom_call_target="tpu_custom_call" | custom-call | flops 1610612736 | bytes 8388608 | tf_op jit(solution)/shard_map/attend/pallas_call | solution.py:471
  105.7 18.2 %collective-permute-done.14 = f32[1024,128]{1,0:T(8,128)} collective-permute-done((f32[1024,128]{1,0:T(8,128)S(1)}, f32[1024,128]{1,0:T(8,128)}, u32[]{:S(2)}, u32[]{:S(2)}) %collective-permute-start.14) | collective-permute-done | bytes 524320 | tf_op jit(solution)/shard_map/ppermute | solution.py:606
  125.0 4.2 %fusion.44 = (f32[1024]{0:T(1024)S(1)}, f32[1024,512]{1,0:T(8,128)S(1)}) fusion(f32[1024,512]{1,0:T(8,128)} %x_ref.1, f32[1024,512]{1,0:T(8,128)S(1)} %get-tuple-element.137.o_ref, f32[4,512,512]{2,1,0:T(8,128)S(1)} %get-tuple-element.129.w_ref), kind=kOutput, calls=%fused_computation.109 | convolution fusion | flops 1611660288 | bytes 7344128 | tf_op jit(solution)/shard_map/dot_general | solution.py:574
  129.8 1.0 copy-done.49
  130.7 1.5 select_select_fusion.3
  132.2 1.4 pad_maximum_fusion.mem_ref
  133.7 1.8 place.3
  135.5 3.2 fusion.2.v_ref
  138.7 3.3 fusion.4.k_ref
  141.9 1.9 fusion.q_ref
  144.0 11.7 %attend.3 = (f32[1024,512]{1,0:T(8,128)S(1)}, f32[1024,128]{1,0:T(8,128)S(1)}) custom-call(s32[8]{0:T(128)S(1)} %get-tuple-element.220.block_low, s32[8]{0:T(128)S(1)} %get-tuple-element.219.block_count, f32[1024,512]{1,0:T(8,128)S(1)} %fusion.q_ref, f32[1024,512]{1,0:T(8,128)} %fusion.4.k_ref, f32[1024,512]{1,0:T(8,128)} %fusion.2.v_ref, ...), custom_call_target="tpu_custom_call" | custom-call | flops 1610612736 | bytes 8388608 | tf_op jit(solution)/shard_map/attend/pallas_call | solution.py:471
  155.7 2.3 fusion.45
  158.5 1.7 multiply_add_fusion.z_ref
  160.2 41.2 %feed_forward.1 = (f32[1024,512]{1,0:T(8,128)}, f32[1024,512]{1,0:T(8,128)}, f32[512,1024]{1,0:T(8,128)}, f32[8,512]{1,0:T(8,128)}, f32[1,512]{1,0:T(1,128)}) custom-call(s32[1]{0:T(128)} %bitcast.model_ref, f32[1024,512]{1,0:T(8,128)} %multiply_add_fusion.z_ref, f32[1024,512]{1,0:T(8,128)} %g_ref.1, f32[8,4,128,512]{3,2,1,0:T(8,128)} %bitcast.174, ...), custom_call_target="tpu_custom_call" | custom-call | flops 28991029248 | bytes 25165824 | tf_op jit(solution)/shard_map/feed_forward/pallas_call | solution.py:783
  201.4 40.2 %cross_back.1 = (f32[4,72,512]{2,1,0:T(8,128)}, f32[4,72,512]{2,1,0:T(8,128)}, f32[1024,512]{1,0:T(8,128)}, f32[1024,128]{1,0:T(8,128)}) custom-call(s32[2]{0:T(128)} %copy-done.28, s32[8]{0:T(128)} %copy-done.32, s32[8]{0:T(128)} %copy-done.31, f32[1024,512]{1,0:T(8,128)} %get-tuple-element.151.g_ref, f32[1024,512]{1,0:T(8,128)} %copy-done.40, ...), custom_call_target="tpu_custom_call" | custom-call | flops 32212254720 | bytes 31457280 | tf_op jit(solution)/shard_map/cross_back/pallas_call | solution.py:508
  241.7 3.4 place_back.1
  245.2 11.8 %all-to-all-start.1 = ((f32[8,176,128]{2,1,0:T(8,128)}), f32[8,176,128]{2,1,0:T(8,128)S(1)}, u32[]{:S(2)}, u32[]{:S(2)}) async-start(f32[8,176,128]{2,1,0:T(8,128)} %bitcast.150), calls=%async_computation.1 | async-start | bytes 1441792 | tf_op jit(solution)/shard_map/all_to_all | solution.py:1166
  257.0 3.0 collective-permute-start.26
  260.7 33.5 %self_back.1 = (f32[4,64,512]{2,1,0:T(8,128)}, f32[4,64,512]{2,1,0:T(8,128)}, f32[1024,512]{1,0:T(8,128)}, f32[1024,512]{1,0:T(8,128)}, f32[1024,512]{1,0:T(8,128)}) custom-call(s32[2]{0:T(128)} %copy-done.28, s32[8]{0:T(128)} %copy-done.30, s32[8]{0:T(128)} %copy-done.29, f32[1024,512]{1,0:T(8,128)} %get-tuple-element.159.g_ref, f32[1024,512]{1,0:T(8,128)} %x_ref.1, ...), custom_call_target="tpu_custom_call" | custom-call | flops 32212254720 | bytes 31457280 | tf_op jit(solution)/shard_map/self_back/pallas_call | solution.py:543
  294.3 2.1 collective-permute-done.27
  296.4 1.1 add.133
  297.6 2.9 collective-permute-start.30
  301.2 3.2 collective-permute-done.30.refs_3_
  304.4 2.7 collective-permute-done.29.refs_2_
  307.3 0.9 copy-done.15
  308.6 3.9 %fusion.13 = f32[1024,512]{1,0:T(8,128)S(1)} fusion(f32[1024,512]{1,0:T(8,128)} %get-tuple-element.173, f32[4,512,512]{2,1,0:T(8,128)} %copy-done), kind=kOutput, calls=%fused_computation.24 | convolution fusion | flops 1610612736 | bytes 5242880 | tf_op jit(solution)/shard_map/dot_general | solution.py:574
  312.5 1.7 collective-permute-start.34
  314.2 1.4 collective-permute-start.33
  316.1 1.8 fusion.10
  318.0 1.2 collective-permute-done.32
  319.1 4.9 %collective-permute-start.37 = (f32[1,128]{1,0:T(1,128)S(1)}, f32[1,128]{1,0:T(1,128)S(1)}, u32[]{:S(2)}, u32[]{:S(2)}) collective-permute-start(f32[1,128]{1,0:T(1,128)S(1)} %add_add_fusion.4), channel_id=1, source_target_pairs={{0,3},{1,2},{2,1},{3,0},{4,7},{5,6},{6,5},{7,4},{8,11},{9,10},{10,... | collective-permute-start | bytes 1544 | tf_op jit(solution)/shard_map/ppermute | solution.py:586
  324.8 3.5 add_add_fusion
  328.6 1.5 moments.1
  330.1 1.1 collective-permute-done.38
  331.2 1.3 collective-permute-start.41
  333.2 1.6 collective-permute-start.39
  334.7 0.9 collective-permute-done.41
  336.7 3.6 %collective-permute-start.44 = (f32[1,128]{1,0:T(1,128)S(1)}, f32[1,128]{1,0:T(1,128)S(1)}, u32[]{:S(2)}, u32[]{:S(2)}) collective-permute-start(f32[1,128]{1,0:T(1,128)S(1)} %add_add_fusion.2), channel_id=1, source_target_pairs={{0,3},{1,2},{2,1},{3,0},{4,7},{5,6},{6,5},{7,4},{8,11},{9,10},{10,... | collective-permute-start | bytes 1544 | tf_op jit(solution)/shard_map/ppermute | solution.py:586
  341.1 2.0 return_rows.1
  343.1 1.6 collective-permute-done.43
  344.7 1.0 apply.1
  (210 shorter events, 17.4 us)
Async XLA Ops:
  11.4 23.0 %copy-start.8 = (f32[512,64]{0,1:T(8,128)S(1)}, f32[512,64]{0,1:T(8,128)}, u32[]{:S(2)}) copy-start(f32[512,64]{0,1:T(8,128)} %param.35) | copy-start | bytes 393220
  11.4 23.0 %copy-start.9 = (f32[64,512]{1,0:T(8,128)S(1)}, f32[64,512]{1,0:T(8,128)}, u32[]{:S(2)}) copy-start(f32[64,512]{1,0:T(8,128)} %refs_2_.1) | copy-start | bytes 393220
  11.4 17.2 %all-to-all-start = ((f32[8,176,128]{2,1,0:T(8,128)}), f32[8,176,128]{2,1,0:T(8,128)S(1)}, u32[]{:S(2)}, u32[]{:S(2)}) async-start(f32[8,176,128]{2,1,0:T(8,128)} %pack_rows.1), calls=%async_computation | async-start | bytes 1441792 | tf_op jit(solution)/shard_map/all_to_all | solution.py:1078
  16.7 143.5 %all-gather.3.cloned.1.call-start = ((), (), s32[]{:S(2)}) async-start(), calls=%async_computation.4 | async-start | bytes 8650752 | tf_op jit(solution)/shard_map/all_gather | solution.py:1104
  16.8 36.0 %copy-start.50 = (s32[1,32]{1,0:T(1,128)S(1)}, s32[1,32]{1,0:T(1,128)}, u32[]{:S(2)}) copy-start(s32[1,32]{1,0:T(1,128)} %param.28) | copy-start | bytes 388
  16.8 43.3 %copy-start.51 = (s32[1,32]{1,0:T(1,128)S(1)}, s32[1,32]{1,0:T(1,128)}, u32[]{:S(2)}) copy-start(s32[1,32]{1,0:T(1,128)} %param.29) | copy-start | bytes 388
  16.9 15.9 %collective-permute-start.2 = (f32[264,128]{1,0:T(8,128)S(1)}, f32[264,128]{1,0:T(8,128)S(1)}, u32[]{:S(2)}, u32[]{:S(2)}) collective-permute-start(f32[264,128]{1,0:T(8,128)S(1)} %get-tuple-element.120), channel_id=1, source_target_pairs={{0,3},{1,0},{2,1},{3,2},{4,7},{5,4},{6,5},{7,6},{8,11},{9,8},{10,9... | collective-permute-start | bytes 405512 | tf_op jit(solution)/shard_map/ppermute | solution.py:606
  20.6 12.4 %collective-permute-start.1 = (f32[264,128]{1,0:T(8,128)S(1)}, f32[264,128]{1,0:T(8,128)S(1)}, u32[]{:S(2)}, u32[]{:S(2)}) collective-permute-start(f32[264,128]{1,0:T(8,128)S(1)} %get-tuple-element.120), channel_id=1, source_target_pairs={{0,2},{1,3},{2,0},{3,1},{4,6},{5,7},{6,4},{7,5},{8,10},{9,11},{10,... | collective-permute-start | bytes 405512 | tf_op jit(solution)/shard_map/ppermute | solution.py:606
  20.6 12.4 %collective-permute-start = (f32[264,128]{1,0:T(8,128)S(1)}, f32[264,128]{1,0:T(8,128)S(1)}, u32[]{:S(2)}, u32[]{:S(2)}) collective-permute-start(f32[264,128]{1,0:T(8,128)S(1)} %get-tuple-element.120), channel_id=1, source_target_pairs={{0,1},{1,2},{2,3},{3,0},{4,5},{5,6},{6,7},{7,4},{8,9},{9,10},{10,1... | collective-permute-start | bytes 405512 | tf_op jit(solution)/shard_map/ppermute | solution.py:606
  32.8 45.0 %copy-start.46 = (f32[1024,128]{1,0:T(8,128)S(1)}, f32[1024,128]{1,0:T(8,128)}, u32[]{:S(2)}) copy-start(f32[1024,128]{1,0:T(8,128)} %unpack_rows.1) | copy-start | bytes 1572868
  32.9 15.5 %collective-permute-start.13 = (f32[1024,128]{1,0:T(8,128)}, f32[1024,128]{1,0:T(8,128)S(1)}, u32[]{:S(2)}, u32[]{:S(2)}) collective-permute-start(f32[1024,128]{1,0:T(8,128)} %unpack_rows.1), channel_id=1, source_target_pairs={{0,1},{1,2},{2,3},{3,0},{4,5},{5,6},{6,7},{7,4},{8,9},{9,10},{10,1... | collective-permute-start | bytes 1572872 | tf_op jit(solution)/shard_map/ppermute | solution.py:606
  48.4 258.9 %reduce-scatter.2.cloned.1.call-start = ((), (), s32[]{:S(2)}) async-start(), calls=%async_computation.3 | async-start | bytes 2359296 | tf_op jit(solution)/shard_map/reduce_scatter | solution.py:1140
  49.2 20.9 %collective-permute-start.5 = (f32[4,264,128]{2,1,0:T(8,128)S(1)}, f32[4,264,128]{2,1,0:T(8,128)S(1)}, u32[]{:S(2)}, u32[]{:S(2)}) collective-permute-start(f32[4,264,128]{2,1,0:T(8,128)S(1)} %pad_maximum_fusion.1.refs_0_), channel_id=1, source_target_pairs={{0,24},{4,28},{8,16},{12,20},{16,8},{20,12},{24,0},{28,4},{1,25},{... | collective-permute-start | bytes 1622024 | tf_op jit(solution)/shard_map/ppermute | solution.py:586
  51.8 24.8 %collective-permute-start.4 = (f32[4,264,128]{2,1,0:T(8,128)S(1)}, f32[4,264,128]{2,1,0:T(8,128)S(1)}, u32[]{:S(2)}, u32[]{:S(2)}) collective-permute-start(f32[4,264,128]{2,1,0:T(8,128)S(1)} %pad_maximum_fusion.1.refs_0_), channel_id=1, source_target_pairs={{0,16},{4,20},{8,24},{12,28},{16,0},{20,4},{24,8},{28,12},{1,17},{... | collective-permute-start | bytes 1622024 | tf_op jit(solution)/shard_map/ppermute | solution.py:586
  52.3 24.4 %collective-permute-start.3 = (f32[4,264,128]{2,1,0:T(8,128)S(1)}, f32[4,264,128]{2,1,0:T(8,128)}, u32[]{:S(2)}, u32[]{:S(2)}) collective-permute-start(f32[4,264,128]{2,1,0:T(8,128)S(1)} %pad_maximum_fusion.1.refs_0_), channel_id=1, source_target_pairs={{0,8},{4,12},{8,0},{12,4},{16,24},{20,28},{24,16},{28,20},{1,9},{5... | collective-permute-start | bytes 1622024 | tf_op jit(solution)/shard_map/ppermute | solution.py:586
  53.1 7.1 %collective-permute-start.8 = (f32[264,128]{1,0:T(8,128)S(1)}, f32[264,128]{1,0:T(8,128)S(1)}, u32[]{:S(2)}, u32[]{:S(2)}) collective-permute-start(f32[264,128]{1,0:T(8,128)S(1)} %get-tuple-element.133), channel_id=1, source_target_pairs={{0,3},{1,0},{2,1},{3,2},{4,7},{5,4},{6,5},{7,6},{8,11},{9,8},{10,9... | collective-permute-start | bytes 405512 | tf_op jit(solution)/shard_map/ppermute | solution.py:606
  53.8 16.3 %collective-permute-start.7 = (f32[264,128]{1,0:T(8,128)S(1)}, f32[264,128]{1,0:T(8,128)}, u32[]{:S(2)}, u32[]{:S(2)}) collective-permute-start(f32[264,128]{1,0:T(8,128)S(1)} %get-tuple-element.133), channel_id=1, source_target_pairs={{0,2},{1,3},{2,0},{3,1},{4,6},{5,7},{6,4},{7,5},{8,10},{9,11},{10,... | collective-permute-start | bytes 405512 | tf_op jit(solution)/shard_map/ppermute | solution.py:606
  60.1 10.0 %collective-permute-start.6 = (f32[264,128]{1,0:T(8,128)S(1)}, f32[264,128]{1,0:T(8,128)}, u32[]{:S(2)}, u32[]{:S(2)}) collective-permute-start(f32[264,128]{1,0:T(8,128)S(1)} %get-tuple-element.133), channel_id=1, source_target_pairs={{0,1},{1,2},{2,3},{3,0},{4,5},{5,6},{6,7},{7,4},{8,9},{9,10},{10,1... | collective-permute-start | bytes 405512 | tf_op jit(solution)/shard_map/ppermute | solution.py:606
  63.0 30.5 %copy-start.10 = (s32[1024,1]{1,0:T(8,128)}, s32[1024,1]{1,0:T(8,128)S(1)}, u32[]{:S(2)}) copy-start(s32[1024,1]{1,0:T(8,128)S(1)} %copy.76.low_ref) | copy-start | bytes 12292
  64.1 69.6 %copy-start.28 = (s32[2]{0:T(128)}, s32[2]{0:T(128)S(1)}, u32[]{:S(2)}) copy-start(s32[2]{0:T(128)S(1)} %pad_add_fusion.index_ref) | copy-start | bytes 28
  76.7 2.8 collective-permute-start.9
  76.7 3.3 collective-permute-start.10
  77.3 5.1 %collective-permute-start.11 = (f32[4,264,128]{2,1,0:T(8,128)S(1)}, f32[4,264,128]{2,1,0:T(8,128)S(1)}, u32[]{:S(2)}, u32[]{:S(2)}) collective-permute-start(f32[4,264,128]{2,1,0:T(8,128)S(1)} %collective-permute-done.4.refs_4_), channel_id=1, source_target_pairs={{0,4},{4,0},{8,12},{12,8},{16,20},{20,16},{24,28},{28,24},{1,5},{5... | collective-permute-start | bytes 1622024 | tf_op jit(solution)/shard_map/ppermute | solution.py:586
  77.3 5.8 %collective-permute-start.12 = (f32[4,264,128]{2,1,0:T(8,128)S(1)}, f32[4,264,128]{2,1,0:T(8,128)S(1)}, u32[]{:S(2)}, u32[]{:S(2)}) collective-permute-start(f32[4,264,128]{2,1,0:T(8,128)S(1)} %collective-permute-done.5.refs_6_), channel_id=1, source_target_pairs={{0,4},{4,0},{8,12},{12,8},{16,20},{20,16},{24,28},{28,24},{1,5},{5... | collective-permute-start | bytes 1622024 | tf_op jit(solution)/shard_map/ppermute | solution.py:586
  77.8 66.1 %copy-start.31 = (s32[8]{0:T(128)}, s32[8]{0:T(128)S(1)}, u32[]{:S(2)}) copy-start(s32[8]{0:T(128)S(1)} %get-tuple-element.219.block_count) | copy-start | bytes 100
  77.8 66.1 %copy-start.32 = (s32[8]{0:T(128)}, s32[8]{0:T(128)S(1)}, u32[]{:S(2)}) copy-start(s32[8]{0:T(128)S(1)} %get-tuple-element.220.block_low) | copy-start | bytes 100
  77.9 27.8 %collective-permute-start.15 = (f32[1024,128]{1,0:T(8,128)S(1)}, f32[1024,128]{1,0:T(8,128)}, u32[]{:S(2)}, u32[]{:S(2)}) collective-permute-start(f32[1024,128]{1,0:T(8,128)S(1)} %copy-done.46), channel_id=1, source_target_pairs={{0,3},{1,0},{2,1},{3,2},{4,7},{5,4},{6,5},{7,6},{8,11},{9,8},{10,9... | collective-permute-start | bytes 1572872 | tf_op jit(solution)/shard_map/ppermute | solution.py:606
  79.5 44.4 %collective-permute-start.14 = (f32[1024,128]{1,0:T(8,128)S(1)}, f32[1024,128]{1,0:T(8,128)}, u32[]{:S(2)}, u32[]{:S(2)}) collective-permute-start(f32[1024,128]{1,0:T(8,128)S(1)} %copy-done.46), channel_id=1, source_target_pairs={{0,2},{1,3},{2,0},{3,1},{4,6},{5,7},{6,4},{7,5},{8,10},{9,11},{10,... | collective-permute-start | bytes 1572872 | tf_op jit(solution)/shard_map/ppermute | solution.py:606
  80.1 43.9 %collective-permute-start.18 = (f32[4,264,128]{2,1,0:T(8,128)S(1)}, f32[4,264,128]{2,1,0:T(8,128)S(1)}, u32[]{:S(2)}, u32[]{:S(2)}) collective-permute-start(f32[4,264,128]{2,1,0:T(8,128)S(1)} %pad_maximum_fusion.2.refs_0_), channel_id=1, source_target_pairs={{0,24},{4,28},{8,16},{12,20},{16,8},{20,12},{24,0},{28,4},{1,25},{... | collective-permute-start | bytes 1622024 | tf_op jit(solution)/shard_map/ppermute | solution.py:586
  82.3 41.6 %collective-permute-start.17 = (f32[4,264,128]{2,1,0:T(8,128)S(1)}, f32[4,264,128]{2,1,0:T(8,128)S(1)}, u32[]{:S(2)}, u32[]{:S(2)}) collective-permute-start(f32[4,264,128]{2,1,0:T(8,128)S(1)} %pad_maximum_fusion.2.refs_0_), channel_id=1, source_target_pairs={{0,16},{4,20},{8,24},{12,28},{16,0},{20,4},{24,8},{28,12},{1,17},{... | collective-permute-start | bytes 1622024 | tf_op jit(solution)/shard_map/ppermute | solution.py:586
  83.0 40.9 %collective-permute-start.16 = (f32[4,264,128]{2,1,0:T(8,128)S(1)}, f32[4,264,128]{2,1,0:T(8,128)S(1)}, u32[]{:S(2)}, u32[]{:S(2)}) collective-permute-start(f32[4,264,128]{2,1,0:T(8,128)S(1)} %pad_maximum_fusion.2.refs_0_), channel_id=1, source_target_pairs={{0,8},{4,12},{8,0},{12,4},{16,24},{20,28},{24,16},{28,20},{1,9},{5... | collective-permute-start | bytes 1622024 | tf_op jit(solution)/shard_map/ppermute | solution.py:586
  85.2 39.8 %copy-start = (f32[4,512,512]{2,1,0:T(8,128)}, f32[4,512,512]{2,1,0:T(8,128)S(1)}, u32[]{:S(2)}) copy-start(f32[4,512,512]{2,1,0:T(8,128)S(1)} %get-tuple-element.129.w_ref) | copy-start | bytes 12582916
  85.2 48.4 %copy-start.33 = (f32[4,8,512]{2,1,0:T(8,128)}, f32[4,8,512]{2,1,0:T(8,128)S(1)}, u32[]{:S(2)}) copy-start(f32[4,8,512]{2,1,0:T(8,128)S(1)} %get-tuple-element.138.all_vec_ref.vec_ref) | copy-start | bytes 196612
  105.7 23.6 %copy-start.6 = (f32[1024,512]{1,0:T(8,128)}, f32[1024,512]{1,0:T(8,128)S(1)}, u32[]{:S(2)}) copy-start(f32[1024,512]{1,0:T(8,128)S(1)} %get-tuple-element.137.o_ref) | copy-start | bytes 6291460
  105.7 23.6 %copy-start.36 = (f32[1024,128]{1,0:T(8,128)}, f32[1024,128]{1,0:T(8,128)S(1)}, u32[]{:S(2)}) copy-start(f32[1024,128]{1,0:T(8,128)S(1)} %get-tuple-element.160.total_ref) | copy-start | bytes 1572868
  124.0 9.7 %collective-permute-start.19 = (f32[4,264,128]{2,1,0:T(8,128)S(1)}, f32[4,264,128]{2,1,0:T(8,128)S(1)}, u32[]{:S(2)}, u32[]{:S(2)}) collective-permute-start(f32[4,264,128]{2,1,0:T(8,128)S(1)} %pad_maximum_fusion.2.refs_0_), channel_id=1, source_target_pairs={{0,4},{4,0},{8,12},{12,8},{16,20},{20,16},{24,28},{28,24},{1,5},{5... | collective-permute-start | bytes 1622024 | tf_op jit(solution)/shard_map/ppermute | solution.py:586
  124.0 9.7 %collective-permute-start.20 = (f32[4,264,128]{2,1,0:T(8,128)S(1)}, f32[4,264,128]{2,1,0:T(8,128)S(1)}, u32[]{:S(2)}, u32[]{:S(2)}) collective-permute-start(f32[4,264,128]{2,1,0:T(8,128)S(1)} %collective-permute-done.16.refs_2_), channel_id=1, source_target_pairs={{0,4},{4,0},{8,12},{12,8},{16,20},{20,16},{24,28},{28,24},{1,5},{5... | collective-permute-start | bytes 1622024 | tf_op jit(solution)/shard_map/ppermute | solution.py:586
  124.5 9.2 %collective-permute-start.21 = (f32[4,264,128]{2,1,0:T(8,128)S(1)}, f32[4,264,128]{2,1,0:T(8,128)S(1)}, u32[]{:S(2)}, u32[]{:S(2)}) collective-permute-start(f32[4,264,128]{2,1,0:T(8,128)S(1)} %collective-permute-done.17.refs_4_), channel_id=1, source_target_pairs={{0,4},{4,0},{8,12},{12,8},{16,20},{20,16},{24,28},{28,24},{1,5},{5... | collective-permute-start | bytes 1622024 | tf_op jit(solution)/shard_map/ppermute | solution.py:586
  124.6 9.1 %collective-permute-start.22 = (f32[4,264,128]{2,1,0:T(8,128)S(1)}, f32[4,264,128]{2,1,0:T(8,128)S(1)}, u32[]{:S(2)}, u32[]{:S(2)}) collective-permute-start(f32[4,264,128]{2,1,0:T(8,128)S(1)} %collective-permute-done.18.refs_6_), channel_id=1, source_target_pairs={{0,4},{4,0},{8,12},{12,8},{16,20},{20,16},{24,28},{28,24},{1,5},{5... | collective-permute-start | bytes 1622024 | tf_op jit(solution)/shard_map/ppermute | solution.py:586
  129.3 26.4 %copy-start.38 = (f32[1024,512]{1,0:T(8,128)}, f32[1024,512]{1,0:T(8,128)S(1)}, u32[]{:S(2)}) copy-start(f32[1024,512]{1,0:T(8,128)S(1)} %get-tuple-element.244.one_ref) | copy-start | bytes 6291460
  135.5 20.2 %copy-start.4 = (f32[4,512,512]{2,1,0:T(8,128)}, f32[4,512,512]{2,1,0:T(8,128)S(1)}, u32[]{:S(2)}) copy-start(f32[4,512,512]{2,1,0:T(8,128)S(1)} %get-tuple-element.143.w_ref) | copy-start | bytes 12582916
  241.6 3.5 collective-permute-start.23
  245.2 49.0 %all-to-all-start.1 = ((f32[8,176,128]{2,1,0:T(8,128)}), f32[8,176,128]{2,1,0:T(8,128)S(1)}, u32[]{:S(2)}, u32[]{:S(2)}) async-start(f32[8,176,128]{2,1,0:T(8,128)} %bitcast.150), calls=%async_computation.1 | async-start | bytes 1441792 | tf_op jit(solution)/shard_map/all_to_all | solution.py:1166
  257.0 37.2 %collective-permute-start.26 = (f32[72,512]{1,0:T(8,128)S(1)}, f32[72,512]{1,0:T(8,128)S(1)}, u32[]{:S(2)}, u32[]{:S(2)}) collective-permute-start(f32[72,512]{1,0:T(8,128)S(1)} %get-tuple-element.225), channel_id=1, source_target_pairs={{0,24},{4,28},{8,16},{12,20},{16,8},{20,12},{24,0},{28,4},{1,25},{... | collective-permute-start | bytes 442376 | tf_op jit(solution)/shard_map/ppermute | solution.py:586
  260.1 34.1 %collective-permute-start.25 = (f32[72,512]{1,0:T(8,128)S(1)}, f32[72,512]{1,0:T(8,128)S(1)}, u32[]{:S(2)}, u32[]{:S(2)}) collective-permute-start(f32[72,512]{1,0:T(8,128)S(1)} %get-tuple-element.226), channel_id=1, source_target_pairs={{0,16},{4,20},{8,24},{12,28},{16,0},{20,4},{24,8},{28,12},{1,17},{... | collective-permute-start | bytes 442376 | tf_op jit(solution)/shard_map/ppermute | solution.py:586
  260.6 33.6 %collective-permute-start.24 = (f32[72,512]{1,0:T(8,128)S(1)}, f32[72,512]{1,0:T(8,128)S(1)}, u32[]{:S(2)}, u32[]{:S(2)}) collective-permute-start(f32[72,512]{1,0:T(8,128)S(1)} %get-tuple-element.227), channel_id=1, source_target_pairs={{0,8},{4,12},{8,0},{12,4},{16,24},{20,28},{24,16},{28,20},{1,9},{5... | collective-permute-start | bytes 442376 | tf_op jit(solution)/shard_map/ppermute | solution.py:586
  294.3 2.2 collective-permute-start.27
  297.6 6.8 %collective-permute-start.30 = (f32[64,512]{1,0:T(8,128)S(1)}, f32[64,512]{1,0:T(8,128)S(1)}, u32[]{:S(2)}, u32[]{:S(2)}) collective-permute-start(f32[64,512]{1,0:T(8,128)S(1)} %get-tuple-element.229), channel_id=1, source_target_pairs={{0,24},{4,28},{8,16},{12,20},{16,8},{20,12},{24,0},{28,4},{1,25},{... | collective-permute-start | bytes 393224 | tf_op jit(solution)/shard_map/ppermute | solution.py:586
  300.5 6.6 %collective-permute-start.29 = (f32[64,512]{1,0:T(8,128)S(1)}, f32[64,512]{1,0:T(8,128)S(1)}, u32[]{:S(2)}, u32[]{:S(2)}) collective-permute-start(f32[64,512]{1,0:T(8,128)S(1)} %get-tuple-element.230), channel_id=1, source_target_pairs={{0,16},{4,20},{8,24},{12,28},{16,0},{20,4},{24,8},{28,12},{1,17},{... | collective-permute-start | bytes 393224 | tf_op jit(solution)/shard_map/ppermute | solution.py:586
  301.0 6.3 %collective-permute-start.28 = (f32[64,512]{1,0:T(8,128)S(1)}, f32[64,512]{1,0:T(8,128)S(1)}, u32[]{:S(2)}, u32[]{:S(2)}) collective-permute-start(f32[64,512]{1,0:T(8,128)S(1)} %get-tuple-element.231), channel_id=1, source_target_pairs={{0,8},{4,12},{8,0},{12,4},{16,24},{20,28},{24,16},{28,20},{1,9},{5... | collective-permute-start | bytes 393224 | tf_op jit(solution)/shard_map/ppermute | solution.py:586
  308.5 4.0 %collective-permute-start.31 = (f32[1,128]{1,0:T(1,128)S(1)}, f32[1,128]{1,0:T(1,128)S(1)}, u32[]{:S(2)}, u32[]{:S(2)}) collective-permute-start(f32[1,128]{1,0:T(1,128)S(1)} %get-tuple-element.172), channel_id=1, source_target_pairs={{0,4},{4,0},{8,12},{12,8},{16,20},{20,16},{24,28},{28,24},{1,5},{5... | collective-permute-start | bytes 1544 | tf_op jit(solution)/shard_map/ppermute | solution.py:586
  312.5 5.4 %collective-permute-start.34 = (f32[1,128]{1,0:T(1,128)S(1)}, f32[1,128]{1,0:T(1,128)S(1)}, u32[]{:S(2)}, u32[]{:S(2)}) collective-permute-start(f32[1,128]{1,0:T(1,128)S(1)} %add.134), channel_id=1, source_target_pairs={{0,24},{4,28},{8,16},{12,20},{16,8},{20,12},{24,0},{28,4},{1,25},{... | collective-permute-start | bytes 1544 | tf_op jit(solution)/shard_map/ppermute | solution.py:586
  314.2 3.8 %collective-permute-start.33 = (f32[1,128]{1,0:T(1,128)S(1)}, f32[1,128]{1,0:T(1,128)S(1)}, u32[]{:S(2)}, u32[]{:S(2)}) collective-permute-start(f32[1,128]{1,0:T(1,128)S(1)} %add.134), channel_id=1, source_target_pairs={{0,16},{4,20},{8,24},{12,28},{16,0},{20,4},{24,8},{28,12},{1,17},{... | collective-permute-start | bytes 1544 | tf_op jit(solution)/shard_map/ppermute | solution.py:586
  315.6 3.5 %collective-permute-start.32 = (f32[1,128]{1,0:T(1,128)S(1)}, f32[1,128]{1,0:T(1,128)S(1)}, u32[]{:S(2)}, u32[]{:S(2)}) collective-permute-start(f32[1,128]{1,0:T(1,128)S(1)} %add.134), channel_id=1, source_target_pairs={{0,8},{4,12},{8,0},{12,4},{16,24},{20,28},{24,16},{28,20},{1,9},{5... | collective-permute-start | bytes 1544 | tf_op jit(solution)/shard_map/ppermute | solution.py:586
  319.1 9.1 %collective-permute-start.37 = (f32[1,128]{1,0:T(1,128)S(1)}, f32[1,128]{1,0:T(1,128)S(1)}, u32[]{:S(2)}, u32[]{:S(2)}) collective-permute-start(f32[1,128]{1,0:T(1,128)S(1)} %add_add_fusion.4), channel_id=1, source_target_pairs={{0,3},{1,2},{2,1},{3,0},{4,7},{5,6},{6,5},{7,4},{8,11},{9,10},{10,... | collective-permute-start | bytes 1544 | tf_op jit(solution)/shard_map/ppermute | solution.py:586
  324.0 4.4 %collective-permute-start.36 = (f32[1,128]{1,0:T(1,128)S(1)}, f32[1,128]{1,0:T(1,128)S(1)}, u32[]{:S(2)}, u32[]{:S(2)}) collective-permute-start(f32[1,128]{1,0:T(1,128)S(1)} %add_add_fusion.4), channel_id=1, source_target_pairs={{0,2},{1,3},{2,0},{3,1},{4,6},{5,7},{6,4},{7,5},{8,10},{9,11},{10,... | collective-permute-start | bytes 1544 | tf_op jit(solution)/shard_map/ppermute | solution.py:586
  324.0 4.4 %collective-permute-start.35 = (f32[1,128]{1,0:T(1,128)S(1)}, f32[1,128]{1,0:T(1,128)S(1)}, u32[]{:S(2)}, u32[]{:S(2)}) collective-permute-start(f32[1,128]{1,0:T(1,128)S(1)} %add_add_fusion.4), channel_id=1, source_target_pairs={{0,1},{1,0},{2,3},{3,2},{4,5},{5,4},{6,7},{7,6},{8,9},{9,8},{10,11... | collective-permute-start | bytes 1544 | tf_op jit(solution)/shard_map/ppermute | solution.py:586
  330.1 1.1 collective-permute-start.38
  331.2 4.4 %collective-permute-start.41 = (f32[1,128]{1,0:T(1,128)S(1)}, f32[1,128]{1,0:T(1,128)S(1)}, u32[]{:S(2)}, u32[]{:S(2)}) collective-permute-start(f32[1,128]{1,0:T(1,128)S(1)} %add.144), channel_id=1, source_target_pairs={{0,24},{4,28},{8,16},{12,20},{16,8},{20,12},{24,0},{28,4},{1,25},{... | collective-permute-start | bytes 1544 | tf_op jit(solution)/shard_map/ppermute | solution.py:586
  332.6 3.5 %collective-permute-start.40 = (f32[1,128]{1,0:T(1,128)S(1)}, f32[1,128]{1,0:T(1,128)S(1)}, u32[]{:S(2)}, u32[]{:S(2)}) collective-permute-start(f32[1,128]{1,0:T(1,128)S(1)} %add.144), channel_id=1, source_target_pairs={{0,16},{4,20},{8,24},{12,28},{16,0},{20,4},{24,8},{28,12},{1,17},{... | collective-permute-start | bytes 1544 | tf_op jit(solution)/shard_map/ppermute | solution.py:586
  333.2 3.5 %collective-permute-start.39 = (f32[1,128]{1,0:T(1,128)S(1)}, f32[1,128]{1,0:T(1,128)S(1)}, u32[]{:S(2)}, u32[]{:S(2)}) collective-permute-start(f32[1,128]{1,0:T(1,128)S(1)} %add.144), channel_id=1, source_target_pairs={{0,8},{4,12},{8,0},{12,4},{16,24},{20,28},{24,16},{28,20},{1,9},{5... | collective-permute-start | bytes 1544 | tf_op jit(solution)/shard_map/ppermute | solution.py:586
  336.7 6.4 %collective-permute-start.44 = (f32[1,128]{1,0:T(1,128)S(1)}, f32[1,128]{1,0:T(1,128)S(1)}, u32[]{:S(2)}, u32[]{:S(2)}) collective-permute-start(f32[1,128]{1,0:T(1,128)S(1)} %add_add_fusion.2), channel_id=1, source_target_pairs={{0,3},{1,2},{2,1},{3,0},{4,7},{5,6},{6,5},{7,4},{8,11},{9,10},{10,... | collective-permute-start | bytes 1544 | tf_op jit(solution)/shard_map/ppermute | solution.py:586
  340.3 4.4 %collective-permute-start.43 = (f32[1,128]{1,0:T(1,128)S(1)}, f32[1,128]{1,0:T(1,128)S(1)}, u32[]{:S(2)}, u32[]{:S(2)}) collective-permute-start(f32[1,128]{1,0:T(1,128)S(1)} %add_add_fusion.2), channel_id=1, source_target_pairs={{0,2},{1,3},{2,0},{3,1},{4,6},{5,7},{6,4},{7,5},{8,10},{9,11},{10,... | collective-permute-start | bytes 1544 | tf_op jit(solution)/shard_map/ppermute | solution.py:586
  340.3 4.4 %collective-permute-start.42 = (f32[1,128]{1,0:T(1,128)S(1)}, f32[1,128]{1,0:T(1,128)S(1)}, u32[]{:S(2)}, u32[]{:S(2)}) collective-permute-start(f32[1,128]{1,0:T(1,128)S(1)} %add_add_fusion.2), channel_id=1, source_target_pairs={{0,1},{1,0},{2,3},{3,2},{4,5},{5,4},{6,7},{7,6},{8,9},{9,8},{10,11... | collective-permute-start | bytes 1544 | tf_op jit(solution)/shard_map/ppermute | solution.py:586
  (37 other events, 212.4 us)
Sparse Core Ops, SparseCore 0:
  48.5 106.9 all-gather.2
  241.9 52.3 reduce-scatter.1
